TPU v7x, 32 devices: a whole 2x2x4 slice. The times are simulated.
32 devices in a mesh: groups: 2 (over y), space: 4 (over z), disp: 4 (over x, core).
Axes of the slice: x: 2, y: 2, z: 4, core: 2. Of those that a mesh axis runs over, the one named last changes fastest.
Arguments:
- volume: bfloat16 [8, 16, 32, 256], P(None, 'disp', ('groups', 'space')), parts along dimension 2, may hold values from -6 to 6
- w_first: bfloat16 [3, 3, 3, 8, 8], replicated, may hold values from -0.4375 to 0.4375
- b_first: float32 [8], replicated, may hold values from -1 to 1
- w_second: bfloat16 [3, 3, 3, 8], replicated, may hold values from -0.4375 to 0.4375
- prior_logits: float32 [16, 32, 256], P('disp', ('groups', 'space')), parts along dimension 1, may hold values from -15 to 310
- cotangent: float32 [32, 256], P(('groups', 'space')), parts along dimension 0, may hold values from -24 to 24
Outputs:
- grad_volume: bfloat16 [8, 16, 32, 256], P(None, 'disp', ('groups', 'space')), parts along dimension 2
- grad_w_first: float32 [3, 3, 3, 16, 8], P(None, None, None, 'groups'), parts along dimension 3
- grad_b_first: float32 [16], P('groups'), parts along dimension 0
- grad_w_second: float32 [3, 3, 3, 16], P(None, None, None, 'groups'), parts along dimension 3
- disparity: float32 [32, 256], P(('groups', 'space')), parts along dimension 0
There are 2 independent parts, one for each index of `groups`. A program takes and returns all parts, laid end to end along the dimension named above; an argument that names none is the same for every part. Nothing has to cross between parts.
All inputs are finite; a program needn't handle non-finite values.
Results may differ from a plain program's by a relative error of at most 0.011.
Values may be sent and summed in bfloat16 or wider, within the bound.
No kernel may reach another device: no remote copies, remote signals or barrier semaphores. Data moves between devices by JAX's collectives and lax.ppermute only.
A program may use at most 64 MiB of HBM per device.

v0:
```python
import math

import jax
import jax.numpy as jnp
from jax import lax
from jax.sharding import PartitionSpec as P


def padded_2(cells, sides, width):
    for axis, dim in sides:
        count = lax.axis_size(axis)
        ends = count - 1
        head = lax.slice_in_dim(cells, 0, width, axis=dim)
        tail = lax.slice_in_dim(cells, cells.shape[dim] - width, cells.shape[dim], axis=dim)
        cells = jnp.concatenate(
            [
                lax.ppermute(tail, axis, [(i, (i + 1) % count) for i in range(ends)]),
                cells,
                lax.ppermute(head, axis, [((i + 1) % count, i) for i in range(ends)]),
            ],
            axis=dim,
        )
    return cells


def combined_all(value, axis, combine):
    everything = jax.tree.map(lambda part: lax.all_gather(part, axis), value)
    first = jax.tree.map(lambda part: part[0], everything)

    def step(k, so_far):
        return combine(so_far, jax.tree.map(lambda part: part[k], everything))

    return lax.fori_loop(1, lax.axis_size(axis), step, first)


def tap_stack(source, planes, rows, width):
    padded = jnp.pad(source, ((0, 0), (0, 0), (0, 0), (1, 1)))
    return jnp.concatenate(
        [
            padded[:, a : a + planes, b : b + rows, c : c + width]
            for a in range(3)
            for b in range(3)
            for c in range(3)
        ],
        axis=0,
    )


def correlate(source, kernel):
    planes = source.shape[1] - 2
    rows = source.shape[2] - 2
    width = source.shape[3]
    stacked = tap_stack(source, planes, rows, width)
    joined = jnp.concatenate(
        [kernel[a, b, c] for a in range(3) for b in range(3) for c in range(3)], axis=1
    )
    return jnp.einsum("oi,idhw->odhw", joined, stacked, preferred_element_type=jnp.float32)


def transposed(kernel):
    return jnp.swapaxes(kernel[::-1, ::-1, ::-1], 3, 4)


def kernel_grad(out_grad, source):
    planes = out_grad.shape[1]
    rows = out_grad.shape[2]
    width = out_grad.shape[3]
    stacked = tap_stack(source, planes, rows, width)
    product = jnp.einsum("odhw,kdhw->ok", out_grad, stacked, preferred_element_type=jnp.float32)
    outputs = product.shape[0]
    inputs = source.shape[0]
    return jnp.transpose(product.reshape(outputs, 3, 3, 3, inputs), (1, 2, 3, 0, 4))


def inside_mask(planes, rows, reach, plane_count, row_count):
    plane_index = (
        lax.axis_index("disp") * plane_count
        - reach
        + lax.broadcasted_iota(jnp.int32, (planes, rows, 1), 0)
    )
    row_index = (
        lax.axis_index("space") * row_count
        - reach
        + lax.broadcasted_iota(jnp.int32, (planes, rows, 1), 1)
    )
    keeper = (
        (plane_index >= 0)
        & (plane_index < plane_count * lax.axis_size("disp"))
        & (row_index >= 0)
        & (row_index < row_count * lax.axis_size("space"))
    )
    return keeper.astype(jnp.float32)


def combine_stats(first_part, second_part):
    highest = jnp.maximum(first_part[0], second_part[0])
    factor_one = jnp.exp(first_part[0] - highest)
    factor_two = jnp.exp(second_part[0] - highest)
    return (
        highest,
        first_part[1] * factor_one + second_part[1] * factor_two,
        first_part[2] * factor_one + second_part[2] * factor_two,
    )


def silu_grad(hidden_grad, pre_act):
    gate_sigmoid = jax.nn.sigmoid(pre_act)
    return (hidden_grad * gate_sigmoid * (1.0 + pre_act * (1.0 - gate_sigmoid))).astype(
        jnp.bfloat16
    )


def shards(volume, w_first, b_first, w_second, prior_logits, cotangent):
    plane_count = volume.shape[1]
    row_count = volume.shape[2]
    width = volume.shape[3]
    disp_size = lax.axis_size("disp")
    space_size = lax.axis_size("space")
    extended = padded_2(volume, (("space", 2), ("disp", 1)), 2)
    pre_act = correlate(extended, w_first) + b_first[:, None, None, None]
    inside = inside_mask(plane_count + 2, row_count + 2, 1, plane_count, row_count)
    hidden = (jax.nn.silu(pre_act) * inside[None]).astype(jnp.bfloat16)
    second_kernel = w_second[:, :, :, None, :]
    logits = correlate(hidden, second_kernel)[0] + prior_logits
    plane_total = plane_count * disp_size
    position = (
        lax.axis_index("disp") * plane_count
        + lax.broadcasted_iota(jnp.int32, (plane_count, 1, 1), 0)
    ).astype(jnp.float32)
    position = (position + 0.5) / plane_total
    local_top = jnp.max(logits, axis=0)
    local_exp = jnp.exp(logits - local_top[None])
    highest, summed, moment = combined_all(
        (local_top, jnp.sum(local_exp, axis=0), jnp.sum(local_exp * position, axis=0)),
        "disp",
        combine_stats,
    )
    disparity = moment / summed
    probability = jnp.exp(logits - highest[None]) / summed[None]
    score_grad = (cotangent[None] * probability * (position - disparity[None])).astype(jnp.bfloat16)
    second_grad = kernel_grad(score_grad[None], hidden)[:, :, :, 0, :]
    flipped_second = transposed(second_kernel)
    score_border = padded_2(score_grad, (("space", 1), ("disp", 0)), 2)
    hidden_grad = correlate(score_border[None], flipped_second)
    grad_border = silu_grad(hidden_grad, pre_act) * inside[None].astype(jnp.bfloat16)
    pre_grad = grad_border[:, 1:-1, 1:-1]
    volume_grad = correlate(grad_border, transposed(w_first)).astype(jnp.bfloat16)
    first_grad = kernel_grad(pre_grad, extended[:, 1:-1, 1:-1])
    bias_grad = jnp.sum(pre_grad, axis=(1, 2, 3), dtype=jnp.float32)
    grad_scale = 16.0 / math.sqrt(plane_total * row_count * space_size * width)
    first_sum, bias_sum, second_sum = lax.psum(
        (first_grad * grad_scale, bias_grad * grad_scale, second_grad * grad_scale),
        ("space", "disp"),
    )
    return (volume_grad, first_sum, bias_sum, second_sum, disparity)


def solution(mesh):
    return jax.shard_map(
        shards,
        mesh=mesh,
        in_specs=(
            P(None, "disp", ("groups", "space"), None),
            P(),
            P(),
            P(),
            P("disp", ("groups", "space"), None),
            P(("groups", "space"), None),
        ),
        out_specs=(
            P(None, "disp", ("groups", "space"), None),
            P(None, None, None, "groups", None),
            P("groups"),
            P(None, None, None, "groups"),
            P(("groups", "space"), None),
        ),
        check_vma=False,
    )
```

profile of v0, /device:TPU:0, one launch (start us, length us, event | category | flops | bytes accessed | tf_op | source)
XLA Modules:
  0.0 138.1 jit_solution(7539240962752502792)
XLA Ops:
  0.6 0.9 copy.121
  1.5 4.9 %collective-permute-start = (bf16[8,4,2,256]{3,0,2,1:T(8,128)(2,1)S(1)}, bf16[8,4,2,256]{3,0,2,1:T(8,128)(2,1)S(1)}, u32[]{:S(2)}, u32[]{:S(2)}) collective-permute-start(bf16[8,4,2,256]{3,0,2,1:T(8,128)(2,1)S(1)} %get-tuple-element.256), channel_id=1, source_target_pairs={{0,4},{4,8},{8,12},{1,5},{5,9},{9,13},{2,6},{6,10},{10,14},{3,7},{... | collective-permute-start | bytes 98312 | tf_op jit(solution)/shard_map/ppermute | solution.py:17
  6.5 1.3 collective-permute-start.1
  7.8 0.9 slice_bitcast_fusion.30
  8.6 0.8 slice_bitcast_fusion.31
  9.4 0.9 slice_bitcast_fusion.57
  10.3 0.8 slice_bitcast_fusion.76
  11.1 0.7 reverse.3
  11.9 0.9 copy.93
  16.1 0.9 constant_dynamic-update-slice_fusion.1
  17.0 1.5 %collective-permute-start.2 = (bf16[8,2,8,256]{3,0,2,1:T(8,128)(2,1)S(1)}, bf16[8,2,8,256]{3,0,2,1:T(8,128)(2,1)S(1)}, u32[]{:S(2)}, u32[]{:S(2)}) collective-permute-start(bf16[8,2,8,256]{3,0,2,1:T(8,128)(2,1)S(1)} %get-tuple-element.226), channel_id=1, source_target_pairs={{0,1},{1,2},{2,3},{4,5},{5,6},{6,7},{8,9},{9,10},{10,11},{12,13},{... | collective-permute-start | bytes 196616 | tf_op jit(solution)/shard_map/ppermute | solution.py:17
  18.5 1.3 collective-permute-start.3
  19.8 3.4 %collective-permute-done.3 = bf16[8,2,8,256]{3,0,2,1:T(8,128)(2,1)S(1)} collective-permute-done((bf16[8,2,8,256]{3,0,2,1:T(8,128)(2,1)S(1)}, bf16[8,2,8,256]{3,0,2,1:T(8,128)(2,1)S(1)}, u32[]{:S(2)}, u32[]{:S(2)}) %collective-permute-start.3) | collective-permute-done | bytes 65568 | tf_op jit(solution)/shard_map/ppermute | solution.py:19
  25.5 0.7 multiply_convert_fusion
  28.5 6.8 %all-gather.5 = f32[4,4,256]{2,1,0:T(4,128)S(1)} all-gather(f32[1,4,256]{2,1,0:T(4,128)S(1)} %bitcast.306), channel_id=4, replica_groups=mesh['groups'=2,'space'=4,'disp'=4] {'disp'}, dimensions={0}, use_global_device_ids=true | all-gather | bytes 20480 | tf_op jit(solution)/shard_map/all_gather | solution.py:27
  35.2 5.2 %all-gather.4 = f32[4,4,256]{2,1,0:T(4,128)S(1)} all-gather(f32[1,4,256]{2,1,0:T(4,128)S(1)} %bitcast.305), channel_id=3, replica_groups=mesh['groups'=2,'space'=4,'disp'=4] {'disp'}, dimensions={0}, use_global_device_ids=true | all-gather | bytes 20480 | tf_op jit(solution)/shard_map/all_gather | solution.py:27
  40.4 5.2 %all-gather.3 = f32[4,4,256]{2,1,0:T(4,128)S(1)} all-gather(f32[1,4,256]{2,1,0:T(4,128)S(1)} %bitcast.304), channel_id=2, replica_groups=mesh['groups'=2,'space'=4,'disp'=4] {'disp'}, dimensions={0}, use_global_device_ids=true | all-gather | bytes 20480 | tf_op jit(solution)/shard_map/all_gather | solution.py:27
  46.0 3.9 %fusion.3 = f32[1,3,3,3,8,1,1]{4,0,6,5,3,2,1:T(1,128)S(1)} fusion(bf16[3,3,3,8,4,4,256]{6,3,2,1,0,5,4:T(8,128)(2,1)S(1)} %bitcast.298, bf16[4,4,256,1,1,1,1]{2,1,0,3,4,5,6:T(4,128)(2,1)S(1)} %fusion.42), kind=kOutput, calls=%fused_computation.8 | convolution fusion | flops 1769472 | bytes 1778528 | tf_op jit(solution)/shard_map/odhw,kdhw->ok/dot_general | solution.py:69
  51.6 4.5 %collective-permute-start.4 = (bf16[4,2,256]{2,1,0:T(2,128)(2,1)S(1)}, bf16[4,2,256]{2,1,0:T(2,128)(2,1)S(1)}, u32[]{:S(2)}, u32[]{:S(2)}) collective-permute-start(bf16[4,2,256]{2,1,0:T(2,128)(2,1)S(1)} %get-tuple-element.367), channel_id=1, source_target_pairs={{0,4},{4,8},{8,12},{1,5},{5,9},{9,13},{2,6},{6,10},{10,14},{3,7},{... | collective-permute-start | bytes 12296 | tf_op jit(solution)/shard_map/ppermute | solution.py:17
  56.2 1.3 collective-permute-start.5
  57.5 4.2 %collective-permute-done.5 = bf16[4,2,256]{2,1,0:T(2,128)(2,1)S(1)} collective-permute-done((bf16[4,2,256]{2,1,0:T(2,128)(2,1)S(1)}, bf16[4,2,256]{2,1,0:T(2,128)(2,1)S(1)}, u32[]{:S(2)}, u32[]{:S(2)}) %collective-permute-start.5) | collective-permute-done | bytes 4128 | tf_op jit(solution)/shard_map/ppermute | solution.py:19
  61.7 1.3 collective-permute-start.6
  63.0 1.3 collective-permute-start.7
  64.4 3.2 %collective-permute-done.7 = bf16[2,8,256]{2,1,0:T(8,128)(2,1)S(1)} collective-permute-done((bf16[2,8,256]{2,1,0:T(8,128)(2,1)S(1)}, bf16[2,8,256]{2,1,0:T(8,128)(2,1)S(1)}, u32[]{:S(2)}, u32[]{:S(2)}) %collective-permute-start.7) | collective-permute-done | bytes 8224 | tf_op jit(solution)/shard_map/ppermute | solution.py:19
  67.7 0.6 pad_slice_fusion.93
  68.3 0.6 pad_slice_fusion.92
  69.2 1.7 %concatenate.74 = bf16[27,6,6,256]{3,0,2,1:T(8,128)(2,1)S(1)} concatenate(bf16[1,6,6,256]{3,0,2,1:T(2,128)(2,1)S(1)} %get-tuple-element.254, bf16[1,6,6,256]{3,0,2,1:T(2,128)(2,1)S(1)} %get-tuple-element.253, bf16[1,6,6,256]{3,0,2,1:T(2,128)(2,1)S(1)} %get-tuple-element.229, bf16[1,6,6,256]{3,0,2,1:T(2,128)(2,1)S(1)} %get-tuple-element.230, ...), dimensions={0} | concatenate | bytes 995328 | tf_op jit(solution)/shard_map/concatenate | solution.py:38
  71.4 1.0 copy-done.1
  72.4 0.6 fusion.8
  73.1 61.6 %all-reduce.5 = (f32[3,3,3,8,8]{4,2,1,0,3:T(4,128)S(1)}, f32[8]{0:T(128)}, f32[3,3,3,8]{3,2,1,0:T(4,128)}) all-reduce(f32[3,3,3,8,8]{4,2,1,0,3:T(4,128)S(1)} %bitcast.299, f32[8]{0:T(128)S(1)} %broadcast_multiply_fusion, f32[3,3,3,8]{3,2,1,0:T(4,128)S(1)} %bitcast_multiply_fusion.2), channel_id=1, replica_groups=mesh['groups'=2,'space'=4,'disp'=4] {'space','disp'}, use_global_device_ids=true, to_apply=%region_5.6 | all-reduce | flops 1952 | bytes 15616 | tf_op jit(solution)/shard_map/psum | solution.py:151
  134.7 0.7 copy.138
  137.4 0.7 copy.137
  (202 shorter events, 12.4 us)
Async XLA Ops:
  1.5 14.5 %collective-permute-start = (bf16[8,4,2,256]{3,0,2,1:T(8,128)(2,1)S(1)}, bf16[8,4,2,256]{3,0,2,1:T(8,128)(2,1)S(1)}, u32[]{:S(2)}, u32[]{:S(2)}) collective-permute-start(bf16[8,4,2,256]{3,0,2,1:T(8,128)(2,1)S(1)} %get-tuple-element.256), channel_id=1, source_target_pairs={{0,4},{4,8},{8,12},{1,5},{5,9},{9,13},{2,6},{6,10},{10,14},{3,7},{... | collective-permute-start | bytes 98312 | tf_op jit(solution)/shard_map/ppermute | solution.py:17
  6.5 10.5 %collective-permute-start.1 = (bf16[8,4,2,256]{3,0,2,1:T(8,128)(2,1)S(1)}, bf16[8,4,2,256]{3,0,2,1:T(8,128)(2,1)S(1)}, u32[]{:S(2)}, u32[]{:S(2)}) collective-permute-start(bf16[8,4,2,256]{3,0,2,1:T(8,128)(2,1)S(1)} %get-tuple-element.255), channel_id=1, source_target_pairs={{4,0},{8,4},{12,8},{5,1},{9,5},{13,9},{6,2},{10,6},{14,10},{7,3},{... | collective-permute-start | bytes 98312 | tf_op jit(solution)/shard_map/ppermute | solution.py:19
  17.0 2.8 %collective-permute-start.2 = (bf16[8,2,8,256]{3,0,2,1:T(8,128)(2,1)S(1)}, bf16[8,2,8,256]{3,0,2,1:T(8,128)(2,1)S(1)}, u32[]{:S(2)}, u32[]{:S(2)}) collective-permute-start(bf16[8,2,8,256]{3,0,2,1:T(8,128)(2,1)S(1)} %get-tuple-element.226), channel_id=1, source_target_pairs={{0,1},{1,2},{2,3},{4,5},{5,6},{6,7},{8,9},{9,10},{10,11},{12,13},{... | collective-permute-start | bytes 196616 | tf_op jit(solution)/shard_map/ppermute | solution.py:17
  18.5 4.7 %collective-permute-start.3 = (bf16[8,2,8,256]{3,0,2,1:T(8,128)(2,1)S(1)}, bf16[8,2,8,256]{3,0,2,1:T(8,128)(2,1)S(1)}, u32[]{:S(2)}, u32[]{:S(2)}) collective-permute-start(bf16[8,2,8,256]{3,0,2,1:T(8,128)(2,1)S(1)} %get-tuple-element.227), channel_id=1, source_target_pairs={{1,0},{2,1},{3,2},{5,4},{6,5},{7,6},{9,8},{10,9},{11,10},{13,12},{... | collective-permute-start | bytes 196616 | tf_op jit(solution)/shard_map/ppermute | solution.py:19
  24.7 0.8 copy-start.6
  27.4 1.0 copy-start.4
  27.6 18.2 %copy-start.5 = (f32[4,256]{1,0:T(4,128)S(1)}, f32[4,256]{1,0:T(4,128)}, u32[]{:S(2)}) copy-start(f32[4,256]{1,0:T(4,128)} %param.13) | copy-start | bytes 12292
  45.8 4.4 %copy-start.3 = (f32[4,256]{1,0:T(4,128)}, f32[4,256]{1,0:T(4,128)S(1)}, u32[]{:S(2)}) copy-start(f32[4,256]{1,0:T(4,128)S(1)} %div.23) | copy-start | bytes 12292
  49.9 0.9 copy-start.2
  51.6 5.9 %collective-permute-start.4 = (bf16[4,2,256]{2,1,0:T(2,128)(2,1)S(1)}, bf16[4,2,256]{2,1,0:T(2,128)(2,1)S(1)}, u32[]{:S(2)}, u32[]{:S(2)}) collective-permute-start(bf16[4,2,256]{2,1,0:T(2,128)(2,1)S(1)} %get-tuple-element.367), channel_id=1, source_target_pairs={{0,4},{4,8},{8,12},{1,5},{5,9},{9,13},{2,6},{6,10},{10,14},{3,7},{... | collective-permute-start | bytes 12296 | tf_op jit(solution)/shard_map/ppermute | solution.py:17
  56.2 5.5 %collective-permute-start.5 = (bf16[4,2,256]{2,1,0:T(2,128)(2,1)S(1)}, bf16[4,2,256]{2,1,0:T(2,128)(2,1)S(1)}, u32[]{:S(2)}, u32[]{:S(2)}) collective-permute-start(bf16[4,2,256]{2,1,0:T(2,128)(2,1)S(1)} %get-tuple-element.368), channel_id=1, source_target_pairs={{4,0},{8,4},{12,8},{5,1},{9,5},{13,9},{6,2},{10,6},{14,10},{7,3},{... | collective-permute-start | bytes 12296 | tf_op jit(solution)/shard_map/ppermute | solution.py:19
  61.7 2.7 %collective-permute-start.6 = (bf16[2,8,256]{2,1,0:T(8,128)(2,1)S(1)}, bf16[2,8,256]{2,1,0:T(8,128)(2,1)S(1)}, u32[]{:S(2)}, u32[]{:S(2)}) collective-permute-start(bf16[2,8,256]{2,1,0:T(8,128)(2,1)S(1)} %get-tuple-element.311), channel_id=1, source_target_pairs={{0,1},{1,2},{2,3},{4,5},{5,6},{6,7},{8,9},{9,10},{10,11},{12,13},{... | collective-permute-start | bytes 24584 | tf_op jit(solution)/shard_map/ppermute | solution.py:17
  63.0 4.6 %collective-permute-start.7 = (bf16[2,8,256]{2,1,0:T(8,128)(2,1)S(1)}, bf16[2,8,256]{2,1,0:T(8,128)(2,1)S(1)}, u32[]{:S(2)}, u32[]{:S(2)}) collective-permute-start(bf16[2,8,256]{2,1,0:T(8,128)(2,1)S(1)} %get-tuple-element.312), channel_id=1, source_target_pairs={{1,0},{2,1},{3,2},{5,4},{6,5},{7,6},{9,8},{10,9},{11,10},{13,12},{... | collective-permute-start | bytes 24584 | tf_op jit(solution)/shard_map/ppermute | solution.py:19
  64.4 3.2 %copy-start = (bf16[216,4,4,256]{3,0,2,1:T(8,128)(2,1)}, bf16[216,4,4,256]{3,0,2,1:T(8,128)(2,1)S(1)}, u32[]{:S(2)}) copy-start(bf16[216,4,4,256]{3,0,2,1:T(8,128)(2,1)S(1)} %constant_dynamic-update-slice_fusion.84) | copy-start | bytes 5308420
  70.9 1.5 %copy-start.1 = (bf16[216,4,4,256]{3,0,2,1:T(8,128)(2,1)S(1)}, bf16[216,4,4,256]{3,0,2,1:T(8,128)(2,1)}, u32[]{:S(2)}) copy-start(bf16[216,4,4,256]{3,0,2,1:T(8,128)(2,1)} %copy-done) | copy-start | bytes 5308420
where the time goes:
time: 139 us; the launch traced here: 138 us
  blocking collectives  78.7 us (57%)
  local copies, waits for them, and re-layouts  22.4 us (16%)
  starting transfers between devices  17.4 us (13%)
  waiting for transfers between devices  10.8 us (8%)
  matrix products  6.02 us (4%)
  between operations  1.86 us (1%)
    psum x1, blocking collectives, shards(): lax.psum((first_grad * grad_scale, bias_grad * grad_scale, second_grad *...  61.6 us
    all_gather x3, blocking collectives, combined_all(): everything = jax.tree.map(lambda part: lax.all_gather(part, axis), value)  17.1 us
    ppermute x4, starting transfers between devices, padded_2(): lax.ppermute(tail, axis, [(i, (i + 1) % count) for i in range(ends)])  12.2 us
    unnamed x109, local copies, waits for them, and re-layouts  11.4 us
    ppermute x4, waiting for transfers between devices, padded_2(): lax.ppermute(head, axis, [((i + 1) % count, i) for i in range(ends)])  10.8 us
    squeeze x35, local copies, waits for them, and re-layouts, correlate(): kernel[a, b, c]  5.99 us
    ppermute x4, starting transfers between devices, padded_2(): lax.ppermute(head, axis, [((i + 1) % count, i) for i in range(ends)])  5.17 us
    dot_general x2, matrix products, kernel_grad(): jnp.einsum('odhw,kdhw->ok', out_grad, stacked, preferred_element_type=jnp...  4.42 us
  transfers between devices with their start and end apart: 8, of which 3 were waited for; matrix products, arithmetic and copies ran while one was open for 7% of the time, Pallas kernels for 0%

commit v1 on v0

v1 whole, which is shorter than its diff:
```python
import functools
import math

import jax
import jax.numpy as jnp
from jax import lax
from jax.experimental import pallas as pl
from jax.experimental.pallas import tpu as pltpu
from jax.sharding import PartitionSpec as P

F32 = jnp.float32
BF16 = jnp.bfloat16


def swap_pairs(count, step):
    pairs = []
    for i in range(count):
        j = i ^ 1 if step == 0 else ((i + 1) ^ 1) - 1
        pairs.append((i, j if 0 <= j < count else i))
    return pairs


def partners(value, axis):
    count = lax.axis_size(axis)
    return [lax.ppermute(value, axis, [(i, i ^ s) for i in range(count)]) for s in range(1, count)]


def radix_stages(count):
    stages = []
    bit = 1
    while bit < count:
        if bit * 4 <= count:
            stages.append((bit, 2 * bit, 3 * bit))
            bit *= 4
        else:
            stages.append((bit,))
            bit *= 2
    return stages


def shift_up(x, lane):
    return jnp.where(lane == 0, 0.0, pltpu.roll(x, 1, 1))


def shift_down(x, lane):
    width = x.shape[1]
    return jnp.where(lane == width - 1, 0.0, pltpu.roll(x, width - 1, 1))


def left(x, amount):
    return x if amount == 0 else pltpu.roll(x, x.shape[1] - amount, 1)


def right(x, amount):
    return x if amount == 0 else pltpu.roll(x, amount, 1)


def dot(a, b):
    return lax.dot_general(a, b, (((1,), (0,)), ((), ())), preferred_element_type=F32)


def dot_t(a, b):
    return lax.dot_general(a, b, (((1,), (1,)), ((), ())), preferred_element_type=F32)


def forward_body(
    dims, mid_ref, da_ref, db_ref, ex_ref, exa_ref, exb_ref, base1_ref, bias_ref, base2_ref,
    logits_ref, slope_ref, hid_ref, xs_ref, cot_ref, x_ref, h_ref, prior_ref
):
    planes, rows, chans, width, disp, space = dims
    zi = lax.axis_index("space")
    di = lax.axis_index("disp")
    z_even = zi % 2 == 0
    d_even = di % 2 == 0
    xr = (rows + 8) * chans
    hr = (rows + 6) * chans
    lane = lax.broadcasted_iota(jnp.int32, (hr, width), 1)

    x_ref[2 * xr : (planes + 2) * xr, :] = mid_ref[...].reshape(planes * xr, width)

    def place(at, size, ok, first, one, two):
        @pl.when(ok & first)
        def _():
            x_ref[at : at + size, :] = one[...].reshape(size, width)

        @pl.when(ok & jnp.logical_not(first))
        def _():
            x_ref[at : at + size, :] = two[...].reshape(size, width)

        @pl.when(jnp.logical_not(ok))
        def _():
            x_ref[at : at + size, :] = jnp.zeros((size, width), BF16)

    place(0, 2 * xr, di > 0, d_even, db_ref, da_ref)
    place((planes + 2) * xr, 2 * xr, di < disp - 1, d_even, da_ref, db_ref)

    zero2 = jnp.zeros((2, width), F32)

    def extras(ok, first, one, two, row, at):
        def put(src):
            for p in range(planes):
                prior_ref[p, at : at + 2, :] = zero2 if src is None else src[p * rows + row : p * rows + row + 2, :]
            base = planes * rows + row
            cot_ref[at : at + 2, :] = zero2 if src is None else src[base : base + 2, :]

        pl.when(ok & first)(lambda: put(one))
        pl.when(ok & jnp.logical_not(first))(lambda: put(two))
        pl.when(jnp.logical_not(ok))(lambda: put(None))

    for p in range(planes):
        prior_ref[p, 2 : 2 + rows, :] = ex_ref[p * rows : (p + 1) * rows, :]
    cot_ref[2 : 2 + rows, :] = ex_ref[planes * rows : (planes + 1) * rows, :]
    extras(zi > 0, z_even, exb_ref, exa_ref, rows - 2, 0)
    extras(zi < space - 1, z_even, exa_ref, exb_ref, 0, rows + 2)

    bands = []
    base1 = base1_ref[...]
    for c in range(3):
        piece = base1[c * chans : (c + 1) * chans]
        for r in range(rows + 6):
            bands.append(right(piece, chans * r))
    band1 = jnp.concatenate(bands, axis=0)[:, : 3 * xr].astype(BF16)
    bias = jnp.concatenate([bias_ref[...]] * (rows + 6), axis=0)
    row_at = zi * rows - 3 + lax.broadcasted_iota(jnp.int32, (hr, width), 0) // chans
    row_ok = ((row_at >= 0) & (row_at < space * rows)).astype(F32)
    for p in range(planes + 2):
        y = dot(band1, x_ref[p * xr : (p + 3) * xr, :])
        pre = y[hr : 2 * hr] + shift_up(y[:hr], lane) + shift_down(y[2 * hr :], lane) + bias
        sig = jax.nn.sigmoid(pre)
        plane_at = di * planes - 1 + p
        ok = row_ok * ((plane_at >= 0) & (plane_at < disp * planes)).astype(F32)
        hidden = (pre * sig * ok).astype(BF16)
        h_ref[p * hr : (p + 1) * hr, :] = hidden
        inner = slice(2 * chans, hr - 2 * chans)
        slope_ref[p] = (sig * (1.0 + pre * (1.0 - sig)) * ok)[inner]
        hid_ref[p] = h_ref[p * hr + chans : (p + 1) * hr - chans, :]
        xs_ref[p] = x_ref[(p + 1) * xr + 2 * chans : (p + 2) * xr - 2 * chans, :]
    hid_ref[planes + 2] = jnp.zeros(hid_ref.shape[1:], BF16)
    xs_ref[planes + 2] = jnp.zeros(xs_ref.shape[1:], BF16)

    lr = rows + 4
    lane2 = lax.broadcasted_iota(jnp.int32, (lr, width), 1)
    bands = []
    for c in range(3):
        piece = base2_ref[c : c + 1, :]
        for r in range(lr):
            bands.append(right(piece, chans * r))
    band2 = jnp.concatenate(bands, axis=0)[:, : 3 * hr].astype(BF16)
    for p in range(planes):
        y = dot(band2, h_ref[p * hr : (p + 3) * hr, :])
        logits_ref[p * lr : (p + 1) * lr, :] = (
            y[lr : 2 * lr] + shift_up(y[:lr], lane2) + shift_down(y[2 * lr :], lane2) + prior_ref[p]
        )


def backward_body(dims, *refs):
    planes, rows, chans, width, disp, space = dims
    logit_refs = refs[:disp]
    cot_ref, slope_ref, hid_ref, xs_ref, base3_ref = refs[disp : disp + 5]
    pay_ref, pg_ref, disp_ref, l_ref, s_ref = refs[disp + 5 :]
    di = lax.axis_index("disp")
    lr = rows + 4
    hr = (rows + 2) * chans
    total = planes * disp
    lane = lax.broadcasted_iota(jnp.int32, (lr, width), 1)

    l_ref[0] = jnp.zeros(l_ref.shape[1:], F32)
    l_ref[disp + 1] = jnp.zeros(l_ref.shape[1:], F32)
    for s in range(disp):
        l_ref[(di ^ s) + 1] = logit_refs[s][...]

    def logit(g, p):
        return l_ref[g, p * lr : (p + 1) * lr, :]

    top = logit(1, 0)
    for k in range(1, total):
        top = jnp.maximum(top, logit(1 + k // planes, k % planes))
    summed = jnp.zeros((lr, width), F32)
    moment = jnp.zeros((lr, width), F32)
    for k in range(total):
        e = jnp.exp(logit(1 + k // planes, k % planes) - top)
        summed = summed + e
        moment = moment + e * ((k + 0.5) / total)
    disparity = moment / summed
    disp_ref[...] = disparity[2 : 2 + rows]
    coef = cot_ref[...] / summed
    scores = []
    for k in range(planes + 4):
        at = di * planes - 2 + k
        group = di + (0 if k < 2 else 1 if k < 2 + planes else 2)
        e = jnp.exp(logit(group, (k - 2) % planes) - top)
        ok = ((at >= 0) & (at < total)).astype(F32)
        position = (at.astype(F32) + 0.5) / total
        score = jnp.where(ok > 0.0, coef * e * (position - disparity), 0.0).astype(BF16)
        scores.append(score.astype(F32))
    s_all = jnp.concatenate(scores, axis=0).astype(BF16)

    lane_h = lax.broadcasted_iota(jnp.int32, (hr, width), 1)
    base3 = base3_ref[...]
    rhs_rows = (rows + 4) * chans
    acc1 = None
    acc2 = None
    bias = jnp.zeros((chans, width), F32)
    for p in range(planes + 2):
        bands = []
        for c in range(3):
            piece = base3[c * chans : (c + 1) * chans]
            for r in range(rows + 2):
                bands.append(right(piece, lr * p + r))
        band3 = jnp.concatenate(bands, axis=0)[:, : (planes + 4) * lr].astype(BF16)
        y = dot(band3, s_all)
        hg = y[hr : 2 * hr] + shift_down(y[:hr], lane_h) + shift_up(y[2 * hr :], lane_h)
        pg = (hg * slope_ref[p]).astype(BF16)
        pg_ref[p] = pg
        if p == 0 or p == planes + 1:
            continue
        k = p - 1
        own = pg.astype(F32)[chans : chans * (rows + 1)]
        lane_o = lane_h[: own.shape[0]]
        moved = (shift_down(own, lane_o), own, shift_up(own, lane_o))
        pieces = []
        for r in range(rows):
            bias = bias + own[r * chans : (r + 1) * chans]
            for c in range(3):
                pieces.append(moved[c][r * chans : (r + 1) * chans])
        lhs = jnp.concatenate(pieces, axis=0).astype(BF16)
        rhs = xs_ref[k : k + 4].reshape(4 * rhs_rows, width)
        part = dot_t(lhs, rhs)
        acc1 = part if acc1 is None else acc1 + part
        sc = scores[k + 2]
        lhs = jnp.concatenate([shift_down(sc, lane), sc, shift_up(sc, lane)], axis=0).astype(BF16)
        part = dot_t(lhs, hid_ref[k : k + 4].reshape(4 * rhs_rows, width))
        acc2 = part if acc2 is None else acc2 + part

    out1 = jnp.zeros((3 * chans, 4 * rhs_rows), F32)
    for r in range(rows):
        out1 = out1 + left(acc1[3 * chans * r : 3 * chans * (r + 1)], chans * (r + 1))
    row_in = lax.broadcasted_iota(jnp.int32, acc2.shape, 0) % lr
    out2 = jnp.zeros(acc2.shape, F32)
    for r in range(2, 2 + rows):
        out2 = out2 + jnp.where(row_in == r, left(acc2, chans * (r - 1)), 0.0)
    out2 = jnp.concatenate(
        [jnp.sum(out2[c * lr : (c + 1) * lr], axis=0, keepdims=True) for c in range(3)]
        + [jnp.zeros((5, out2.shape[1]), F32)],
        axis=0,
    )
    out = jnp.concatenate([out1, out2], axis=0)
    lane_p = lax.broadcasted_iota(jnp.int32, (out.shape[0], 128), 1)
    tap = 3 * chans
    packed = jnp.zeros((out.shape[0], 128), F32)
    for a in range(3):
        moved = left(out, a * (rhs_rows - tap))[:, :128]
        packed = jnp.where((lane_p >= a * tap) & (lane_p < (a + 1) * tap), moved, packed)
    bias = jnp.sum(bias, axis=1, keepdims=True)
    sub = lax.broadcasted_iota(jnp.int32, (chans, 128), 0)
    lane_b = lax.broadcasted_iota(jnp.int32, (chans, 128), 1)
    bias = jnp.sum(jnp.where(sub == lane_b, bias, 0.0), axis=0, keepdims=True)
    pay_ref[...] = packed
    pay_ref[3 * chans + 3 : 3 * chans + 4, :] = bias


def volume_grad_body(dims, pg_ref, base4_ref, out_ref):
    planes, rows, chans, width, disp, space = dims
    hr = (rows + 2) * chans
    n = rows * chans
    lane = lax.broadcasted_iota(jnp.int32, (n, width), 1)
    base4 = base4_ref[...]
    bands = []
    for c in range(3):
        piece = base4[c * chans : (c + 1) * chans]
        for r in range(rows):
            bands.append(right(piece, chans * r))
    band4 = jnp.concatenate(bands, axis=0)[:, : 3 * hr].astype(BF16)
    for p in range(planes):
        y = dot(band4, pg_ref[p : p + 3].reshape(3 * hr, width))
        out_ref[p] = (
            y[n : 2 * n] + shift_down(y[:n], lane) + shift_up(y[2 * n :], lane)
        ).astype(BF16)


def finish_body(chans, scale, *refs):
    parts = refs[:-3]
    gw_ref, gb_ref, gs_ref = refs[-3:]
    sums = [r[...] for r in parts]
    while len(sums) > 1:
        sums = [sums[k] + sums[k + 1] for k in range(0, len(sums), 2)]
    total = sums[0] * scale
    for a in range(3):
        for b in range(3):
            at = (a * 3 + b) * chans
            for c in range(3):
                gw_ref[a, b, c] = total[c * chans : (c + 1) * chans, at : at + chans]
            gs_ref[a, b] = total[3 * chans : 3 * chans + 3, at : at + chans]
    gb_ref[...] = total[3 * chans + 3 : 3 * chans + 4, :chans]


def tree_sum(parts):
    while len(parts) > 1:
        parts = [parts[k] + parts[k + 1] for k in range(0, len(parts), 2)]
    return parts[0]


def shards(volume, w_first, b_first, w_second, prior_logits, cotangent):
    chans, planes, rows, width = volume.shape
    disp = lax.axis_size("disp")
    space = lax.axis_size("space")
    dims = (planes, rows, chans, width, disp, space)
    zi = lax.axis_index("space")
    di = lax.axis_index("disp")

    own = jnp.transpose(volume, (1, 2, 0, 3)).reshape(planes, rows * chans, width)
    z_one = lax.ppermute(own, "space", swap_pairs(space, 0))
    z_two = lax.ppermute(own, "space", swap_pairs(space, 1))
    extra = jnp.concatenate([prior_logits.reshape(planes * rows, width), cotangent], axis=0)
    e_one = lax.ppermute(extra, "space", swap_pairs(space, 0))
    e_two = lax.ppermute(extra, "space", swap_pairs(space, 1))
    z_even = zi % 2 == 0
    zero = jnp.zeros((), BF16)
    above = jnp.where(zi > 0, jnp.where(z_even, z_two, z_one), zero)
    below = jnp.where(zi < space - 1, jnp.where(z_even, z_one, z_two), zero)
    mid = jnp.concatenate([above, own, below], axis=1)
    even = (di % 2 == 0).astype(jnp.int32)
    d_one = lax.ppermute(
        lax.dynamic_slice_in_dim(mid, (planes - 2) * even, 2, axis=0), "disp", swap_pairs(disp, 0)
    )
    d_two = lax.ppermute(
        lax.dynamic_slice_in_dim(mid, (planes - 2) * (1 - even), 2, axis=0), "disp", swap_pairs(disp, 1)
    )

    xr = rows + 8
    base1 = jnp.transpose(w_first, (2, 3, 0, 1, 4)).astype(F32)
    base1 = jnp.pad(base1, ((0, 0), (0, 0), (0, 0), (0, xr - 3), (0, 0))).reshape(3 * chans, 3 * xr * chans)
    base1 = jnp.pad(base1, ((0, 0), (0, -base1.shape[1] % 128)))
    base2 = jnp.transpose(w_second, (2, 0, 1, 3)).astype(F32)
    base2 = jnp.pad(base2, ((0, 0), (0, 0), (0, rows + 3), (0, 0))).reshape(3, 3 * (rows + 6) * chans)
    base2 = jnp.pad(base2, ((0, 5), (0, -base2.shape[1] % 128)))
    base3 = jnp.transpose(w_second[::-1, ::-1], (2, 3, 0, 1)).astype(F32)
    base3 = jnp.pad(base3, ((0, 0), (0, 0), (0, 0), (0, rows + 1))).reshape(3 * chans, 3 * (rows + 4))
    base3 = jnp.pad(base3, ((0, 0), (0, 128 - base3.shape[1])))
    base4 = jnp.transpose(w_first[::-1, ::-1], (2, 4, 0, 1, 3)).astype(F32)
    base4 = jnp.pad(base4, ((0, 0), (0, 0), (0, 0), (0, rows - 1), (0, 0))).reshape(
        3 * chans, 3 * (rows + 2) * chans
    )
    base4 = jnp.pad(base4, ((0, 0), (0, -base4.shape[1] % 128)))

    lr = rows + 4
    hr = rows + 6
    logits, slope, hid, xs, cot = pl.pallas_call(
        functools.partial(forward_body, dims),
        out_shape=(
            jax.ShapeDtypeStruct((planes * lr, width), F32),
            jax.ShapeDtypeStruct((planes + 2, (rows + 2) * chans, width), F32),
            jax.ShapeDtypeStruct((planes + 3, (rows + 4) * chans, width), BF16),
            jax.ShapeDtypeStruct((planes + 3, (rows + 4) * chans, width), BF16),
            jax.ShapeDtypeStruct((lr, width), F32),
        ),
        scratch_shapes=[
            pltpu.VMEM(((planes + 4) * xr * chans, width), BF16),
            pltpu.VMEM(((planes + 2) * hr * chans, width), BF16),
            pltpu.VMEM((planes, lr, width), F32),
        ],
        name="forward",
    )(mid, d_one, d_two, extra, e_one, e_two, base1, b_first[:, None], base2)

    pieces = [logits] + partners(logits, "disp")
    pay, pg, disparity = pl.pallas_call(
        functools.partial(backward_body, dims),
        out_shape=(
            jax.ShapeDtypeStruct((3 * chans + 8, 128), F32),
            jax.ShapeDtypeStruct((planes + 2, (rows + 2) * chans, width), BF16),
            jax.ShapeDtypeStruct((rows, width), F32),
        ),
        scratch_shapes=[
            pltpu.VMEM((disp + 2, planes * lr, width), F32),
            pltpu.VMEM(((planes + 4) * lr, width), F32),
        ],
        name="backward",
    )(*pieces, cot, slope, hid, xs, base3)

    stages = [("disp", s) for s in radix_stages(disp)] + [("space", s) for s in radix_stages(space)]
    for n, (axis, steps) in enumerate(stages):
        count = lax.axis_size(axis)
        parts = [pay] + [lax.ppermute(pay, axis, [(i, i ^ s) for i in range(count)]) for s in steps]
        if n < len(stages) - 1:
            pay = tree_sum(parts)

    volume_grad = pl.pallas_call(
        functools.partial(volume_grad_body, dims),
        out_shape=jax.ShapeDtypeStruct((planes, rows * chans, width), BF16),
        name="volume_grad",
    )(pg, base4)
    volume_grad = jnp.transpose(volume_grad.reshape(planes, rows, chans, width), (2, 0, 1, 3))

    scale = 16.0 / math.sqrt(planes * disp * rows * space * width)
    first_sum, bias_sum, second_sum = pl.pallas_call(
        functools.partial(finish_body, chans, scale),
        out_shape=(
            jax.ShapeDtypeStruct((3, 3, 3, chans, chans), F32),
            jax.ShapeDtypeStruct((1, chans), F32),
            jax.ShapeDtypeStruct((3, 3, 3, chans), F32),
        ),
        name="finish",
    )(*parts)
    return (volume_grad, first_sum, bias_sum[0], second_sum, disparity)


def solution(mesh):
    return jax.shard_map(
        shards,
        mesh=mesh,
        in_specs=(
            P(None, "disp", ("groups", "space"), None),
            P(),
            P(),
            P(),
            P("disp", ("groups", "space"), None),
            P(("groups", "space"), None),
        ),
        out_specs=(
            P(None, "disp", ("groups", "space"), None),
            P(None, None, None, "groups", None),
            P("groups"),
            P(None, None, None, "groups"),
            P(("groups", "space"), None),
        ),
        check_vma=False,
    )
```

time: 139 us -> 47.8 us (0.34)
  blocking collectives: 78.7 us -> 0 us
  local copies, waits for them, and re-layouts: 22.4 us -> 8.99 us
  Pallas kernels: 0 us -> 9.13 us
  matrix products: 6.02 us -> 0 us
  waiting for transfers between devices: 10.8 us -> 5.1 us
  starting transfers between devices: 17.4 us -> 20.7 us
  other arithmetic: 0.87 us -> 2.48 us
    psum x1 -> x0, blocking collectives: 61.6 us -> none  [shards(): lax.psum((first_grad * grad_scale, bias_grad * grad_scale, second_grad *...]
    all_gather x3 -> x0, blocking collectives: 17.1 us -> none  [combined_all(): everything = jax.tree.map(lambda part: lax.all_gather(part, axis), value)]
    pallas_call x0 -> x4, Pallas kernels: none -> 9.13 us  [the longest x1 2.96 us: shards(): pl.pallas_call(functools.partial(backward_body, dims), out_shape=(jax.Sha...]
    unnamed x109 -> x42, local copies, waits for them, and re-layouts: 11.4 us -> 5.14 us
    dot_general x6 -> x0, matrix products: 6.02 us -> none  [the longest x2 4.42 us: kernel_grad(): jnp.einsum('odhw,kdhw->ok', out_grad, stacked, preferred_element_type=jnp...]
    squeeze x35 -> x0, local copies, waits for them, and re-layouts: 5.99 us -> none  [correlate(): kernel[a, b, c]]
    ppermute x8 -> x15, waiting for transfers between devices: 10.8 us -> 5.1 us  [the longest x3 2.59 us: partners(): lax.ppermute(value, axis, [(i, i ^ s) for i in range(count)])]
    ppermute x8 -> x15, starting transfers between devices: 17.4 us -> 20.7 us  [the longest x6 8.38 us: shards(): lax.ppermute(pay, axis, [(i, i ^ s) for i in range(count)])]
  transfers between devices with their start and end apart: 8 -> 15, of which waited for: 3 -> 5; matrix products, arithmetic and copies ran while one was open for 7% -> 12% of each run, Pallas kernels for 0% -> 4%
where the time goes in v1:
time: 47.8 us; the launch traced here: 47.3 us
  starting transfers between devices  20.7 us (43%)
  Pallas kernels  9.13 us (19%)
  local copies, waits for them, and re-layouts  8.99 us (19%)
  waiting for transfers between devices  5.1 us (11%)
  other arithmetic  2.48 us (5%)
  between operations  0.93 us (2%)
    ppermute x6, starting transfers between devices, shards(): lax.ppermute(pay, axis, [(i, i ^ s) for i in range(count)])  8.38 us
    ppermute x1, starting transfers between devices, shards(): z_one = lax.ppermute(own, 'space', swap_pairs(space, 0))  5.91 us
    unnamed x42, local copies, waits for them, and re-layouts  5.14 us
    ppermute x3, starting transfers between devices, partners(): lax.ppermute(value, axis, [(i, i ^ s) for i in range(count)])  4.39 us
    pallas_call x1, Pallas kernels, shards(): pl.pallas_call(functools.partial(backward_body, dims), out_shape=(jax.Sha...  2.96 us
    pallas_call x1, Pallas kernels, shards(): pl.pallas_call(functools.partial(forward_body, dims), out_shape=(jax.Shap...  2.77 us
    ppermute x3, waiting for transfers between devices, partners(): lax.ppermute(value, axis, [(i, i ^ s) for i in range(count)])  2.59 us
    ppermute x6, waiting for transfers between devices, shards(): lax.ppermute(pay, axis, [(i, i ^ s) for i in range(count)])  2.49 us
  transfers between devices with their start and end apart: 15, of which 5 were waited for; matrix products, arithmetic and copies ran while one was open for 12% of the time, Pallas kernels for 4%

profile of v1, /device:TPU:0, one launch (start us, length us, event | category | flops | bytes accessed | tf_op | source)
XLA Modules:
  0.0 47.3 jit_solution(16019952161395390700)
XLA Ops:
  0.6 0.9 %copy.32 = bf16[4,4,8,256]{3,2,1,0:T(8,128)(2,1)S(1)} copy(bf16[4,4,8,256]{3,1,0,2:T(4,128)(2,1)} %bitcast.23) | data formatting | bytes 131072 | tf_op jit(solution)/shard_map/transpose | solution.py:311
  1.5 0.7 %collective-permute-start = (bf16[4,32,256]{2,1,0:T(8,128)(2,1)S(1)}, bf16[4,32,256]{2,1,0:T(8,128)(2,1)S(1)}, u32[]{:S(2)}, u32[]{:S(2)}) collective-permute-start(bf16[4,32,256]{2,1,0:T(8,128)(2,1)S(1)} %bitcast.18), channel_id=1, source_target_pairs={{0,0},{4,8},{8,4},{12,12},{1,1},{5,9},{9,5},{13,13},{2,2},{6,10},{... | collective-permute-start | bytes 196616 | tf_op jit(solution)/shard_map/ppermute | solution.py:313
  2.2 5.9 %collective-permute-start.1 = (bf16[4,32,256]{2,1,0:T(8,128)(2,1)S(1)}, bf16[4,32,256]{2,1,0:T(8,128)(2,1)S(1)}, u32[]{:S(2)}, u32[]{:S(2)}) collective-permute-start(bf16[4,32,256]{2,1,0:T(8,128)(2,1)S(1)} %bitcast.19), channel_id=1, source_target_pairs={{0,4},{4,0},{8,12},{12,8},{1,5},{5,1},{9,13},{13,9},{2,6},{6,2},{1... | collective-permute-start | bytes 196616 | tf_op jit(solution)/shard_map/ppermute | solution.py:312
  8.1 0.7 %copy-done.17 = f32[4,256]{1,0:T(4,128)S(1)} copy-done((f32[4,256]{1,0:T(4,128)S(1)}, f32[4,256]{1,0:T(4,128)}, u32[]{:S(2)}) %copy-start.17) | copy-done | bytes 4120
  8.8 0.7 %collective-permute-start.5 = (f32[20,256]{1,0:T(8,128)S(1)}, f32[20,256]{1,0:T(8,128)S(1)}, u32[]{:S(2)}, u32[]{:S(2)}) collective-permute-start(f32[20,256]{1,0:T(8,128)S(1)} %constant_dynamic-update-slice_fusion.ex_ref), channel_id=1, source_target_pairs={{0,0},{4,8},{8,4},{12,12},{1,1},{5,9},{9,5},{13,13},{2,2},{6,10},{... | collective-permute-start | bytes 61448 | tf_op jit(solution)/shard_map/ppermute | solution.py:316
  9.9 0.6 %pad_convert_fusion.base1_ref = f32[24,384]{1,0:T(8,128)} fusion(bf16[24,288]{1,0:T(8,128)(2,1)S(1)} %reshape.37), kind=kLoop, calls=%fused_computation.6 | loop fusion | flops 9216 | bytes 50688 | tf_op jit(solution)/shard_map/jit(_pad)/pad | solution.py:333
  10.8 0.7 %copy-done = bf16[4,96,256]{2,1,0:T(8,128)(2,1)} copy-done((bf16[4,96,256]{2,1,0:T(8,128)(2,1)}, bf16[4,96,256]{2,1,0:T(8,128)(2,1)S(1)}, u32[]{:S(2)}) %copy-start) | copy-done | bytes 196632
  11.5 0.7 %collective-permute-start.3 = (bf16[2,96,256]{2,1,0:T(8,128)(2,1)S(1)}, bf16[2,96,256]{2,1,0:T(8,128)(2,1)S(1)}, u32[]{:S(2)}, u32[]{:S(2)}) collective-permute-start(bf16[2,96,256]{2,1,0:T(8,128)(2,1)S(1)} %get-tuple-element.27), channel_id=1, source_target_pairs={{0,0},{1,2},{2,1},{3,3},{4,4},{5,6},{6,5},{7,7},{8,8},{9,10},{10,9... | collective-permute-start | bytes 294920 | tf_op jit(solution)/shard_map/ppermute | solution.py:326
  12.1 0.6 %pad_convert_fusion.3.base2_ref = f32[8,256]{1,0:T(8,128)} fusion(bf16[3,240]{1,0:T(4,128)(2,1)S(1)} %reshape.38), kind=kLoop, calls=%fused_computation.13 | loop fusion | flops 2048 | bytes 9632 | tf_op jit(solution)/shard_map/jit(_pad)/pad | solution.py:336
  12.7 0.7 %copy-done.18 = f32[8]{0:T(128)S(1)} copy-done((f32[8]{0:T(128)S(1)}, f32[8]{0:T(128)}, u32[]{:S(2)}) %copy-start.18) | copy-done | bytes 56
  13.4 0.7 %copy.21.bias_ref = f32[8,1]{1,0:T(8,128)} copy(f32[8,1]{0,1:T(1,128)S(1)} %bitcast.26) | data formatting | bytes 64 | tf_op jit(solution)/shard_map/broadcast_in_dim | solution.py:363
  14.3 0.6 %copy-done.10 = f32[20,256]{1,0:T(8,128)} copy-done((f32[20,256]{1,0:T(8,128)}, f32[20,256]{1,0:T(8,128)S(1)}, u32[]{:S(2)}) %copy-start.10) | copy-done | bytes 20504
  14.9 0.6 %copy-done.3 = bf16[2,96,256]{2,1,0:T(8,128)(2,1)} copy-done((bf16[2,96,256]{2,1,0:T(8,128)(2,1)}, bf16[2,96,256]{2,1,0:T(8,128)(2,1)S(1)}, u32[]{:S(2)}) %copy-start.3) | copy-done | bytes 98328
  15.6 2.8 %forward.1 = (f32[32,256]{1,0:T(8,128)}, f32[6,48,256]{2,1,0:T(8,128)}, bf16[7,64,256]{2,1,0:T(8,128)(2,1)}, bf16[7,64,256]{2,1,0:T(8,128)(2,1)}, f32[8,256]{1,0:T(8,128)}) custom-call(bf16[4,96,256]{2,1,0:T(8,128)(2,1)} %copy-done, bf16[2,96,256]{2,1,0:T(8,128)(2,1)} %copy-done.2, bf16[2,96,256]{2,1,0:T(8,128)(2,1)} %copy-done.3, f32[20,256]{1,0:T(8,128)} %copy-done.4, ...), custom_call_target="tpu_custom_call" | custom-call | tf_op jit(solution)/shard_map/forward/pallas_call | solution.py:348
  18.3 3.0 %collective-permute-start.6 = (f32[32,256]{1,0:T(8,128)}, f32[32,256]{1,0:T(8,128)S(1)}, u32[]{:S(2)}, u32[]{:S(2)}) collective-permute-start(f32[32,256]{1,0:T(8,128)} %get-tuple-element.16.refs_0_), channel_id=1, source_target_pairs={{0,1},{1,0},{2,3},{3,2},{4,5},{5,4},{6,7},{7,6},{8,9},{9,8},{10,11... | collective-permute-start | bytes 98312 | tf_op jit(solution)/shard_map/ppermute | solution.py:25
  21.3 1.1 %collective-permute-start.7 = (f32[32,256]{1,0:T(8,128)}, f32[32,256]{1,0:T(8,128)S(1)}, u32[]{:S(2)}, u32[]{:S(2)}) collective-permute-start(f32[32,256]{1,0:T(8,128)} %get-tuple-element.16.refs_0_), channel_id=1, source_target_pairs={{0,2},{1,3},{2,0},{3,1},{4,6},{5,7},{6,4},{7,5},{8,10},{9,11},{10,... | collective-permute-start | bytes 98312 | tf_op jit(solution)/shard_map/ppermute | solution.py:25
  22.7 0.6 %pad_convert_fusion.2.refs_8_ = f32[24,128]{1,0:T(8,128)} fusion(bf16[24,24]{1,0:T(8,128)(2,1)S(1)} %copy.25), kind=kLoop, calls=%fused_computation.12 | loop fusion | flops 3072 | bytes 13440 | tf_op jit(solution)/shard_map/jit(_pad)/pad | solution.py:339
  23.3 2.1 %collective-permute-done.7.refs_2_ = f32[32,256]{1,0:T(8,128)S(1)} collective-permute-done((f32[32,256]{1,0:T(8,128)}, f32[32,256]{1,0:T(8,128)S(1)}, u32[]{:S(2)}, u32[]{:S(2)}) %collective-permute-start.7) | collective-permute-done | bytes 32800 | tf_op jit(solution)/shard_map/ppermute | solution.py:25
  25.4 0.5 %collective-permute-done.8.refs_3_ = f32[32,256]{1,0:T(8,128)S(1)} collective-permute-done((f32[32,256]{1,0:T(8,128)}, f32[32,256]{1,0:T(8,128)S(1)}, u32[]{:S(2)}, u32[]{:S(2)}) %collective-permute-start.8) | collective-permute-done | bytes 32800 | tf_op jit(solution)/shard_map/ppermute | solution.py:25
  26.5 3.0 %backward.1 = (f32[32,128]{1,0:T(8,128)}, bf16[6,48,256]{2,1,0:T(8,128)(2,1)}, f32[4,256]{1,0:T(4,128)}) custom-call(f32[32,256]{1,0:T(8,128)} %get-tuple-element.16.refs_0_, f32[32,256]{1,0:T(8,128)} %copy-done.7, f32[32,256]{1,0:T(8,128)} %copy-done.8, f32[32,256]{1,0:T(8,128)} %copy-done.9, f32[8,256]{1,0:T(8,128)} %get-tuple-element.17.refs_4_, ...), custom_call_target="tpu_custom_call" | custom-call | tf_op jit(solution)/shard_map/backward/pallas_call | solution.py:366
  29.5 1.3 %collective-permute-start.10 = (f32[32,128]{1,0:T(8,128)}, f32[32,128]{1,0:T(8,128)S(1)}, u32[]{:S(2)}, u32[]{:S(2)}) collective-permute-start(f32[32,128]{1,0:T(8,128)} %get-tuple-element.22), channel_id=1, source_target_pairs={{0,2},{1,3},{2,0},{3,1},{4,6},{5,7},{6,4},{7,5},{8,10},{9,11},{10,... | collective-permute-start | bytes 49160 | tf_op jit(solution)/shard_map/ppermute | solution.py:383
  31.0 0.6 %collective-permute-start.9 = (f32[32,128]{1,0:T(8,128)}, f32[32,128]{1,0:T(8,128)S(1)}, u32[]{:S(2)}, u32[]{:S(2)}) collective-permute-start(f32[32,128]{1,0:T(8,128)} %get-tuple-element.22), channel_id=1, source_target_pairs={{0,1},{1,0},{2,3},{3,2},{4,5},{5,4},{6,7},{7,6},{8,9},{9,8},{10,11... | collective-permute-start | bytes 49160 | tf_op jit(solution)/shard_map/ppermute | solution.py:383
  32.0 1.5 %collective-permute-done.10 = f32[32,128]{1,0:T(8,128)S(1)} collective-permute-done((f32[32,128]{1,0:T(8,128)}, f32[32,128]{1,0:T(8,128)S(1)}, u32[]{:S(2)}, u32[]{:S(2)}) %collective-permute-start.10) | collective-permute-done | bytes 16416 | tf_op jit(solution)/shard_map/ppermute | solution.py:383
  33.5 0.9 %collective-permute-done.11 = f32[32,128]{1,0:T(8,128)S(1)} collective-permute-done((f32[32,128]{1,0:T(8,128)}, f32[32,128]{1,0:T(8,128)S(1)}, u32[]{:S(2)}, u32[]{:S(2)}) %collective-permute-start.11) | collective-permute-done | bytes 16416 | tf_op jit(solution)/shard_map/ppermute | solution.py:383
  34.3 3.8 %collective-permute-start.12 = (f32[32,128]{1,0:T(8,128)S(1)}, f32[32,128]{1,0:T(8,128)S(1)}, u32[]{:S(2)}, u32[]{:S(2)}) collective-permute-start(f32[32,128]{1,0:T(8,128)S(1)} %add_add_fusion.refs_0_), channel_id=1, source_target_pairs={{0,4},{4,0},{8,12},{12,8},{1,5},{5,1},{9,13},{13,9},{2,6},{6,2},{1... | collective-permute-start | bytes 49160 | tf_op jit(solution)/shard_map/ppermute | solution.py:383
  38.1 1.1 %collective-permute-start.13 = (f32[32,128]{1,0:T(8,128)S(1)}, f32[32,128]{1,0:T(8,128)S(1)}, u32[]{:S(2)}, u32[]{:S(2)}) collective-permute-start(f32[32,128]{1,0:T(8,128)S(1)} %add_add_fusion.refs_0_), channel_id=1, source_target_pairs={{0,8},{4,12},{8,0},{12,4},{1,9},{5,13},{9,1},{13,5},{2,10},{6,14},... | collective-permute-start | bytes 49160 | tf_op jit(solution)/shard_map/ppermute | solution.py:383
  39.2 1.4 %collective-permute-start.14 = (f32[32,128]{1,0:T(8,128)S(1)}, f32[32,128]{1,0:T(8,128)S(1)}, u32[]{:S(2)}, u32[]{:S(2)}) collective-permute-start(f32[32,128]{1,0:T(8,128)S(1)} %add_add_fusion.refs_0_), channel_id=1, source_target_pairs={{0,12},{4,8},{8,4},{12,0},{1,13},{5,9},{9,5},{13,1},{2,14},{6,10},... | collective-permute-start | bytes 49160 | tf_op jit(solution)/shard_map/ppermute | solution.py:383
  40.6 0.6 %pad_convert_fusion.1.base4_ref = f32[24,256]{1,0:T(8,128)} fusion(bf16[24,144]{1,0:T(8,128)(2,1)S(1)} %reshape.40), kind=kLoop, calls=%fused_computation.8 | loop fusion | flops 6144 | bytes 31488 | tf_op jit(solution)/shard_map/jit(_pad)/pad | solution.py:344
  41.2 1.9 %volume_grad.1 = bf16[4,32,256]{2,1,0:T(8,128)(2,1)} custom-call(bf16[6,48,256]{2,1,0:T(8,128)(2,1)} %get-tuple-element.21.pg_ref, f32[24,256]{1,0:T(8,128)} %pad_convert_fusion.1.base4_ref), custom_call_target="tpu_custom_call" | custom-call | tf_op jit(solution)/shard_map/volume_grad/pallas_call | solution.py:387
  43.1 1.5 %copy.31 = bf16[4,4,8,256]{3,1,0,2:T(4,128)(2,1)} copy(bf16[4,4,8,256]{3,2,1,0:T(8,128)(2,1)} %bitcast.21) | data formatting | bytes 131072 | tf_op jit(solution)/shard_map/reshape | solution.py:392
  45.2 0.6 %copy-done.16 = f32[32,128]{1,0:T(8,128)} copy-done((f32[32,128]{1,0:T(8,128)}, f32[32,128]{1,0:T(8,128)S(1)}, u32[]{:S(2)}) %copy-start.16) | copy-done | bytes 16408
  45.8 1.5 %finish.1 = (f32[3,3,3,8,8]{4,3,2,1,0:T(8,128)}, f32[1,8]{1,0:T(1,128)}, f32[3,3,3,8]{3,2,1,0:T(4,128)}) custom-call(f32[32,128]{1,0:T(8,128)} %copy-done.5, f32[32,128]{1,0:T(8,128)} %copy-done.14, f32[32,128]{1,0:T(8,128)} %copy-done.15, f32[32,128]{1,0:T(8,128)} %copy-done.16), custom_call_target="tpu_custom_call" | custom-call | tf_op jit(solution)/shard_map/finish/pallas_call | solution.py:395
  (68 shorter events, 3.0 us)
Async XLA Ops:
  0.6 7.5 %copy-start.13 = (f32[4,4,256]{2,1,0:T(4,128)S(1)}, f32[4,4,256]{2,1,0:T(4,128)}, u32[]{:S(2)}) copy-start(f32[4,4,256]{2,1,0:T(4,128)} %param.10) | copy-start | bytes 49156
  1.5 9.2 %collective-permute-start = (bf16[4,32,256]{2,1,0:T(8,128)(2,1)S(1)}, bf16[4,32,256]{2,1,0:T(8,128)(2,1)S(1)}, u32[]{:S(2)}, u32[]{:S(2)}) collective-permute-start(bf16[4,32,256]{2,1,0:T(8,128)(2,1)S(1)} %bitcast.18), channel_id=1, source_target_pairs={{0,0},{4,8},{8,4},{12,12},{1,1},{5,9},{9,5},{13,13},{2,2},{6,10},{... | collective-permute-start | bytes 196616 | tf_op jit(solution)/shard_map/ppermute | solution.py:313
  2.2 8.5 %collective-permute-start.1 = (bf16[4,32,256]{2,1,0:T(8,128)(2,1)S(1)}, bf16[4,32,256]{2,1,0:T(8,128)(2,1)S(1)}, u32[]{:S(2)}, u32[]{:S(2)}) collective-permute-start(bf16[4,32,256]{2,1,0:T(8,128)(2,1)S(1)} %bitcast.19), channel_id=1, source_target_pairs={{0,4},{4,0},{8,12},{12,8},{1,5},{5,1},{9,13},{13,9},{2,6},{6,2},{1... | collective-permute-start | bytes 196616 | tf_op jit(solution)/shard_map/ppermute | solution.py:312
  8.1 0.7 %copy-start.17 = (f32[4,256]{1,0:T(4,128)S(1)}, f32[4,256]{1,0:T(4,128)}, u32[]{:S(2)}) copy-start(f32[4,256]{1,0:T(4,128)} %param.11) | copy-start | bytes 12292
  8.1 1.4 %copy-start.1 = (bf16[3,3,3,8,8]{4,3,2,1,0:T(8,128)(2,1)S(1)}, bf16[3,3,3,8,8]{4,3,2,1,0:T(8,128)(2,1)}, u32[]{:S(2)}) copy-start(bf16[3,3,3,8,8]{4,3,2,1,0:T(8,128)(2,1)} %param.7) | copy-start | bytes 10372
  8.8 0.7 %copy-start.4 = (f32[20,256]{1,0:T(8,128)}, f32[20,256]{1,0:T(8,128)S(1)}, u32[]{:S(2)}) copy-start(f32[20,256]{1,0:T(8,128)S(1)} %constant_dynamic-update-slice_fusion.ex_ref) | copy-start | bytes 61444
  8.8 5.5 %collective-permute-start.4 = (f32[20,256]{1,0:T(8,128)S(1)}, f32[20,256]{1,0:T(8,128)S(1)}, u32[]{:S(2)}, u32[]{:S(2)}) collective-permute-start(f32[20,256]{1,0:T(8,128)S(1)} %constant_dynamic-update-slice_fusion.ex_ref), channel_id=1, source_target_pairs={{0,4},{4,0},{8,12},{12,8},{1,5},{5,1},{9,13},{13,9},{2,6},{6,2},{1... | collective-permute-start | bytes 61448 | tf_op jit(solution)/shard_map/ppermute | solution.py:315
  8.8 5.4 %collective-permute-start.5 = (f32[20,256]{1,0:T(8,128)S(1)}, f32[20,256]{1,0:T(8,128)S(1)}, u32[]{:S(2)}, u32[]{:S(2)}) collective-permute-start(f32[20,256]{1,0:T(8,128)S(1)} %constant_dynamic-update-slice_fusion.ex_ref), channel_id=1, source_target_pairs={{0,0},{4,8},{8,4},{12,12},{1,1},{5,9},{9,5},{13,13},{2,2},{6,10},{... | collective-permute-start | bytes 61448 | tf_op jit(solution)/shard_map/ppermute | solution.py:316
  9.9 0.7 %copy-start.6 = (bf16[3,3,3,8]{3,2,1,0:T(4,128)(2,1)S(1)}, bf16[3,3,3,8]{3,2,1,0:T(4,128)(2,1)}, u32[]{:S(2)}) copy-start(bf16[3,3,3,8]{3,2,1,0:T(4,128)(2,1)} %param.9) | copy-start | bytes 1300
  10.8 0.7 %copy-start = (bf16[4,96,256]{2,1,0:T(8,128)(2,1)}, bf16[4,96,256]{2,1,0:T(8,128)(2,1)S(1)}, u32[]{:S(2)}) copy-start(bf16[4,96,256]{2,1,0:T(8,128)(2,1)S(1)} %pad_maximum_fusion.mid_ref) | copy-start | bytes 589828
  11.5 2.8 %collective-permute-start.2 = (bf16[2,96,256]{2,1,0:T(8,128)(2,1)S(1)}, bf16[2,96,256]{2,1,0:T(8,128)(2,1)S(1)}, u32[]{:S(2)}, u32[]{:S(2)}) collective-permute-start(bf16[2,96,256]{2,1,0:T(8,128)(2,1)S(1)} %get-tuple-element.28), channel_id=1, source_target_pairs={{0,1},{1,0},{2,3},{3,2},{4,5},{5,4},{6,7},{7,6},{8,9},{9,8},{10,11... | collective-permute-start | bytes 294920 | tf_op jit(solution)/shard_map/ppermute | solution.py:323
  11.5 2.8 %collective-permute-start.3 = (bf16[2,96,256]{2,1,0:T(8,128)(2,1)S(1)}, bf16[2,96,256]{2,1,0:T(8,128)(2,1)S(1)}, u32[]{:S(2)}, u32[]{:S(2)}) collective-permute-start(bf16[2,96,256]{2,1,0:T(8,128)(2,1)S(1)} %get-tuple-element.27), channel_id=1, source_target_pairs={{0,0},{1,2},{2,1},{3,3},{4,4},{5,6},{6,5},{7,7},{8,8},{9,10},{10,9... | collective-permute-start | bytes 294920 | tf_op jit(solution)/shard_map/ppermute | solution.py:326
  12.7 0.7 %copy-start.18 = (f32[8]{0:T(128)S(1)}, f32[8]{0:T(128)}, u32[]{:S(2)}) copy-start(f32[8]{0:T(128)} %param.8) | copy-start | bytes 100
  14.3 0.6 %copy-start.10 = (f32[20,256]{1,0:T(8,128)}, f32[20,256]{1,0:T(8,128)S(1)}, u32[]{:S(2)}) copy-start(f32[20,256]{1,0:T(8,128)S(1)} %collective-permute-done.4.exa_ref) | copy-start | bytes 61444
  14.3 0.6 %copy-start.11 = (f32[20,256]{1,0:T(8,128)}, f32[20,256]{1,0:T(8,128)S(1)}, u32[]{:S(2)}) copy-start(f32[20,256]{1,0:T(8,128)S(1)} %collective-permute-done.5.exb_ref) | copy-start | bytes 61444
  14.3 0.6 %copy-start.2 = (bf16[2,96,256]{2,1,0:T(8,128)(2,1)}, bf16[2,96,256]{2,1,0:T(8,128)(2,1)S(1)}, u32[]{:S(2)}) copy-start(bf16[2,96,256]{2,1,0:T(8,128)(2,1)S(1)} %collective-permute-done.2.da_ref) | copy-start | bytes 294916
  14.9 0.6 %copy-start.3 = (bf16[2,96,256]{2,1,0:T(8,128)(2,1)}, bf16[2,96,256]{2,1,0:T(8,128)(2,1)S(1)}, u32[]{:S(2)}) copy-start(bf16[2,96,256]{2,1,0:T(8,128)(2,1)S(1)} %collective-permute-done.3.db_ref) | copy-start | bytes 294916
  18.3 5.0 %collective-permute-start.6 = (f32[32,256]{1,0:T(8,128)}, f32[32,256]{1,0:T(8,128)S(1)}, u32[]{:S(2)}, u32[]{:S(2)}) collective-permute-start(f32[32,256]{1,0:T(8,128)} %get-tuple-element.16.refs_0_), channel_id=1, source_target_pairs={{0,1},{1,0},{2,3},{3,2},{4,5},{5,4},{6,7},{7,6},{8,9},{9,8},{10,11... | collective-permute-start | bytes 98312 | tf_op jit(solution)/shard_map/ppermute | solution.py:25
  21.3 4.1 %collective-permute-start.7 = (f32[32,256]{1,0:T(8,128)}, f32[32,256]{1,0:T(8,128)S(1)}, u32[]{:S(2)}, u32[]{:S(2)}) collective-permute-start(f32[32,256]{1,0:T(8,128)} %get-tuple-element.16.refs_0_), channel_id=1, source_target_pairs={{0,2},{1,3},{2,0},{3,1},{4,6},{5,7},{6,4},{7,5},{8,10},{9,11},{10,... | collective-permute-start | bytes 98312 | tf_op jit(solution)/shard_map/ppermute | solution.py:25
  22.4 3.6 %collective-permute-start.8 = (f32[32,256]{1,0:T(8,128)}, f32[32,256]{1,0:T(8,128)S(1)}, u32[]{:S(2)}, u32[]{:S(2)}) collective-permute-start(f32[32,256]{1,0:T(8,128)} %get-tuple-element.16.refs_0_), channel_id=1, source_target_pairs={{0,3},{1,2},{2,1},{3,0},{4,7},{5,6},{6,5},{7,4},{8,11},{9,10},{10,... | collective-permute-start | bytes 98312 | tf_op jit(solution)/shard_map/ppermute | solution.py:25
  23.3 2.6 %copy-start.7 = (f32[32,256]{1,0:T(8,128)}, f32[32,256]{1,0:T(8,128)S(1)}, u32[]{:S(2)}) copy-start(f32[32,256]{1,0:T(8,128)S(1)} %collective-permute-done.6.refs_1_) | copy-start | bytes 98308
  25.4 0.6 %copy-start.8 = (f32[32,256]{1,0:T(8,128)}, f32[32,256]{1,0:T(8,128)S(1)}, u32[]{:S(2)}) copy-start(f32[32,256]{1,0:T(8,128)S(1)} %collective-permute-done.7.refs_2_) | copy-start | bytes 98308
  25.9 0.6 %copy-start.9 = (f32[32,256]{1,0:T(8,128)}, f32[32,256]{1,0:T(8,128)S(1)}, u32[]{:S(2)}) copy-start(f32[32,256]{1,0:T(8,128)S(1)} %collective-permute-done.8.refs_3_) | copy-start | bytes 98308
  29.5 3.9 %collective-permute-start.10 = (f32[32,128]{1,0:T(8,128)}, f32[32,128]{1,0:T(8,128)S(1)}, u32[]{:S(2)}, u32[]{:S(2)}) collective-permute-start(f32[32,128]{1,0:T(8,128)} %get-tuple-element.22), channel_id=1, source_target_pairs={{0,2},{1,3},{2,0},{3,1},{4,6},{5,7},{6,4},{7,5},{8,10},{9,11},{10,... | collective-permute-start | bytes 49160 | tf_op jit(solution)/shard_map/ppermute | solution.py:383
  30.8 3.5 %collective-permute-start.11 = (f32[32,128]{1,0:T(8,128)}, f32[32,128]{1,0:T(8,128)S(1)}, u32[]{:S(2)}, u32[]{:S(2)}) collective-permute-start(f32[32,128]{1,0:T(8,128)} %get-tuple-element.22), channel_id=1, source_target_pairs={{0,3},{1,2},{2,1},{3,0},{4,7},{5,6},{6,5},{7,4},{8,11},{9,10},{10,... | collective-permute-start | bytes 49160 | tf_op jit(solution)/shard_map/ppermute | solution.py:383
  31.0 3.3 %collective-permute-start.9 = (f32[32,128]{1,0:T(8,128)}, f32[32,128]{1,0:T(8,128)S(1)}, u32[]{:S(2)}, u32[]{:S(2)}) collective-permute-start(f32[32,128]{1,0:T(8,128)} %get-tuple-element.22), channel_id=1, source_target_pairs={{0,1},{1,0},{2,3},{3,2},{4,5},{5,4},{6,7},{7,6},{8,9},{9,8},{10,11... | collective-permute-start | bytes 49160 | tf_op jit(solution)/shard_map/ppermute | solution.py:383
  31.8 2.5 %copy-start.12 = (f32[32,128]{1,0:T(8,128)S(1)}, f32[32,128]{1,0:T(8,128)}, u32[]{:S(2)}) copy-start(f32[32,128]{1,0:T(8,128)} %get-tuple-element.22) | copy-start | bytes 49156
  34.3 6.9 %copy-start.5 = (f32[32,128]{1,0:T(8,128)}, f32[32,128]{1,0:T(8,128)S(1)}, u32[]{:S(2)}) copy-start(f32[32,128]{1,0:T(8,128)S(1)} %add_add_fusion.refs_0_) | copy-start | bytes 49156
  34.3 10.2 %collective-permute-start.12 = (f32[32,128]{1,0:T(8,128)S(1)}, f32[32,128]{1,0:T(8,128)S(1)}, u32[]{:S(2)}, u32[]{:S(2)}) collective-permute-start(f32[32,128]{1,0:T(8,128)S(1)} %add_add_fusion.refs_0_), channel_id=1, source_target_pairs={{0,4},{4,0},{8,12},{12,8},{1,5},{5,1},{9,13},{13,9},{2,6},{6,2},{1... | collective-permute-start | bytes 49160 | tf_op jit(solution)/shard_map/ppermute | solution.py:383
  38.1 6.5 %collective-permute-start.13 = (f32[32,128]{1,0:T(8,128)S(1)}, f32[32,128]{1,0:T(8,128)S(1)}, u32[]{:S(2)}, u32[]{:S(2)}) collective-permute-start(f32[32,128]{1,0:T(8,128)S(1)} %add_add_fusion.refs_0_), channel_id=1, source_target_pairs={{0,8},{4,12},{8,0},{12,4},{1,9},{5,13},{9,1},{13,5},{2,10},{6,14},... | collective-permute-start | bytes 49160 | tf_op jit(solution)/shard_map/ppermute | solution.py:383
  39.2 5.5 %collective-permute-start.14 = (f32[32,128]{1,0:T(8,128)S(1)}, f32[32,128]{1,0:T(8,128)S(1)}, u32[]{:S(2)}, u32[]{:S(2)}) collective-permute-start(f32[32,128]{1,0:T(8,128)S(1)} %add_add_fusion.refs_0_), channel_id=1, source_target_pairs={{0,12},{4,8},{8,4},{12,0},{1,13},{5,9},{9,5},{13,1},{2,14},{6,10},... | collective-permute-start | bytes 49160 | tf_op jit(solution)/shard_map/ppermute | solution.py:383
  44.6 0.6 %copy-start.15 = (f32[32,128]{1,0:T(8,128)}, f32[32,128]{1,0:T(8,128)S(1)}, u32[]{:S(2)}) copy-start(f32[32,128]{1,0:T(8,128)S(1)} %collective-permute-done.13.refs_2_) | copy-start | bytes 49156
  (2 other events, 1.2 us)

commit v2 on v1

--- a/solution.py
+++ b/solution.py
@@ -53,6 +53,21 @@
 
 def right(x, amount):
     return x if amount == 0 else pltpu.roll(x, amount, 1)
+
+
+def call(body, name, outs, *operands, scratch=()):
+    operands = [pltpu.with_memory_space_constraint(x, pltpu.VMEM) for x in operands]
+    return pl.pallas_call(
+        body,
+        out_shape=tuple(
+            pltpu.VMEM(shape, dtype) if inside else jax.ShapeDtypeStruct(shape, dtype)
+            for shape, dtype, inside in outs
+        ),
+        in_specs=[pl.BlockSpec(memory_space=pltpu.VMEM)] * len(operands),
+        out_specs=tuple(pl.BlockSpec(memory_space=pltpu.VMEM) for _ in outs),
+        scratch_shapes=list(scratch),
+        name=name,
+    )(*operands)
 
 
 def dot(a, b):
@@ -120,7 +135,11 @@
         for r in range(rows + 6):
             bands.append(right(piece, chans * r))
     band1 = jnp.concatenate(bands, axis=0)[:, : 3 * xr].astype(BF16)
-    bias = jnp.concatenate([bias_ref[...]] * (rows + 6), axis=0)
+    diag = lax.broadcasted_iota(jnp.int32, (chans, chans), 0) == lax.broadcasted_iota(
+        jnp.int32, (chans, chans), 1
+    )
+    bias = jnp.sum(jnp.where(diag, bias_ref[...], 0.0), axis=1, keepdims=True)
+    bias = jnp.concatenate([jnp.broadcast_to(bias, (chans, width))] * (rows + 6), axis=0)
     row_at = zi * rows - 3 + lax.broadcasted_iota(jnp.int32, (hr, width), 0) // chans
     row_ok = ((row_at >= 0) & (row_at < space * rows)).astype(F32)
     for p in range(planes + 2):
@@ -157,7 +176,7 @@
     planes, rows, chans, width, disp, space = dims
     logit_refs = refs[:disp]
     cot_ref, slope_ref, hid_ref, xs_ref, base3_ref = refs[disp : disp + 5]
-    pay_ref, pg_ref, disp_ref, l_ref, s_ref = refs[disp + 5 :]
+    pay_ref, pg_ref, disp_ref, l_ref = refs[disp + 5 :]
     di = lax.axis_index("disp")
     lr = rows + 4
     hr = (rows + 2) * chans
@@ -271,11 +290,15 @@
         for r in range(rows):
             bands.append(right(piece, chans * r))
     band4 = jnp.concatenate(bands, axis=0)[:, : 3 * hr].astype(BF16)
+    to = lax.broadcasted_iota(jnp.int32, (3 * n, 3 * n), 0)
+    at = lax.broadcasted_iota(jnp.int32, (3 * n, 3 * n), 1)
+    source = (to // n) * n + (to % rows) * chans + (to % n) // rows
+    band4 = dot((at == source).astype(BF16), band4).astype(BF16)
     for p in range(planes):
         y = dot(band4, pg_ref[p : p + 3].reshape(3 * hr, width))
-        out_ref[p] = (
-            y[n : 2 * n] + shift_down(y[:n], lane) + shift_up(y[2 * n :], lane)
-        ).astype(BF16)
+        y = (y[n : 2 * n] + shift_down(y[:n], lane) + shift_up(y[2 * n :], lane)).astype(BF16)
+        for i in range(chans):
+            out_ref[i, p] = y[i * rows : (i + 1) * rows]
 
 
 def finish_body(chans, scale, *refs):
@@ -345,37 +368,36 @@
 
     lr = rows + 4
     hr = rows + 6
-    logits, slope, hid, xs, cot = pl.pallas_call(
+    logits, slope, hid, xs, cot = call(
         functools.partial(forward_body, dims),
-        out_shape=(
-            jax.ShapeDtypeStruct((planes * lr, width), F32),
-            jax.ShapeDtypeStruct((planes + 2, (rows + 2) * chans, width), F32),
-            jax.ShapeDtypeStruct((planes + 3, (rows + 4) * chans, width), BF16),
-            jax.ShapeDtypeStruct((planes + 3, (rows + 4) * chans, width), BF16),
-            jax.ShapeDtypeStruct((lr, width), F32),
-        ),
-        scratch_shapes=[
+        "forward",
+        (
+            ((planes * lr, width), F32, True),
+            ((planes + 2, (rows + 2) * chans, width), F32, True),
+            ((planes + 3, (rows + 4) * chans, width), BF16, True),
+            ((planes + 3, (rows + 4) * chans, width), BF16, True),
+            ((lr, width), F32, True),
+        ),
+        mid, d_one, d_two, extra, e_one, e_two, base1, b_first[None, :], base2,
+        scratch=[
             pltpu.VMEM(((planes + 4) * xr * chans, width), BF16),
             pltpu.VMEM(((planes + 2) * hr * chans, width), BF16),
             pltpu.VMEM((planes, lr, width), F32),
         ],
-        name="forward",
-    )(mid, d_one, d_two, extra, e_one, e_two, base1, b_first[:, None], base2)
+    )
 
     pieces = [logits] + partners(logits, "disp")
-    pay, pg, disparity = pl.pallas_call(
+    pay, pg, disparity = call(
         functools.partial(backward_body, dims),
-        out_shape=(
-            jax.ShapeDtypeStruct((3 * chans + 8, 128), F32),
-            jax.ShapeDtypeStruct((planes + 2, (rows + 2) * chans, width), BF16),
-            jax.ShapeDtypeStruct((rows, width), F32),
-        ),
-        scratch_shapes=[
-            pltpu.VMEM((disp + 2, planes * lr, width), F32),
-            pltpu.VMEM(((planes + 4) * lr, width), F32),
-        ],
-        name="backward",
-    )(*pieces, cot, slope, hid, xs, base3)
+        "backward",
+        (
+            ((3 * chans + 8, 128), F32, True),
+            ((planes + 2, (rows + 2) * chans, width), BF16, True),
+            ((rows, width), F32, False),
+        ),
+        *pieces, cot, slope, hid, xs, base3,
+        scratch=[pltpu.VMEM((disp + 2, planes * lr, width), F32)],
+    )
 
     stages = [("disp", s) for s in radix_stages(disp)] + [("space", s) for s in radix_stages(space)]
     for n, (axis, steps) in enumerate(stages):
@@ -384,23 +406,24 @@
         if n < len(stages) - 1:
             pay = tree_sum(parts)
 
-    volume_grad = pl.pallas_call(
+    (volume_grad,) = call(
         functools.partial(volume_grad_body, dims),
-        out_shape=jax.ShapeDtypeStruct((planes, rows * chans, width), BF16),
-        name="volume_grad",
-    )(pg, base4)
-    volume_grad = jnp.transpose(volume_grad.reshape(planes, rows, chans, width), (2, 0, 1, 3))
+        "volume_grad",
+        (((chans, planes, rows, width), BF16, False),),
+        pg, base4,
+    )
 
     scale = 16.0 / math.sqrt(planes * disp * rows * space * width)
-    first_sum, bias_sum, second_sum = pl.pallas_call(
+    first_sum, bias_sum, second_sum = call(
         functools.partial(finish_body, chans, scale),
-        out_shape=(
-            jax.ShapeDtypeStruct((3, 3, 3, chans, chans), F32),
-            jax.ShapeDtypeStruct((1, chans), F32),
-            jax.ShapeDtypeStruct((3, 3, 3, chans), F32),
-        ),
-        name="finish",
-    )(*parts)
+        "finish",
+        (
+            ((3, 3, 3, chans, chans), F32, False),
+            ((1, chans), F32, False),
+            ((3, 3, 3, chans), F32, False),
+        ),
+        *parts,
+    )
     return (volume_grad, first_sum, bias_sum[0], second_sum, disparity)
 
 

time: 47.8 us -> 40.4 us (0.85)
  local copies, waits for them, and re-layouts: 8.99 us -> 3.18 us
  Pallas kernels: 9.13 us -> 4.5 us
  waiting for transfers between devices: 5.1 us -> 8.98 us
  other arithmetic: 2.48 us -> 0.06 us
  starting transfers between devices: 20.7 us -> 22.5 us
    pallas_call x4, Pallas kernels: 9.13 us -> 4.5 us  [call(): pl.pallas_call(body, out_shape=tuple((pltpu.VMEM(shape, dtype) if inside...]
    unnamed x42 -> x14, local copies, waits for them, and re-layouts: 5.14 us -> 1.5 us
    ppermute x6, waiting for transfers between devices: 2.49 us -> 5.1 us  [shards(): lax.ppermute(pay, axis, [(i, i ^ s) for i in range(count)])]
    ppermute x3, starting transfers between devices: 4.39 us -> 6.13 us  [partners(): lax.ppermute(value, axis, [(i, i ^ s) for i in range(count)])]
    reshape x1 -> x0, local copies, waits for them, and re-layouts: 1.49 us -> none  [shards(): volume_grad.reshape(planes, rows, chans, width)]
    ppermute x1, waiting for transfers between devices: 0.01 us -> 0.87 us  [shards(): e_one = lax.ppermute(extra, 'space', swap_pairs(space, 0))]
    broadcast_in_dim x1 -> x0, local copies, waits for them, and re-layouts: 0.67 us -> none  [shards(): b_first[:, None]]
    pad x1, other arithmetic: 0.62 us -> 0.01 us  [shards(): base1 = jnp.pad(base1, ((0, 0), (0, -base1.shape[1] % 128)))]
  transfers between devices with their start and end apart: 15 -> 15, of which waited for: 5 -> 7; matrix products, arithmetic and copies ran while one was open for 12% -> 3% of each run, Pallas kernels for 4% -> 3%
where the time goes in v2:
time: 40.4 us; the launch traced here: 40.1 us
  starting transfers between devices  22.5 us (56%)
  waiting for transfers between devices  8.98 us (22%)
  Pallas kernels  4.5 us (11%)
  local copies, waits for them, and re-layouts  3.18 us (8%)
  between operations  0.88 us (2%)
    ppermute x6, starting transfers between devices, shards(): lax.ppermute(pay, axis, [(i, i ^ s) for i in range(count)])  8.38 us
    ppermute x3, starting transfers between devices, partners(): lax.ppermute(value, axis, [(i, i ^ s) for i in range(count)])  6.13 us
    ppermute x1, starting transfers between devices, shards(): z_one = lax.ppermute(own, 'space', swap_pairs(space, 0))  5.91 us
    ppermute x6, waiting for transfers between devices, shards(): lax.ppermute(pay, axis, [(i, i ^ s) for i in range(count)])  5.1 us
    pallas_call x4, Pallas kernels, call(): pl.pallas_call(body, out_shape=tuple((pltpu.VMEM(shape, dtype) if inside...  4.5 us
    ppermute x3, waiting for transfers between devices, partners(): lax.ppermute(value, axis, [(i, i ^ s) for i in range(count)])  2.99 us
    unnamed x14, local copies, waits for them, and re-layouts  1.5 us
    ppermute x1, waiting for transfers between devices, shards(): e_one = lax.ppermute(extra, 'space', swap_pairs(space, 0))  0.87 us
  transfers between devices with their start and end apart: 15, of which 7 were waited for; matrix products, arithmetic and copies ran while one was open for 3% of the time, Pallas kernels for 3%

profile of v2, /device:TPU:0, one launch (start us, length us, event | category | flops | bytes accessed | tf_op | source)
XLA Modules:
  0.0 40.1 jit_solution(3045850433719247472)
XLA Ops:
  0.6 0.9 %copy.26 = bf16[4,4,8,256]{3,2,1,0:T(8,128)(2,1)S(1)} copy(bf16[4,4,8,256]{3,1,0,2:T(4,128)(2,1)} %bitcast.19) | data formatting | bytes 131072 | tf_op jit(solution)/shard_map/transpose | solution.py:334
  1.5 0.7 %collective-permute-start = (bf16[4,32,256]{2,1,0:T(8,128)(2,1)S(1)}, bf16[4,32,256]{2,1,0:T(8,128)(2,1)S(1)}, u32[]{:S(2)}, u32[]{:S(2)}) collective-permute-start(bf16[4,32,256]{2,1,0:T(8,128)(2,1)S(1)} %bitcast.15), channel_id=1, source_target_pairs={{0,0},{4,8},{8,4},{12,12},{1,1},{5,9},{9,5},{13,13},{2,2},{6,10},{... | collective-permute-start | bytes 196616 | tf_op jit(solution)/shard_map/ppermute | solution.py:336
  2.2 5.9 %collective-permute-start.1 = (bf16[4,32,256]{2,1,0:T(8,128)(2,1)S(1)}, bf16[4,32,256]{2,1,0:T(8,128)(2,1)S(1)}, u32[]{:S(2)}, u32[]{:S(2)}) collective-permute-start(bf16[4,32,256]{2,1,0:T(8,128)(2,1)S(1)} %bitcast.16), channel_id=1, source_target_pairs={{0,4},{4,0},{8,12},{12,8},{1,5},{5,1},{9,13},{13,9},{2,6},{6,2},{1... | collective-permute-start | bytes 196616 | tf_op jit(solution)/shard_map/ppermute | solution.py:335
  8.1 0.7 %copy-done.4 = f32[4,256]{1,0:T(4,128)S(1)} copy-done((f32[4,256]{1,0:T(4,128)S(1)}, f32[4,256]{1,0:T(4,128)}, u32[]{:S(2)}) %copy-start.4) | copy-done | bytes 4120
  8.8 0.7 %collective-permute-start.5 = (f32[20,256]{1,0:T(8,128)S(1)}, f32[20,256]{1,0:T(8,128)S(1)}, u32[]{:S(2)}, u32[]{:S(2)}) collective-permute-start(f32[20,256]{1,0:T(8,128)S(1)} %constant_dynamic-update-slice_fusion.ex_ref), channel_id=1, source_target_pairs={{0,0},{4,8},{8,4},{12,12},{1,1},{5,9},{9,5},{13,13},{2,2},{6,10},{... | collective-permute-start | bytes 61448 | tf_op jit(solution)/shard_map/ppermute | solution.py:339
  9.6 0.2 reshape.34
  9.9 0.7 %copy-done.2 = bf16[3,3,3,8]{3,2,1,0:T(4,128)(2,1)S(1)} copy-done((bf16[3,3,3,8]{3,2,1,0:T(4,128)(2,1)S(1)}, bf16[3,3,3,8]{3,2,1,0:T(4,128)(2,1)}, u32[]{:S(2)}) %copy-start.2) | copy-done | bytes 456
  10.6 0.1 reshape.35
  10.9 0.7 %collective-permute-start.3 = (bf16[2,96,256]{2,1,0:T(8,128)(2,1)S(1)}, bf16[2,96,256]{2,1,0:T(8,128)(2,1)S(1)}, u32[]{:S(2)}, u32[]{:S(2)}) collective-permute-start(bf16[2,96,256]{2,1,0:T(8,128)(2,1)S(1)} %get-tuple-element.27), channel_id=1, source_target_pairs={{0,0},{1,2},{2,1},{3,3},{4,4},{5,6},{6,5},{7,7},{8,8},{9,10},{10,9... | collective-permute-start | bytes 294920 | tf_op jit(solution)/shard_map/ppermute | solution.py:349
  11.6 0.1 reshape.38
  11.7 0.9 %collective-permute-done.4.exa_ref = f32[20,256]{1,0:T(8,128)S(1)} collective-permute-done((f32[20,256]{1,0:T(8,128)S(1)}, f32[20,256]{1,0:T(8,128)S(1)}, u32[]{:S(2)}, u32[]{:S(2)}) %collective-permute-start.4) | collective-permute-done | bytes 20512 | tf_op jit(solution)/shard_map/ppermute | solution.py:338
  12.6 1.0 %forward.1 = (f32[32,256]{1,0:T(8,128)S(1)}, f32[6,48,256]{2,1,0:T(8,128)S(1)}, bf16[7,64,256]{2,1,0:T(8,128)(2,1)S(1)}, bf16[7,64,256]{2,1,0:T(8,128)(2,1)S(1)}, f32[8,256]{1,0:T(8,128)S(1)}) custom-call(bf16[4,96,256]{2,1,0:T(8,128)(2,1)S(1)} %pad_maximum_fusion.mid_ref, bf16[2,96,256]{2,1,0:T(8,128)(2,1)S(1)} %collective-permute-done.2.da_ref, ...), custom_call_target="tpu_custom_call" | custom-call | tf_op jit(solution)/shard_map/forward/pallas_call | solution.py:60
  13.7 4.7 %collective-permute-start.6 = (f32[32,256]{1,0:T(8,128)S(1)}, f32[32,256]{1,0:T(8,128)S(1)}, u32[]{:S(2)}, u32[]{:S(2)}) collective-permute-start(f32[32,256]{1,0:T(8,128)S(1)} %get-tuple-element.16.refs_0_), channel_id=1, source_target_pairs={{0,1},{1,0},{2,3},{3,2},{4,5},{5,4},{6,7},{7,6},{8,9},{9,8},{10,11... | collective-permute-start | bytes 98312 | tf_op jit(solution)/shard_map/ppermute | solution.py:25
  18.4 1.1 %collective-permute-start.7 = (f32[32,256]{1,0:T(8,128)S(1)}, f32[32,256]{1,0:T(8,128)S(1)}, u32[]{:S(2)}, u32[]{:S(2)}) collective-permute-start(f32[32,256]{1,0:T(8,128)S(1)} %get-tuple-element.16.refs_0_), channel_id=1, source_target_pairs={{0,2},{1,3},{2,0},{3,1},{4,6},{5,7},{6,4},{7,5},{8,10},{9,11},{10,... | collective-permute-start | bytes 98312 | tf_op jit(solution)/shard_map/ppermute | solution.py:25
  19.5 0.3 collective-permute-start.8
  19.8 2.5 %collective-permute-done.7.refs_2_ = f32[32,256]{1,0:T(8,128)S(1)} collective-permute-done((f32[32,256]{1,0:T(8,128)S(1)}, f32[32,256]{1,0:T(8,128)S(1)}, u32[]{:S(2)}, u32[]{:S(2)}) %collective-permute-start.7) | collective-permute-done | bytes 32800 | tf_op jit(solution)/shard_map/ppermute | solution.py:25
  22.3 0.5 %collective-permute-done.8.refs_3_ = f32[32,256]{1,0:T(8,128)S(1)} collective-permute-done((f32[32,256]{1,0:T(8,128)S(1)}, f32[32,256]{1,0:T(8,128)S(1)}, u32[]{:S(2)}, u32[]{:S(2)}) %collective-permute-start.8) | collective-permute-done | bytes 32800 | tf_op jit(solution)/shard_map/ppermute | solution.py:25
  22.8 1.6 %backward.1 = (f32[32,128]{1,0:T(8,128)S(1)}, bf16[6,48,256]{2,1,0:T(8,128)(2,1)S(1)}, f32[4,256]{1,0:T(4,128)}) custom-call(f32[32,256]{1,0:T(8,128)S(1)} %get-tuple-element.16.refs_0_, f32[32,256]{1,0:T(8,128)S(1)} %collective-permute-done.6.refs_1_, f32[32,256]{1,0:T(8,128)S(1)} %collective-permute-done.7.refs_2_, ...), custom_call_target="tpu_custom_call" | custom-call | tf_op jit(solution)/shard_map/backward/pallas_call | solution.py:60
  24.4 1.2 %collective-permute-start.10 = (f32[32,128]{1,0:T(8,128)S(1)}, f32[32,128]{1,0:T(8,128)S(1)}, u32[]{:S(2)}, u32[]{:S(2)}) collective-permute-start(f32[32,128]{1,0:T(8,128)S(1)} %get-tuple-element.22), channel_id=1, source_target_pairs={{0,2},{1,3},{2,0},{3,1},{4,6},{5,7},{6,4},{7,5},{8,10},{9,11},{10,... | collective-permute-start | bytes 49160 | tf_op jit(solution)/shard_map/ppermute | solution.py:405
  25.6 0.3 collective-permute-start.11
  25.9 0.6 %collective-permute-start.9 = (f32[32,128]{1,0:T(8,128)S(1)}, f32[32,128]{1,0:T(8,128)S(1)}, u32[]{:S(2)}, u32[]{:S(2)}) collective-permute-start(f32[32,128]{1,0:T(8,128)S(1)} %get-tuple-element.22), channel_id=1, source_target_pairs={{0,1},{1,0},{2,3},{3,2},{4,5},{5,4},{6,7},{7,6},{8,9},{9,8},{10,11... | collective-permute-start | bytes 49160 | tf_op jit(solution)/shard_map/ppermute | solution.py:405
  26.6 0.1 copy.24
  26.7 0.1 reshape.37
  26.9 1.3 %collective-permute-done.10 = f32[32,128]{1,0:T(8,128)S(1)} collective-permute-done((f32[32,128]{1,0:T(8,128)S(1)}, f32[32,128]{1,0:T(8,128)S(1)}, u32[]{:S(2)}, u32[]{:S(2)}) %collective-permute-start.10) | collective-permute-done | bytes 16416 | tf_op jit(solution)/shard_map/ppermute | solution.py:405
  28.2 0.8 %collective-permute-done.11 = f32[32,128]{1,0:T(8,128)S(1)} collective-permute-done((f32[32,128]{1,0:T(8,128)S(1)}, f32[32,128]{1,0:T(8,128)S(1)}, u32[]{:S(2)}, u32[]{:S(2)}) %collective-permute-start.11) | collective-permute-done | bytes 16416 | tf_op jit(solution)/shard_map/ppermute | solution.py:405
  29.0 3.8 %collective-permute-start.12 = (f32[32,128]{1,0:T(8,128)S(1)}, f32[32,128]{1,0:T(8,128)S(1)}, u32[]{:S(2)}, u32[]{:S(2)}) collective-permute-start(f32[32,128]{1,0:T(8,128)S(1)} %add_add_fusion.refs_0_), channel_id=1, source_target_pairs={{0,4},{4,0},{8,12},{12,8},{1,5},{5,1},{9,13},{13,9},{2,6},{6,2},{1... | collective-permute-start | bytes 49160 | tf_op jit(solution)/shard_map/ppermute | solution.py:405
  32.7 1.1 %collective-permute-start.13 = (f32[32,128]{1,0:T(8,128)S(1)}, f32[32,128]{1,0:T(8,128)S(1)}, u32[]{:S(2)}, u32[]{:S(2)}) collective-permute-start(f32[32,128]{1,0:T(8,128)S(1)} %add_add_fusion.refs_0_), channel_id=1, source_target_pairs={{0,8},{4,12},{8,0},{12,4},{1,9},{5,13},{9,1},{13,5},{2,10},{6,14},... | collective-permute-start | bytes 49160 | tf_op jit(solution)/shard_map/ppermute | solution.py:405
  33.8 1.4 %collective-permute-start.14 = (f32[32,128]{1,0:T(8,128)S(1)}, f32[32,128]{1,0:T(8,128)S(1)}, u32[]{:S(2)}, u32[]{:S(2)}) collective-permute-start(f32[32,128]{1,0:T(8,128)S(1)} %add_add_fusion.refs_0_), channel_id=1, source_target_pairs={{0,12},{4,8},{8,4},{12,0},{1,13},{5,9},{9,5},{13,1},{2,14},{6,10},... | collective-permute-start | bytes 49160 | tf_op jit(solution)/shard_map/ppermute | solution.py:405
  35.2 1.1 %volume_grad.1 = bf16[8,4,4,256]{3,2,1,0:T(4,128)(2,1)} custom-call(bf16[6,48,256]{2,1,0:T(8,128)(2,1)S(1)} %get-tuple-element.21.pg_ref, f32[24,256]{1,0:T(8,128)S(1)} %pad_convert_fusion.1.base4_ref), custom_call_target="tpu_custom_call" | custom-call | tf_op jit(solution)/shard_map/volume_grad/pallas_call | solution.py:60
  36.3 1.1 %collective-permute-done.13.refs_2_ = f32[32,128]{1,0:T(8,128)S(1)} collective-permute-done((f32[32,128]{1,0:T(8,128)S(1)}, f32[32,128]{1,0:T(8,128)S(1)}, u32[]{:S(2)}, u32[]{:S(2)}) %collective-permute-start.13) | collective-permute-done | bytes 16416 | tf_op jit(solution)/shard_map/ppermute | solution.py:405
  37.4 2.0 %collective-permute-done.14.refs_3_ = f32[32,128]{1,0:T(8,128)S(1)} collective-permute-done((f32[32,128]{1,0:T(8,128)S(1)}, f32[32,128]{1,0:T(8,128)S(1)}, u32[]{:S(2)}, u32[]{:S(2)}) %collective-permute-start.14) | collective-permute-done | bytes 16416 | tf_op jit(solution)/shard_map/ppermute | solution.py:405
  39.3 0.8 %finish.1 = (f32[3,3,3,8,8]{4,3,2,1,0:T(8,128)}, f32[1,8]{1,0:T(1,128)}, f32[3,3,3,8]{3,2,1,0:T(4,128)}) custom-call(f32[32,128]{1,0:T(8,128)S(1)} %add_add_fusion.refs_0_, f32[32,128]{1,0:T(8,128)S(1)} %collective-permute-done.12.refs_1_, f32[32,128]{1,0:T(8,128)S(1)} %collective-permute-done.13.refs_2_, f32[32,128]{1,0:T(8,128)S(1)} %collective-permute-done.14.refs_3_), custom_call_target="tpu_custom_call" | custom-call | tf_op jit(solution)/shard_map/finish/pallas_call | solution.py:60
  (38 shorter events, 0.5 us)
Async XLA Ops:
  0.6 7.5 %copy-start.3 = (f32[4,4,256]{2,1,0:T(4,128)S(1)}, f32[4,4,256]{2,1,0:T(4,128)}, u32[]{:S(2)}) copy-start(f32[4,4,256]{2,1,0:T(4,128)} %param.10) | copy-start | bytes 49156
  1.5 9.2 %collective-permute-start = (bf16[4,32,256]{2,1,0:T(8,128)(2,1)S(1)}, bf16[4,32,256]{2,1,0:T(8,128)(2,1)S(1)}, u32[]{:S(2)}, u32[]{:S(2)}) collective-permute-start(bf16[4,32,256]{2,1,0:T(8,128)(2,1)S(1)} %bitcast.15), channel_id=1, source_target_pairs={{0,0},{4,8},{8,4},{12,12},{1,1},{5,9},{9,5},{13,13},{2,2},{6,10},{... | collective-permute-start | bytes 196616 | tf_op jit(solution)/shard_map/ppermute | solution.py:336
  2.2 8.5 %collective-permute-start.1 = (bf16[4,32,256]{2,1,0:T(8,128)(2,1)S(1)}, bf16[4,32,256]{2,1,0:T(8,128)(2,1)S(1)}, u32[]{:S(2)}, u32[]{:S(2)}) collective-permute-start(bf16[4,32,256]{2,1,0:T(8,128)(2,1)S(1)} %bitcast.16), channel_id=1, source_target_pairs={{0,4},{4,0},{8,12},{12,8},{1,5},{5,1},{9,13},{13,9},{2,6},{6,2},{1... | collective-permute-start | bytes 196616 | tf_op jit(solution)/shard_map/ppermute | solution.py:335
  8.1 0.7 %copy-start.4 = (f32[4,256]{1,0:T(4,128)S(1)}, f32[4,256]{1,0:T(4,128)}, u32[]{:S(2)}) copy-start(f32[4,256]{1,0:T(4,128)} %param.11) | copy-start | bytes 12292
  8.1 1.4 %copy-start.1 = (bf16[3,3,3,8,8]{4,3,2,1,0:T(8,128)(2,1)S(1)}, bf16[3,3,3,8,8]{4,3,2,1,0:T(8,128)(2,1)}, u32[]{:S(2)}) copy-start(bf16[3,3,3,8,8]{4,3,2,1,0:T(8,128)(2,1)} %param.7) | copy-start | bytes 10372
  8.8 3.8 %collective-permute-start.4 = (f32[20,256]{1,0:T(8,128)S(1)}, f32[20,256]{1,0:T(8,128)S(1)}, u32[]{:S(2)}, u32[]{:S(2)}) collective-permute-start(f32[20,256]{1,0:T(8,128)S(1)} %constant_dynamic-update-slice_fusion.ex_ref), channel_id=1, source_target_pairs={{0,4},{4,0},{8,12},{12,8},{1,5},{5,1},{9,13},{13,9},{2,6},{6,2},{1... | collective-permute-start | bytes 61448 | tf_op jit(solution)/shard_map/ppermute | solution.py:338
  8.8 3.8 %collective-permute-start.5 = (f32[20,256]{1,0:T(8,128)S(1)}, f32[20,256]{1,0:T(8,128)S(1)}, u32[]{:S(2)}, u32[]{:S(2)}) collective-permute-start(f32[20,256]{1,0:T(8,128)S(1)} %constant_dynamic-update-slice_fusion.ex_ref), channel_id=1, source_target_pairs={{0,0},{4,8},{8,4},{12,12},{1,1},{5,9},{9,5},{13,13},{2,2},{6,10},{... | collective-permute-start | bytes 61448 | tf_op jit(solution)/shard_map/ppermute | solution.py:339
  9.8 0.7 %copy-start.2 = (bf16[3,3,3,8]{3,2,1,0:T(4,128)(2,1)S(1)}, bf16[3,3,3,8]{3,2,1,0:T(4,128)(2,1)}, u32[]{:S(2)}) copy-start(bf16[3,3,3,8]{3,2,1,0:T(4,128)(2,1)} %param.9) | copy-start | bytes 1300
  10.8 1.8 %collective-permute-start.2 = (bf16[2,96,256]{2,1,0:T(8,128)(2,1)S(1)}, bf16[2,96,256]{2,1,0:T(8,128)(2,1)S(1)}, u32[]{:S(2)}, u32[]{:S(2)}) collective-permute-start(bf16[2,96,256]{2,1,0:T(8,128)(2,1)S(1)} %get-tuple-element.28), channel_id=1, source_target_pairs={{0,1},{1,0},{2,3},{3,2},{4,5},{5,4},{6,7},{7,6},{8,9},{9,8},{10,11... | collective-permute-start | bytes 294920 | tf_op jit(solution)/shard_map/ppermute | solution.py:346
  10.9 1.8 %collective-permute-start.3 = (bf16[2,96,256]{2,1,0:T(8,128)(2,1)S(1)}, bf16[2,96,256]{2,1,0:T(8,128)(2,1)S(1)}, u32[]{:S(2)}, u32[]{:S(2)}) collective-permute-start(bf16[2,96,256]{2,1,0:T(8,128)(2,1)S(1)} %get-tuple-element.27), channel_id=1, source_target_pairs={{0,0},{1,2},{2,1},{3,3},{4,4},{5,6},{6,5},{7,7},{8,8},{9,10},{10,9... | collective-permute-start | bytes 294920 | tf_op jit(solution)/shard_map/ppermute | solution.py:349
  11.7 0.9 %copy-start = (f32[8]{0:T(128)S(1)}, f32[8]{0:T(128)}, u32[]{:S(2)}) copy-start(f32[8]{0:T(128)} %param.8) | copy-start | bytes 100
  13.7 6.1 %collective-permute-start.6 = (f32[32,256]{1,0:T(8,128)S(1)}, f32[32,256]{1,0:T(8,128)S(1)}, u32[]{:S(2)}, u32[]{:S(2)}) collective-permute-start(f32[32,256]{1,0:T(8,128)S(1)} %get-tuple-element.16.refs_0_), channel_id=1, source_target_pairs={{0,1},{1,0},{2,3},{3,2},{4,5},{5,4},{6,7},{7,6},{8,9},{9,8},{10,11... | collective-permute-start | bytes 98312 | tf_op jit(solution)/shard_map/ppermute | solution.py:25
  18.4 3.9 %collective-permute-start.7 = (f32[32,256]{1,0:T(8,128)S(1)}, f32[32,256]{1,0:T(8,128)S(1)}, u32[]{:S(2)}, u32[]{:S(2)}) collective-permute-start(f32[32,256]{1,0:T(8,128)S(1)} %get-tuple-element.16.refs_0_), channel_id=1, source_target_pairs={{0,2},{1,3},{2,0},{3,1},{4,6},{5,7},{6,4},{7,5},{8,10},{9,11},{10,... | collective-permute-start | bytes 98312 | tf_op jit(solution)/shard_map/ppermute | solution.py:25
  19.5 3.3 %collective-permute-start.8 = (f32[32,256]{1,0:T(8,128)S(1)}, f32[32,256]{1,0:T(8,128)S(1)}, u32[]{:S(2)}, u32[]{:S(2)}) collective-permute-start(f32[32,256]{1,0:T(8,128)S(1)} %get-tuple-element.16.refs_0_), channel_id=1, source_target_pairs={{0,3},{1,2},{2,1},{3,0},{4,7},{5,6},{6,5},{7,4},{8,11},{9,10},{10,... | collective-permute-start | bytes 98312 | tf_op jit(solution)/shard_map/ppermute | solution.py:25
  24.4 3.7 %collective-permute-start.10 = (f32[32,128]{1,0:T(8,128)S(1)}, f32[32,128]{1,0:T(8,128)S(1)}, u32[]{:S(2)}, u32[]{:S(2)}) collective-permute-start(f32[32,128]{1,0:T(8,128)S(1)} %get-tuple-element.22), channel_id=1, source_target_pairs={{0,2},{1,3},{2,0},{3,1},{4,6},{5,7},{6,4},{7,5},{8,10},{9,11},{10,... | collective-permute-start | bytes 49160 | tf_op jit(solution)/shard_map/ppermute | solution.py:405
  25.6 3.3 %collective-permute-start.11 = (f32[32,128]{1,0:T(8,128)S(1)}, f32[32,128]{1,0:T(8,128)S(1)}, u32[]{:S(2)}, u32[]{:S(2)}) collective-permute-start(f32[32,128]{1,0:T(8,128)S(1)} %get-tuple-element.22), channel_id=1, source_target_pairs={{0,3},{1,2},{2,1},{3,0},{4,7},{5,6},{6,5},{7,4},{8,11},{9,10},{10,... | collective-permute-start | bytes 49160 | tf_op jit(solution)/shard_map/ppermute | solution.py:405
  25.9 3.0 %collective-permute-start.9 = (f32[32,128]{1,0:T(8,128)S(1)}, f32[32,128]{1,0:T(8,128)S(1)}, u32[]{:S(2)}, u32[]{:S(2)}) collective-permute-start(f32[32,128]{1,0:T(8,128)S(1)} %get-tuple-element.22), channel_id=1, source_target_pairs={{0,1},{1,0},{2,3},{3,2},{4,5},{5,4},{6,7},{7,6},{8,9},{9,8},{10,11... | collective-permute-start | bytes 49160 | tf_op jit(solution)/shard_map/ppermute | solution.py:405
  29.0 7.4 %collective-permute-start.12 = (f32[32,128]{1,0:T(8,128)S(1)}, f32[32,128]{1,0:T(8,128)S(1)}, u32[]{:S(2)}, u32[]{:S(2)}) collective-permute-start(f32[32,128]{1,0:T(8,128)S(1)} %add_add_fusion.refs_0_), channel_id=1, source_target_pairs={{0,4},{4,0},{8,12},{12,8},{1,5},{5,1},{9,13},{13,9},{2,6},{6,2},{1... | collective-permute-start | bytes 49160 | tf_op jit(solution)/shard_map/ppermute | solution.py:405
  32.7 4.7 %collective-permute-start.13 = (f32[32,128]{1,0:T(8,128)S(1)}, f32[32,128]{1,0:T(8,128)S(1)}, u32[]{:S(2)}, u32[]{:S(2)}) collective-permute-start(f32[32,128]{1,0:T(8,128)S(1)} %add_add_fusion.refs_0_), channel_id=1, source_target_pairs={{0,8},{4,12},{8,0},{12,4},{1,9},{5,13},{9,1},{13,5},{2,10},{6,14},... | collective-permute-start | bytes 49160 | tf_op jit(solution)/shard_map/ppermute | solution.py:405
  33.8 5.5 %collective-permute-start.14 = (f32[32,128]{1,0:T(8,128)S(1)}, f32[32,128]{1,0:T(8,128)S(1)}, u32[]{:S(2)}, u32[]{:S(2)}) collective-permute-start(f32[32,128]{1,0:T(8,128)S(1)} %add_add_fusion.refs_0_), channel_id=1, source_target_pairs={{0,12},{4,8},{8,4},{12,0},{1,13},{5,9},{9,5},{13,1},{2,14},{6,10},... | collective-permute-start | bytes 49160 | tf_op jit(solution)/shard_map/ppermute | solution.py:405

commit v3 on v2

--- a/solution.py
+++ b/solution.py
@@ -78,8 +78,34 @@
     return lax.dot_general(a, b, (((1,), (1,)), ((), ())), preferred_element_type=F32)
 
 
+def pack_body(dims, own_ref, prior_ref, cot_ref, one_ref, two_ref, wide_ref):
+    planes, rows, chans, width, disp, space = dims
+    even = lax.axis_index("space") % 2 == 0
+    n = planes * rows * chans
+    k = 2 * (planes + 1)
+    own = own_ref[...].reshape(n, width)
+    wide_ref[...] = jnp.zeros(wide_ref.shape, F32)
+    for out_ref in (one_ref, two_ref):
+        out_ref[:n] = own
+
+        def put(at):
+            for p in range(planes):
+                wide_ref[2 * p : 2 * p + 2] = prior_ref[p, at : at + 2]
+            wide_ref[2 * planes : k] = cot_ref[at : at + 2]
+
+        goes_down = even if out_ref is one_ref else jnp.logical_not(even)
+        pl.when(goes_down)(functools.partial(put, rows - 2))
+        pl.when(jnp.logical_not(goes_down))(functools.partial(put, 0))
+        rest = wide_ref[:k]
+        for t in range(3):
+            term = rest.astype(BF16).astype(F32)
+            wide_ref[t * k : (t + 1) * k] = term
+            rest = rest - term
+        out_ref[n:] = wide_ref[...].astype(BF16)
+
+
 def forward_body(
-    dims, mid_ref, da_ref, db_ref, ex_ref, exa_ref, exb_ref, base1_ref, bias_ref, base2_ref,
+    dims, mid_ref, db_ref, da_ref, prior_in_ref, cot_in_ref, za_ref, zb_ref, base1_ref, bias_ref, base2_ref,
     logits_ref, slope_ref, hid_ref, xs_ref, cot_ref, x_ref, h_ref, prior_ref
 ):
     planes, rows, chans, width, disp, space = dims
@@ -109,24 +135,28 @@
     place(0, 2 * xr, di > 0, d_even, db_ref, da_ref)
     place((planes + 2) * xr, 2 * xr, di < disp - 1, d_even, da_ref, db_ref)
 
-    zero2 = jnp.zeros((2, width), F32)
-
-    def extras(ok, first, one, two, row, at):
+    n = planes * rows * chans
+    k = 2 * (planes + 1)
+
+    def extras(ok, first, one, two, at):
         def put(src):
+            wide = None if src is None else src[n:, :].astype(F32)
+            total = jnp.zeros((k, width), F32)
+            if wide is not None:
+                total = wide[:k] + wide[k : 2 * k] + wide[2 * k : 3 * k]
             for p in range(planes):
-                prior_ref[p, at : at + 2, :] = zero2 if src is None else src[p * rows + row : p * rows + row + 2, :]
-            base = planes * rows + row
-            cot_ref[at : at + 2, :] = zero2 if src is None else src[base : base + 2, :]
+                prior_ref[p, at : at + 2, :] = total[2 * p : 2 * p + 2]
+            cot_ref[at : at + 2, :] = total[2 * planes : k]
 
         pl.when(ok & first)(lambda: put(one))
         pl.when(ok & jnp.logical_not(first))(lambda: put(two))
         pl.when(jnp.logical_not(ok))(lambda: put(None))
 
     for p in range(planes):
-        prior_ref[p, 2 : 2 + rows, :] = ex_ref[p * rows : (p + 1) * rows, :]
-    cot_ref[2 : 2 + rows, :] = ex_ref[planes * rows : (planes + 1) * rows, :]
-    extras(zi > 0, z_even, exb_ref, exa_ref, rows - 2, 0)
-    extras(zi < space - 1, z_even, exa_ref, exb_ref, 0, rows + 2)
+        prior_ref[p, 2 : 2 + rows, :] = prior_in_ref[p]
+    cot_ref[2 : 2 + rows, :] = cot_in_ref[...]
+    extras(zi > 0, z_even, zb_ref, za_ref, 0)
+    extras(zi < space - 1, z_even, za_ref, zb_ref, rows + 2)
 
     bands = []
     base1 = base1_ref[...]
@@ -186,7 +216,7 @@
     l_ref[0] = jnp.zeros(l_ref.shape[1:], F32)
     l_ref[disp + 1] = jnp.zeros(l_ref.shape[1:], F32)
     for s in range(disp):
-        l_ref[(di ^ s) + 1] = logit_refs[s][...]
+        l_ref[(di ^ s) + 1] = logit_refs[-s % disp][...]
 
     def logit(g, p):
         return l_ref[g, p * lr : (p + 1) * lr, :]
@@ -332,15 +362,23 @@
     di = lax.axis_index("disp")
 
     own = jnp.transpose(volume, (1, 2, 0, 3)).reshape(planes, rows * chans, width)
-    z_one = lax.ppermute(own, "space", swap_pairs(space, 0))
-    z_two = lax.ppermute(own, "space", swap_pairs(space, 1))
-    extra = jnp.concatenate([prior_logits.reshape(planes * rows, width), cotangent], axis=0)
-    e_one = lax.ppermute(extra, "space", swap_pairs(space, 0))
-    e_two = lax.ppermute(extra, "space", swap_pairs(space, 1))
+    n = planes * rows * chans
+    extra = -(-6 * (planes + 1) // 16) * 16
+    send_one, send_two = call(
+        functools.partial(pack_body, dims),
+        "pack",
+        (((n + extra, width), BF16, True), ((n + extra, width), BF16, True)),
+        own, prior_logits, cotangent,
+        scratch=[pltpu.VMEM((extra, width), F32)],
+    )
+    z_one = lax.ppermute(send_one, "space", swap_pairs(space, 0))
+    z_two = lax.ppermute(send_two, "space", swap_pairs(space, 1))
     z_even = zi % 2 == 0
     zero = jnp.zeros((), BF16)
-    above = jnp.where(zi > 0, jnp.where(z_even, z_two, z_one), zero)
-    below = jnp.where(zi < space - 1, jnp.where(z_even, z_one, z_two), zero)
+    block_one = z_one[:n].reshape(own.shape)
+    block_two = z_two[:n].reshape(own.shape)
+    above = jnp.where(zi > 0, jnp.where(z_even, block_two, block_one), zero)
+    below = jnp.where(zi < space - 1, jnp.where(z_even, block_one, block_two), zero)
     mid = jnp.concatenate([above, own, below], axis=1)
     even = (di % 2 == 0).astype(jnp.int32)
     d_one = lax.ppermute(
@@ -378,7 +416,7 @@
             ((planes + 3, (rows + 4) * chans, width), BF16, True),
             ((lr, width), F32, True),
         ),
-        mid, d_one, d_two, extra, e_one, e_two, base1, b_first[None, :], base2,
+        mid, d_two, d_one, prior_logits, cotangent, z_one, z_two, base1, b_first[None, :], base2,
         scratch=[
             pltpu.VMEM(((planes + 4) * xr * chans, width), BF16),
             pltpu.VMEM(((planes + 2) * hr * chans, width), BF16),
@@ -386,7 +424,7 @@
         ],
     )
 
-    pieces = [logits] + partners(logits, "disp")
+    pieces = [logits] + partners(logits, "disp")[::-1]
     pay, pg, disparity = call(
         functools.partial(backward_body, dims),
         "backward",

time: 40.4 us -> 36.9 us (0.913)
  starting transfers between devices: 22.5 us -> 19.9 us
  local copies, waits for them, and re-layouts: 3.18 us -> 2.31 us
    ppermute x3, starting transfers between devices: 6.13 us -> 3.09 us  [partners(): lax.ppermute(value, axis, [(i, i ^ s) for i in range(count)])]
    ppermute x1, starting transfers between devices: 0.07 us -> 2.91 us  [shards(): lax.ppermute(lax.dynamic_slice_in_dim(mid, (planes - 2) * even, 2, axis=0...]
    ppermute x6, starting transfers between devices: 8.38 us -> 6.51 us  [shards(): lax.ppermute(pay, axis, [(i, i ^ s) for i in range(count)])]
    ppermute x1, waiting for transfers between devices: 0.01 us -> 0.93 us  [shards(): lax.ppermute(lax.dynamic_slice_in_dim(mid, (planes - 2) * even, 2, axis=0...]
    ppermute x3, waiting for transfers between devices: 2.99 us -> 2.13 us  [partners(): lax.ppermute(value, axis, [(i, i ^ s) for i in range(count)])]
    unnamed x14 -> x13, local copies, waits for them, and re-layouts: 1.5 us -> 0.63 us
    ppermute x4 -> x2, starting transfers between devices: 7.25 us -> 6.71 us  [the longest x1 5.91 us: shards(): z_one = lax.ppermute(send_one, 'space', swap_pairs(space, 0))]
    ppermute x6, waiting for transfers between devices: 5.1 us -> 4.65 us  [shards(): lax.ppermute(pay, axis, [(i, i ^ s) for i in range(count)])]
  transfers between devices with their start and end apart: 15 -> 13, of which waited for: 7 -> 8; matrix products, arithmetic and copies ran while one was open for 3% -> 3% of each run, Pallas kernels for 3% -> 3%
where the time goes in v3:
time: 36.9 us; the launch traced here: 36.6 us
  starting transfers between devices  19.9 us (54%)
  waiting for transfers between devices  8.97 us (24%)
  Pallas kernels  4.58 us (12%)
  local copies, waits for them, and re-layouts  2.31 us (6%)
  between operations  0.81 us (2%)
    ppermute x6, starting transfers between devices, shards(): lax.ppermute(pay, axis, [(i, i ^ s) for i in range(count)])  6.51 us
    ppermute x1, starting transfers between devices, shards(): z_one = lax.ppermute(send_one, 'space', swap_pairs(space, 0))  5.91 us
    ppermute x6, waiting for transfers between devices, shards(): lax.ppermute(pay, axis, [(i, i ^ s) for i in range(count)])  4.65 us
    pallas_call x5, Pallas kernels, call(): pl.pallas_call(body, out_shape=tuple((pltpu.VMEM(shape, dtype) if inside...  4.58 us
    ppermute x3, starting transfers between devices, partners(): lax.ppermute(value, axis, [(i, i ^ s) for i in range(count)])  3.09 us
    ppermute x1, starting transfers between devices, shards(): lax.ppermute(lax.dynamic_slice_in_dim(mid, (planes - 2) * even, 2, axis=0...  2.91 us
    ppermute x3, waiting for transfers between devices, partners(): lax.ppermute(value, axis, [(i, i ^ s) for i in range(count)])  2.13 us
    ppermute x1, waiting for transfers between devices, shards(): z_one = lax.ppermute(send_one, 'space', swap_pairs(space, 0))  1.26 us
  transfers between devices with their start and end apart: 13, of which 8 were waited for; matrix products, arithmetic and copies ran while one was open for 3% of the time, Pallas kernels for 3%

profile of v3, /device:TPU:0, one launch (start us, length us, event | category | flops | bytes accessed | tf_op | source)
XLA Modules:
  0.0 36.6 jit_solution(12005024881773265796)
XLA Ops:
  0.7 0.9 %copy.26 = bf16[4,4,8,256]{3,2,1,0:T(8,128)(2,1)S(1)} copy(bf16[4,4,8,256]{3,1,0,2:T(4,128)(2,1)} %bitcast.22) | data formatting | bytes 131072 | tf_op jit(solution)/shard_map/transpose | solution.py:364
  1.5 0.1 pack.1
  1.6 0.8 %collective-permute-start = (bf16[160,256]{1,0:T(8,128)(2,1)S(1)}, bf16[160,256]{1,0:T(8,128)(2,1)S(1)}, u32[]{:S(2)}, u32[]{:S(2)}) collective-permute-start(bf16[160,256]{1,0:T(8,128)(2,1)S(1)} %get-tuple-element.18), channel_id=1, source_target_pairs={{0,0},{4,8},{8,4},{12,12},{1,1},{5,9},{9,5},{13,13},{2,2},{6,10},{... | collective-permute-start | bytes 245768 | tf_op jit(solution)/shard_map/ppermute | solution.py:375
  2.4 5.9 %collective-permute-start.1 = (bf16[160,256]{1,0:T(8,128)(2,1)S(1)}, bf16[160,256]{1,0:T(8,128)(2,1)S(1)}, u32[]{:S(2)}, u32[]{:S(2)}) collective-permute-start(bf16[160,256]{1,0:T(8,128)(2,1)S(1)} %get-tuple-element.19), channel_id=1, source_target_pairs={{0,4},{4,0},{8,12},{12,8},{1,5},{5,1},{9,13},{13,9},{2,6},{6,2},{1... | collective-permute-start | bytes 245768 | tf_op jit(solution)/shard_map/ppermute | solution.py:374
  8.5 0.2 reshape.42
  8.7 0.5 %copy-done.4 = bf16[3,3,3,8]{3,2,1,0:T(4,128)(2,1)S(1)} copy-done((bf16[3,3,3,8]{3,2,1,0:T(4,128)(2,1)S(1)}, bf16[3,3,3,8]{3,2,1,0:T(4,128)(2,1)}, u32[]{:S(2)}) %copy-start.4) | copy-done | bytes 456
  9.2 0.1 reshape.43
  9.3 0.1 reshape.46
  9.4 0.1 copy.21
  9.5 1.3 %collective-permute-done.1.za_ref = bf16[160,256]{1,0:T(8,128)(2,1)S(1)} collective-permute-done((bf16[160,256]{1,0:T(8,128)(2,1)S(1)}, bf16[160,256]{1,0:T(8,128)(2,1)S(1)}, u32[]{:S(2)}, u32[]{:S(2)}) %collective-permute-start.1) | collective-permute-done | bytes 81952 | tf_op jit(solution)/shard_map/ppermute | solution.py:374
  10.8 0.7 %collective-permute-start.2 = (bf16[2,96,256]{2,1,0:T(8,128)(2,1)S(1)}, bf16[2,96,256]{2,1,0:T(8,128)(2,1)S(1)}, u32[]{:S(2)}, u32[]{:S(2)}) collective-permute-start(bf16[2,96,256]{2,1,0:T(8,128)(2,1)S(1)} %get-tuple-element.32), channel_id=1, source_target_pairs={{0,0},{1,2},{2,1},{3,3},{4,4},{5,6},{6,5},{7,7},{8,8},{9,10},{10,9... | collective-permute-start | bytes 294920 | tf_op jit(solution)/shard_map/ppermute | solution.py:387
  11.5 2.9 %collective-permute-start.3 = (bf16[2,96,256]{2,1,0:T(8,128)(2,1)S(1)}, bf16[2,96,256]{2,1,0:T(8,128)(2,1)S(1)}, u32[]{:S(2)}, u32[]{:S(2)}) collective-permute-start(bf16[2,96,256]{2,1,0:T(8,128)(2,1)S(1)} %get-tuple-element.31), channel_id=1, source_target_pairs={{0,1},{1,0},{2,3},{3,2},{4,5},{5,4},{6,7},{7,6},{8,9},{9,8},{10,11... | collective-permute-start | bytes 294920 | tf_op jit(solution)/shard_map/ppermute | solution.py:384
  14.5 0.9 %collective-permute-done.3.da_ref = bf16[2,96,256]{2,1,0:T(8,128)(2,1)S(1)} collective-permute-done((bf16[2,96,256]{2,1,0:T(8,128)(2,1)S(1)}, bf16[2,96,256]{2,1,0:T(8,128)(2,1)S(1)}, u32[]{:S(2)}, u32[]{:S(2)}) %collective-permute-start.3) | collective-permute-done | bytes 98336 | tf_op jit(solution)/shard_map/ppermute | solution.py:384
  15.4 1.0 %forward.1 = (f32[32,256]{1,0:T(8,128)S(1)}, f32[6,48,256]{2,1,0:T(8,128)S(1)}, bf16[7,64,256]{2,1,0:T(8,128)(2,1)S(1)}, bf16[7,64,256]{2,1,0:T(8,128)(2,1)S(1)}, f32[8,256]{1,0:T(8,128)S(1)}) custom-call(bf16[4,96,256]{2,1,0:T(8,128)(2,1)S(1)} %pad_maximum_fusion.mid_ref, bf16[2,96,256]{2,1,0:T(8,128)(2,1)S(1)} %collective-permute-done.2.db_ref, ...), custom_call_target="tpu_custom_call" | custom-call | tf_op jit(solution)/shard_map/forward/pallas_call | solution.py:60
  16.4 0.1 collective-permute-start.4
  16.5 3.0 %collective-permute-start.5 = (f32[32,256]{1,0:T(8,128)S(1)}, f32[32,256]{1,0:T(8,128)S(1)}, u32[]{:S(2)}, u32[]{:S(2)}) collective-permute-start(f32[32,256]{1,0:T(8,128)S(1)} %get-tuple-element.20.refs_0_), channel_id=1, source_target_pairs={{0,2},{1,3},{2,0},{3,1},{4,6},{5,7},{6,4},{7,5},{8,10},{9,11},{10,... | collective-permute-start | bytes 98312 | tf_op jit(solution)/shard_map/ppermute | solution.py:25
  19.5 0.3 collective-permute-done.4.refs_1_
  19.8 1.8 %collective-permute-done.5.refs_2_ = f32[32,256]{1,0:T(8,128)S(1)} collective-permute-done((f32[32,256]{1,0:T(8,128)S(1)}, f32[32,256]{1,0:T(8,128)S(1)}, u32[]{:S(2)}, u32[]{:S(2)}) %collective-permute-start.5) | collective-permute-done | bytes 32800 | tf_op jit(solution)/shard_map/ppermute | solution.py:25
  21.6 1.6 %backward.1 = (f32[32,128]{1,0:T(8,128)S(1)}, bf16[6,48,256]{2,1,0:T(8,128)(2,1)S(1)}, f32[4,256]{1,0:T(4,128)}) custom-call(f32[32,256]{1,0:T(8,128)S(1)} %get-tuple-element.20.refs_0_, f32[32,256]{1,0:T(8,128)S(1)} %collective-permute-done.4.refs_1_, f32[32,256]{1,0:T(8,128)S(1)} %collective-permute-done.5.refs_2_, ...), custom_call_target="tpu_custom_call" | custom-call | tf_op jit(solution)/shard_map/backward/pallas_call | solution.py:60
  23.3 0.6 %collective-permute-start.7 = (f32[32,128]{1,0:T(8,128)S(1)}, f32[32,128]{1,0:T(8,128)S(1)}, u32[]{:S(2)}, u32[]{:S(2)}) collective-permute-start(f32[32,128]{1,0:T(8,128)S(1)} %get-tuple-element.26), channel_id=1, source_target_pairs={{0,1},{1,0},{2,3},{3,2},{4,5},{5,4},{6,7},{7,6},{8,9},{9,8},{10,11... | collective-permute-start | bytes 49160 | tf_op jit(solution)/shard_map/ppermute | solution.py:443
  23.9 1.2 %collective-permute-start.8 = (f32[32,128]{1,0:T(8,128)S(1)}, f32[32,128]{1,0:T(8,128)S(1)}, u32[]{:S(2)}, u32[]{:S(2)}) collective-permute-start(f32[32,128]{1,0:T(8,128)S(1)} %get-tuple-element.26), channel_id=1, source_target_pairs={{0,2},{1,3},{2,0},{3,1},{4,6},{5,7},{6,4},{7,5},{8,10},{9,11},{10,... | collective-permute-start | bytes 49160 | tf_op jit(solution)/shard_map/ppermute | solution.py:443
  25.1 0.2 collective-permute-start.9
  25.2 0.1 copy.24
  25.4 0.1 reshape.45
  25.6 2.1 %collective-permute-done.8 = f32[32,128]{1,0:T(8,128)S(1)} collective-permute-done((f32[32,128]{1,0:T(8,128)S(1)}, f32[32,128]{1,0:T(8,128)S(1)}, u32[]{:S(2)}, u32[]{:S(2)}) %collective-permute-start.8) | collective-permute-done | bytes 16416 | tf_op jit(solution)/shard_map/ppermute | solution.py:443
  27.6 0.6 %collective-permute-done.9 = f32[32,128]{1,0:T(8,128)S(1)} collective-permute-done((f32[32,128]{1,0:T(8,128)S(1)}, f32[32,128]{1,0:T(8,128)S(1)}, u32[]{:S(2)}, u32[]{:S(2)}) %collective-permute-start.9) | collective-permute-done | bytes 16416 | tf_op jit(solution)/shard_map/ppermute | solution.py:443
  28.2 2.1 %collective-permute-start.10 = (f32[32,128]{1,0:T(8,128)S(1)}, f32[32,128]{1,0:T(8,128)S(1)}, u32[]{:S(2)}, u32[]{:S(2)}) collective-permute-start(f32[32,128]{1,0:T(8,128)S(1)} %add_add_fusion.refs_0_), channel_id=1, source_target_pairs={{0,4},{4,0},{8,12},{12,8},{1,5},{5,1},{9,13},{13,9},{2,6},{6,2},{1... | collective-permute-start | bytes 49160 | tf_op jit(solution)/shard_map/ppermute | solution.py:443
  30.3 2.4 %collective-permute-start.12 = (f32[32,128]{1,0:T(8,128)S(1)}, f32[32,128]{1,0:T(8,128)S(1)}, u32[]{:S(2)}, u32[]{:S(2)}) collective-permute-start(f32[32,128]{1,0:T(8,128)S(1)} %add_add_fusion.refs_0_), channel_id=1, source_target_pairs={{0,12},{4,8},{8,4},{12,0},{1,13},{5,9},{9,5},{13,1},{2,14},{6,10},... | collective-permute-start | bytes 49160 | tf_op jit(solution)/shard_map/ppermute | solution.py:443
  32.8 1.1 %volume_grad.1 = bf16[8,4,4,256]{3,2,1,0:T(4,128)(2,1)} custom-call(bf16[6,48,256]{2,1,0:T(8,128)(2,1)S(1)} %get-tuple-element.25.pg_ref, f32[24,256]{1,0:T(8,128)S(1)} %pad_convert_fusion.1.base4_ref), custom_call_target="tpu_custom_call" | custom-call | tf_op jit(solution)/shard_map/volume_grad/pallas_call | solution.py:60
  33.9 1.1 %collective-permute-done.11.refs_2_ = f32[32,128]{1,0:T(8,128)S(1)} collective-permute-done((f32[32,128]{1,0:T(8,128)S(1)}, f32[32,128]{1,0:T(8,128)S(1)}, u32[]{:S(2)}, u32[]{:S(2)}) %collective-permute-start.11) | collective-permute-done | bytes 16416 | tf_op jit(solution)/shard_map/ppermute | solution.py:443
  35.0 0.8 %collective-permute-done.12.refs_3_ = f32[32,128]{1,0:T(8,128)S(1)} collective-permute-done((f32[32,128]{1,0:T(8,128)S(1)}, f32[32,128]{1,0:T(8,128)S(1)}, u32[]{:S(2)}, u32[]{:S(2)}) %collective-permute-start.12) | collective-permute-done | bytes 16416 | tf_op jit(solution)/shard_map/ppermute | solution.py:443
  35.8 0.8 %finish.1 = (f32[3,3,3,8,8]{4,3,2,1,0:T(8,128)}, f32[1,8]{1,0:T(1,128)}, f32[3,3,3,8]{3,2,1,0:T(4,128)}) custom-call(f32[32,128]{1,0:T(8,128)S(1)} %add_add_fusion.refs_0_, f32[32,128]{1,0:T(8,128)S(1)} %collective-permute-done.10.refs_1_, f32[32,128]{1,0:T(8,128)S(1)} %collective-permute-done.11.refs_2_, f32[32,128]{1,0:T(8,128)S(1)} %collective-permute-done.12.refs_3_), custom_call_target="tpu_custom_call" | custom-call | tf_op jit(solution)/shard_map/finish/pallas_call | solution.py:60
  (32 shorter events, 0.3 us)
Async XLA Ops:
  0.6 0.9 %copy-start = (f32[4,4,256]{2,1,0:T(4,128)S(1)}, f32[4,4,256]{2,1,0:T(4,128)}, u32[]{:S(2)}) copy-start(f32[4,4,256]{2,1,0:T(4,128)} %prior_in_ref.1) | copy-start | bytes 49156
  0.6 0.9 %copy-start.1 = (f32[4,256]{1,0:T(4,128)S(1)}, f32[4,256]{1,0:T(4,128)}, u32[]{:S(2)}) copy-start(f32[4,256]{1,0:T(4,128)} %cot_in_ref.1) | copy-start | bytes 12292
  1.6 6.7 %copy-start.3 = (bf16[3,3,3,8,8]{4,3,2,1,0:T(8,128)(2,1)S(1)}, bf16[3,3,3,8,8]{4,3,2,1,0:T(8,128)(2,1)}, u32[]{:S(2)}) copy-start(bf16[3,3,3,8,8]{4,3,2,1,0:T(8,128)(2,1)} %param.7) | copy-start | bytes 10372
  1.6 7.9 %collective-permute-start = (bf16[160,256]{1,0:T(8,128)(2,1)S(1)}, bf16[160,256]{1,0:T(8,128)(2,1)S(1)}, u32[]{:S(2)}, u32[]{:S(2)}) collective-permute-start(bf16[160,256]{1,0:T(8,128)(2,1)S(1)} %get-tuple-element.18), channel_id=1, source_target_pairs={{0,0},{4,8},{8,4},{12,12},{1,1},{5,9},{9,5},{13,13},{2,2},{6,10},{... | collective-permute-start | bytes 245768 | tf_op jit(solution)/shard_map/ppermute | solution.py:375
  2.4 8.3 %collective-permute-start.1 = (bf16[160,256]{1,0:T(8,128)(2,1)S(1)}, bf16[160,256]{1,0:T(8,128)(2,1)S(1)}, u32[]{:S(2)}, u32[]{:S(2)}) collective-permute-start(bf16[160,256]{1,0:T(8,128)(2,1)S(1)} %get-tuple-element.19), channel_id=1, source_target_pairs={{0,4},{4,0},{8,12},{12,8},{1,5},{5,1},{9,13},{13,9},{2,6},{6,2},{1... | collective-permute-start | bytes 245768 | tf_op jit(solution)/shard_map/ppermute | solution.py:374
  8.5 0.7 %copy-start.4 = (bf16[3,3,3,8]{3,2,1,0:T(4,128)(2,1)S(1)}, bf16[3,3,3,8]{3,2,1,0:T(4,128)(2,1)}, u32[]{:S(2)}) copy-start(bf16[3,3,3,8]{3,2,1,0:T(4,128)(2,1)} %param.9) | copy-start | bytes 1300
  10.8 3.6 %collective-permute-start.2 = (bf16[2,96,256]{2,1,0:T(8,128)(2,1)S(1)}, bf16[2,96,256]{2,1,0:T(8,128)(2,1)S(1)}, u32[]{:S(2)}, u32[]{:S(2)}) collective-permute-start(bf16[2,96,256]{2,1,0:T(8,128)(2,1)S(1)} %get-tuple-element.32), channel_id=1, source_target_pairs={{0,0},{1,2},{2,1},{3,3},{4,4},{5,6},{6,5},{7,7},{8,8},{9,10},{10,9... | collective-permute-start | bytes 294920 | tf_op jit(solution)/shard_map/ppermute | solution.py:387
  11.5 3.9 %collective-permute-start.3 = (bf16[2,96,256]{2,1,0:T(8,128)(2,1)S(1)}, bf16[2,96,256]{2,1,0:T(8,128)(2,1)S(1)}, u32[]{:S(2)}, u32[]{:S(2)}) collective-permute-start(bf16[2,96,256]{2,1,0:T(8,128)(2,1)S(1)} %get-tuple-element.31), channel_id=1, source_target_pairs={{0,1},{1,0},{2,3},{3,2},{4,5},{5,4},{6,7},{7,6},{8,9},{9,8},{10,11... | collective-permute-start | bytes 294920 | tf_op jit(solution)/shard_map/ppermute | solution.py:384
  14.4 0.9 %copy-start.2 = (f32[8]{0:T(128)S(1)}, f32[8]{0:T(128)}, u32[]{:S(2)}) copy-start(f32[8]{0:T(128)} %param.8) | copy-start | bytes 100
  16.4 3.4 %collective-permute-start.4 = (f32[32,256]{1,0:T(8,128)S(1)}, f32[32,256]{1,0:T(8,128)S(1)}, u32[]{:S(2)}, u32[]{:S(2)}) collective-permute-start(f32[32,256]{1,0:T(8,128)S(1)} %get-tuple-element.20.refs_0_), channel_id=1, source_target_pairs={{0,3},{1,2},{2,1},{3,0},{4,7},{5,6},{6,5},{7,4},{8,11},{9,10},{10,... | collective-permute-start | bytes 98312 | tf_op jit(solution)/shard_map/ppermute | solution.py:25
  16.5 5.1 %collective-permute-start.5 = (f32[32,256]{1,0:T(8,128)S(1)}, f32[32,256]{1,0:T(8,128)S(1)}, u32[]{:S(2)}, u32[]{:S(2)}) collective-permute-start(f32[32,256]{1,0:T(8,128)S(1)} %get-tuple-element.20.refs_0_), channel_id=1, source_target_pairs={{0,2},{1,3},{2,0},{3,1},{4,6},{5,7},{6,4},{7,5},{8,10},{9,11},{10,... | collective-permute-start | bytes 98312 | tf_op jit(solution)/shard_map/ppermute | solution.py:25
  19.5 2.2 %collective-permute-start.6 = (f32[32,256]{1,0:T(8,128)S(1)}, f32[32,256]{1,0:T(8,128)S(1)}, u32[]{:S(2)}, u32[]{:S(2)}) collective-permute-start(f32[32,256]{1,0:T(8,128)S(1)} %get-tuple-element.20.refs_0_), channel_id=1, source_target_pairs={{0,1},{1,0},{2,3},{3,2},{4,5},{5,4},{6,7},{7,6},{8,9},{9,8},{10,11... | collective-permute-start | bytes 98312 | tf_op jit(solution)/shard_map/ppermute | solution.py:25
  23.3 2.3 %collective-permute-start.7 = (f32[32,128]{1,0:T(8,128)S(1)}, f32[32,128]{1,0:T(8,128)S(1)}, u32[]{:S(2)}, u32[]{:S(2)}) collective-permute-start(f32[32,128]{1,0:T(8,128)S(1)} %get-tuple-element.26), channel_id=1, source_target_pairs={{0,1},{1,0},{2,3},{3,2},{4,5},{5,4},{6,7},{7,6},{8,9},{9,8},{10,11... | collective-permute-start | bytes 49160 | tf_op jit(solution)/shard_map/ppermute | solution.py:443
  23.9 3.7 %collective-permute-start.8 = (f32[32,128]{1,0:T(8,128)S(1)}, f32[32,128]{1,0:T(8,128)S(1)}, u32[]{:S(2)}, u32[]{:S(2)}) collective-permute-start(f32[32,128]{1,0:T(8,128)S(1)} %get-tuple-element.26), channel_id=1, source_target_pairs={{0,2},{1,3},{2,0},{3,1},{4,6},{5,7},{6,4},{7,5},{8,10},{9,11},{10,... | collective-permute-start | bytes 49160 | tf_op jit(solution)/shard_map/ppermute | solution.py:443
  25.1 3.2 %collective-permute-start.9 = (f32[32,128]{1,0:T(8,128)S(1)}, f32[32,128]{1,0:T(8,128)S(1)}, u32[]{:S(2)}, u32[]{:S(2)}) collective-permute-start(f32[32,128]{1,0:T(8,128)S(1)} %get-tuple-element.26), channel_id=1, source_target_pairs={{0,3},{1,2},{2,1},{3,0},{4,7},{5,6},{6,5},{7,4},{8,11},{9,10},{10,... | collective-permute-start | bytes 49160 | tf_op jit(solution)/shard_map/ppermute | solution.py:443
  28.2 5.6 %collective-permute-start.10 = (f32[32,128]{1,0:T(8,128)S(1)}, f32[32,128]{1,0:T(8,128)S(1)}, u32[]{:S(2)}, u32[]{:S(2)}) collective-permute-start(f32[32,128]{1,0:T(8,128)S(1)} %add_add_fusion.refs_0_), channel_id=1, source_target_pairs={{0,4},{4,0},{8,12},{12,8},{1,5},{5,1},{9,13},{13,9},{2,6},{6,2},{1... | collective-permute-start | bytes 49160 | tf_op jit(solution)/shard_map/ppermute | solution.py:443
  30.3 4.7 %collective-permute-start.11 = (f32[32,128]{1,0:T(8,128)S(1)}, f32[32,128]{1,0:T(8,128)S(1)}, u32[]{:S(2)}, u32[]{:S(2)}) collective-permute-start(f32[32,128]{1,0:T(8,128)S(1)} %add_add_fusion.refs_0_), channel_id=1, source_target_pairs={{0,8},{4,12},{8,0},{12,4},{1,9},{5,13},{9,1},{13,5},{2,10},{6,14},... | collective-permute-start | bytes 49160 | tf_op jit(solution)/shard_map/ppermute | solution.py:443
  30.3 5.5 %collective-permute-start.12 = (f32[32,128]{1,0:T(8,128)S(1)}, f32[32,128]{1,0:T(8,128)S(1)}, u32[]{:S(2)}, u32[]{:S(2)}) collective-permute-start(f32[32,128]{1,0:T(8,128)S(1)} %add_add_fusion.refs_0_), channel_id=1, source_target_pairs={{0,12},{4,8},{8,4},{12,0},{1,13},{5,9},{9,5},{13,1},{2,14},{6,10},... | collective-permute-start | bytes 49160 | tf_op jit(solution)/shard_map/ppermute | solution.py:443

commit v4 on v0

v4 whole, which is shorter than its diff:
```python
import functools
import math

import jax
import jax.numpy as jnp
from jax import lax
from jax.experimental import pallas as pl
from jax.experimental.pallas import tpu as pltpu
from jax.sharding import PartitionSpec as P

F32 = jnp.float32
BF16 = jnp.bfloat16


def swap_pairs(count, step):
    pairs = []
    for i in range(count):
        j = i ^ 1 if step == 0 else ((i + 1) ^ 1) - 1
        pairs.append((i, j if 0 <= j < count else i))
    return pairs


def radix_stages(count):
    stages = []
    bit = 1
    while bit < count:
        if bit * 4 <= count:
            stages.append((bit, 2 * bit, 3 * bit))
            bit *= 4
        else:
            stages.append((bit,))
            bit *= 2
    return stages


def shift_up(x):
    return pltpu.roll(x, 1, 1)


def shift_down(x):
    return pltpu.roll(x, x.shape[1] - 1, 1)


def left(x, amount):
    return x if amount == 0 else pltpu.roll(x, x.shape[1] - amount, 1)


def right(x, amount):
    return x if amount == 0 else pltpu.roll(x, amount, 1)


def call(body, name, outs, *operands, scratch=()):
    operands = [pltpu.with_memory_space_constraint(x, pltpu.VMEM) for x in operands]
    return pl.pallas_call(
        body,
        out_shape=tuple(
            pltpu.VMEM(shape, dtype) if inside else jax.ShapeDtypeStruct(shape, dtype)
            for shape, dtype, inside in outs
        ),
        in_specs=[pl.BlockSpec(memory_space=pltpu.VMEM)] * len(operands),
        out_specs=tuple(pl.BlockSpec(memory_space=pltpu.VMEM) for _ in outs),
        scratch_shapes=list(scratch),
        name=name,
    )(*operands)


def dot(a, b):
    return lax.dot_general(a, b, (((1,), (0,)), ((), ())), preferred_element_type=F32)


def dot_t(a, b):
    return lax.dot_general(a, b, (((1,), (1,)), ((), ())), preferred_element_type=F32)


def terms(value):
    out = []
    for _ in range(3):
        term = value.astype(BF16).astype(F32)
        out.append(term)
        value = value - term
    return out


def window(x, start, size):
    width = x.shape[1]
    moved = pltpu.roll(x, (width - start) % width, 1)[:, :size]
    column = start + lax.broadcasted_iota(jnp.int32, moved.shape, 1)
    return jnp.where((column >= 0) & (column < width), moved, 0.0)


def split_body(dims, own_ref, prior_ref, *refs):
    planes, rows, chans, width, disp, space, cols, lanes = dims
    out_refs = refs[:disp]
    wide_ref = refs[disp]
    di = lax.axis_index("disp")
    half = 2 * planes
    for h in range(2):
        for p in range(planes):
            at = h * half + 2 * p
            wide_ref[at : at + 2] = prior_ref[p, 2 * h : 2 * h + 2]
    wide = wide_ref[...]
    pieces = [own_ref[...].reshape(planes * rows * chans, width).astype(F32)]
    for h in range(2):
        pieces += terms(wide[h * half : (h + 1) * half])
    whole = jnp.concatenate(pieces, axis=0)
    for s in range(disp):
        start = (di ^ s) * cols - 4
        out_refs[s][...] = window(whole, start, lanes).astype(BF16)


def rows_body(dims, *refs):
    planes, rows, chans, width, disp, space, cols, lanes = dims
    piece_refs = refs[:disp]
    cot_in_ref, one_ref, two_ref, prior_ref, cot_ref, wide_ref = refs[disp:]
    di = lax.axis_index("disp")
    even = lax.axis_index("space") % 2 == 0
    n = planes * rows * chans
    total = n * disp
    half = 2 * planes
    cot = window(jnp.concatenate([cot_in_ref[...]] * 2, axis=0), di * cols - 4, lanes)[:rows]
    cot_ref[...] = jnp.zeros(cot_ref.shape, F32)
    cot_ref[2 : 2 + rows] = cot
    for s in range(disp):
        g = di ^ s
        block = piece_refs[s][:n]
        at = pl.multiple_of(g * n, n)
        one_ref[pl.ds(at, n)] = block
        two_ref[pl.ds(at, n)] = block
        prior = piece_refs[s][n:].astype(F32)
        for h in range(2):
            base = 3 * half * h
            value = prior[base : base + half] + prior[base + half : base + 2 * half] + prior[base + 2 * half : base + 3 * half]
            for p in range(planes):
                prior_ref[g * planes + p, 2 + 2 * h : 4 + 2 * h] = value[2 * p : 2 * p + 2]
    for out_ref, down in ((one_ref, even), (two_ref, jnp.logical_not(even))):

        def put(h):
            for s in range(disp):
                prior = piece_refs[s][n:].astype(F32)
                at = pl.multiple_of((di ^ s) * 3 * half, 8)
                wide_ref[pl.ds(at, 3 * half)] = prior[3 * half * h : 3 * half * (h + 1)]
            for t, term in enumerate(terms(cot_ref[2 + 2 * h : 4 + 2 * h])):
                at = disp * 3 * half + 2 * t
                wide_ref[at : at + 2] = term
            rest = disp * 3 * half + 6
            wide_ref[rest:] = jnp.zeros((wide_ref.shape[0] - rest, lanes), F32)

        pl.when(down)(functools.partial(put, 1))
        pl.when(jnp.logical_not(down))(functools.partial(put, 0))
        out_ref[total:] = wide_ref[...].astype(BF16)


def bands_body(dims, base1_ref, base2_ref, base3_ref, base4_ref, bias_ref, band1_ref, band2_ref, band3_ref, band4_ref, col_ref):
    planes, rows, chans, width, disp, space, cols, lanes = dims

    def band(base, groups, count, step, used):
        pieces = []
        for c in range(3):
            piece = base[c * groups : (c + 1) * groups]
            for r in range(count):
                pieces.append(right(piece, step * r))
        return jnp.concatenate(pieces, axis=0)[:, :used].astype(BF16)

    band1_ref[...] = band(base1_ref[...], chans, rows + 6, chans, band1_ref.shape[1])
    band2_ref[...] = band(base2_ref[...], 1, rows + 4, chans, band2_ref.shape[1])
    band3_ref[...] = band(base3_ref[...], chans, rows + 2, 1, band3_ref.shape[1])
    band4 = band(base4_ref[...], chans, rows, chans, band4_ref.shape[1])
    n = rows * chans
    to = lax.broadcasted_iota(jnp.int32, (3 * n, 3 * n), 0)
    at = lax.broadcasted_iota(jnp.int32, (3 * n, 3 * n), 1)
    source = (to // n) * n + (to % rows) * chans + (to % n) // rows
    band4_ref[...] = dot((at == source).astype(BF16), band4).astype(BF16)
    diag = lax.broadcasted_iota(jnp.int32, (chans, chans), 0) == lax.broadcasted_iota(
        jnp.int32, (chans, chans), 1
    )
    bias = jnp.sum(jnp.where(diag, bias_ref[...], 0.0), axis=1, keepdims=True)
    col_ref[...] = jnp.concatenate([jnp.broadcast_to(bias, (chans, 2 * lanes))] * (rows + 6), axis=0)


def main_body(dims, *refs):
    planes, rows, chans, width, disp, space, cols, lanes = dims
    own_ref, za_ref, zb_ref, prior_in_ref, cot_in_ref, band1_ref, band2_ref, band3_ref, band4_ref, col_ref = refs[:10]
    back_refs = refs[10 : 10 + disp]
    x_ref, h_ref, slope_ref, prior_ref, cot_ref, s_ref, pg_ref, v_ref = refs[10 + disp :]
    zi = lax.axis_index("space")
    di = lax.axis_index("disp")
    z_even = zi % 2 == 0
    count = planes * disp
    n = count * rows * chans
    block = rows * chans
    xr = (rows + 8) * chans
    hr = (rows + 6) * chans
    gr = (rows + 2) * chans
    lr = rows + 4
    sr = 16
    two = 2 * lanes

    x_ref[:xr] = jnp.zeros((xr, lanes), BF16)
    x_ref[(count + 1) * xr :] = jnp.zeros((2 * xr, lanes), BF16)
    h_ref[:hr] = jnp.zeros((hr, lanes), BF16)
    h_ref[(count + 1) * hr :] = jnp.zeros((2 * hr, lanes), BF16)
    s_ref[...] = jnp.zeros(s_ref.shape, BF16)
    pg_ref[:gr] = jnp.zeros((gr, lanes), BF16)
    pg_ref[(count + 1) * gr :] = jnp.zeros((gr, lanes), BF16)
    for k in range(count):
        at = (k + 1) * xr + 4 * chans
        x_ref[at : at + block] = own_ref[k * block : (k + 1) * block]
    prior_ref[...] = prior_in_ref[...]
    cot_ref[...] = cot_in_ref[...]
    half = 2 * planes

    def place(ok, first, one, other, row, at8):
        def put(src):
            for k in range(count):
                at = (k + 1) * xr + row * chans
                if src is None:
                    x_ref[at : at + 4 * chans] = jnp.zeros((4 * chans, lanes), BF16)
                else:
                    x_ref[at : at + 4 * chans] = src[k * block : k * block + 4 * chans]
            if src is None:
                for k in range(count):
                    prior_ref[k, at8 : at8 + 2] = jnp.zeros((2, lanes), F32)
                cot_ref[at8 : at8 + 2] = jnp.zeros((2, lanes), F32)
                return
            extra = src[n:].astype(F32)
            for g in range(disp):
                base = g * 3 * half
                value = extra[base : base + half] + extra[base + half : base + 2 * half] + extra[base + 2 * half : base + 3 * half]
                for p in range(planes):
                    prior_ref[g * planes + p, at8 : at8 + 2] = value[2 * p : 2 * p + 2]
            base = disp * 3 * half
            cot_ref[at8 : at8 + 2] = extra[base : base + 2] + extra[base + 2 : base + 4] + extra[base + 4 : base + 6]

        pl.when(ok & first)(lambda: put(one))
        pl.when(ok & jnp.logical_not(first))(lambda: put(other))
        pl.when(jnp.logical_not(ok))(lambda: put(None))

    place(zi > 0, z_even, zb_ref, za_ref, 0, 0)
    place(zi < space - 1, z_even, za_ref, zb_ref, 4 + rows, 2 + rows)

    def pair(ref, p, size, taken):
        return jnp.concatenate([ref[p * size : p * size + taken], ref[(p + 1) * size : (p + 1) * size + taken]], axis=1)

    lane = lax.broadcasted_iota(jnp.int32, (hr, two), 1) % lanes
    column = di * cols - 4 + lane
    row_at = zi * rows - 3 + lax.broadcasted_iota(jnp.int32, (hr, two), 0) // chans
    inside = ((row_at >= 0) & (row_at < space * rows) & (column >= 0) & (column < width)).astype(F32)
    band1 = band1_ref[...]
    bias = col_ref[...]
    for p in range(0, count, 2):
        y = dot(band1, pair(x_ref, p, xr, 3 * xr))
        pre = y[hr : 2 * hr] + shift_up(y[:hr]) + shift_down(y[2 * hr :]) + bias
        sig = jax.nn.sigmoid(pre)
        hidden = (pre * sig * inside).astype(BF16)
        slope = (sig * (1.0 + pre * (1.0 - sig)) * inside)[2 * chans : hr - 2 * chans]
        for q in range(2):
            part = slice(q * lanes, (q + 1) * lanes)
            h_ref[(p + q + 1) * hr : (p + q + 2) * hr] = hidden[:, part]
            slope_ref[p + q] = slope[:, part]

    band2 = band2_ref[...]
    logits = []
    for p in range(0, count, 2):
        y = dot(band2, pair(h_ref, p, hr, 3 * hr))
        y = y[lr : 2 * lr] + shift_up(y[:lr]) + shift_down(y[2 * lr :])
        logits += [y[:, :lanes] + prior_ref[p], y[:, lanes:] + prior_ref[p + 1]]

    top = logits[0]
    for value in logits[1:]:
        top = jnp.maximum(top, value)
    summed = jnp.zeros((lr, lanes), F32)
    moment = jnp.zeros((lr, lanes), F32)
    weights = []
    for k, value in enumerate(logits):
        e = jnp.exp(value - top)
        weights.append(e)
        summed = summed + e
        moment = moment + e * ((k + 0.5) / count)
    disparity = moment / summed
    coef = cot_ref[...] / summed
    mine = lax.broadcasted_iota(jnp.int32, (lr, lanes), 1)
    mine = (mine >= 4) & (mine < 4 + cols)
    left2 = []
    for k in range(count):
        score = (coef * weights[k] * ((k + 0.5) / count - disparity)).astype(BF16)
        s_ref[(k + 1) * sr : (k + 1) * sr + lr] = score
        score = jnp.where(mine, score.astype(F32), 0.0)
        left2.append(jnp.concatenate([shift_down(score), score, shift_up(score)], axis=0).astype(BF16))

    band3 = band3_ref[...]
    mine = lax.broadcasted_iota(jnp.int32, (block, two), 1) % lanes
    mine = (mine >= 4) & (mine < 4 + cols)
    bias_sum = jnp.zeros((chans, two), F32)
    left1 = []
    for p in range(0, count, 2):
        y = dot(band3, pair(s_ref, p, sr, 3 * sr))
        hg = y[gr : 2 * gr] + shift_down(y[:gr]) + shift_up(y[2 * gr :])
        slope = jnp.concatenate([slope_ref[p], slope_ref[p + 1]], axis=1)
        pg = (hg * slope).astype(BF16)
        for q in range(2):
            pg_ref[(p + q + 1) * gr : (p + q + 2) * gr] = pg[:, q * lanes : (q + 1) * lanes]
        own = jnp.where(mine, pg.astype(F32)[chans : chans + block], 0.0)
        moved = (shift_down(own), own, shift_up(own))
        pieces = []
        for r in range(rows):
            part = slice(r * chans, (r + 1) * chans)
            bias_sum = bias_sum + own[part]
            pieces += [moved[c][part] for c in range(3)]
        left1.append(jnp.concatenate(pieces, axis=0).astype(BF16))

    inner = (rows + 4) * chans
    acc1 = None
    acc2 = None
    for p in range(0, count, 2):
        rhs = []
        for q in range(2):
            at = [(p + q + a) * xr + 2 * chans for a in range(4)]
            rhs.append(jnp.concatenate([x_ref[k : k + inner] for k in at], axis=0))
        part = dot_t(left1[p // 2], jnp.concatenate(rhs, axis=1))
        acc1 = part if acc1 is None else acc1 + part
        lhs = jnp.concatenate([left2[p], left2[p + 1]], axis=1)
        part = dot_t(lhs, pair(h_ref, p, hr, 4 * hr))
        acc2 = part if acc2 is None else acc2 + part

    out1 = jnp.zeros((3 * chans, acc1.shape[1]), F32)
    for r in range(rows):
        out1 = out1 + left(acc1[3 * chans * r : 3 * chans * (r + 1)], chans * (r + 1))
    acc2 = acc2[:, :256]
    row_in = lax.broadcasted_iota(jnp.int32, acc2.shape, 0) % lr
    out2 = jnp.zeros(acc2.shape, F32)
    for r in range(2, 2 + rows):
        out2 = out2 + jnp.where(row_in == r, left(acc2, chans * r), 0.0)
    out2 = jnp.concatenate(
        [jnp.sum(out2[c * lr : (c + 1) * lr], axis=0, keepdims=True) for c in range(3)]
        + [jnp.zeros((5, out2.shape[1]), F32)],
        axis=0,
    )
    tap = 3 * chans

    def packed(out, pitch):
        lane_p = lax.broadcasted_iota(jnp.int32, (out.shape[0], lanes), 1)
        total = jnp.zeros((out.shape[0], lanes), F32)
        for a in range(3):
            moved = left(out, a * (pitch - tap))[:, :lanes]
            total = jnp.where((lane_p >= a * tap) & (lane_p < (a + 1) * tap), moved, total)
        return total

    bias_sum = jnp.sum(bias_sum, axis=1, keepdims=True)
    sub = lax.broadcasted_iota(jnp.int32, (chans, lanes), 0)
    lane_b = lax.broadcasted_iota(jnp.int32, (chans, lanes), 1)
    bias_sum = jnp.sum(jnp.where(sub == lane_b, bias_sum, 0.0), axis=0, keepdims=True)
    second = packed(out2, hr)
    row_in = lax.broadcasted_iota(jnp.int32, second.shape, 0)
    second = jnp.where(row_in == 3, bias_sum, second)
    payload = jnp.concatenate([packed(out1, inner), second], axis=0)
    shown = jnp.concatenate([disparity[2 : 2 + rows]] * 2, axis=0)
    tail = jnp.concatenate(terms(payload) + terms(shown) + [jnp.zeros((8, lanes), F32)], axis=0).astype(BF16)

    band4 = band4_ref[...]
    for p in range(0, count, 2):
        y = dot(band4, pair(pg_ref, p, gr, 3 * gr))
        y = (y[block : 2 * block] + shift_down(y[:block]) + shift_up(y[2 * block :])).astype(BF16)
        for q in range(2):
            v_ref[(p + q) * block : (p + q + 1) * block] = y[:, q * lanes : (q + 1) * lanes]
    size = planes * block
    for s in range(disp):
        back_refs[s][:size] = v_ref[pl.ds(pl.multiple_of((di ^ s) * size, size), size)]
        back_refs[s][size:] = tail


def sum_body(chans, *refs):
    parts = refs[:-1]
    k = 3 * chans + 8
    sums = []
    for r in parts:
        n = r.shape[0] - 3 * k - 32
        value = r[n:].astype(F32)
        sums.append(value[:k] + value[k : 2 * k] + value[2 * k : 3 * k])
    refs[-1][...] = tree_sum(sums)


def join_body(dims, *refs):
    planes, rows, chans, width, disp, space, cols, lanes = dims
    parts = refs[:disp]
    grad_ref, disp_ref = refs[disp:]
    di = lax.axis_index("disp")
    n = planes * rows * chans
    k = 3 * (3 * chans + 8)
    total = None
    for s in range(disp):
        j = di ^ s
        shown = parts[s][n + k :].astype(F32)
        shown = shown[:8] + shown[8:16] + shown[16:24]
        value = jnp.concatenate([parts[s][:n].astype(F32), shown], axis=0)
        lane = lax.broadcasted_iota(jnp.int32, value.shape, 1)
        value = jnp.where((lane >= 4) & (lane < 4 + cols), value, 0.0)
        value = jnp.concatenate([value, jnp.zeros((value.shape[0], width - lanes), F32)], axis=1)
        value = pltpu.roll(value, (j * cols - 4 + width) % width, 1)
        total = value if total is None else total + value
    disp_ref[...] = total[n : n + rows]
    grad = total[:n].astype(BF16)
    for p in range(planes):
        for i in range(chans):
            at = (p * chans + i) * rows
            grad_ref[i, p] = grad[at : at + rows]


def tree_sum(parts):
    while len(parts) > 1:
        parts = [parts[k] + parts[k + 1] for k in range(0, len(parts), 2)]
    return parts[0]


def finish_body(chans, scale, *refs):
    gw_ref, gb_ref, gs_ref = refs[-3:]
    total = tree_sum([r[...] for r in refs[:-3]]) * scale
    for a in range(3):
        for b in range(3):
            at = (a * 3 + b) * chans
            for c in range(3):
                gw_ref[a, b, c] = total[c * chans : (c + 1) * chans, at : at + chans]
            gs_ref[a, b] = total[3 * chans : 3 * chans + 3, at : at + chans]
    gb_ref[...] = total[3 * chans + 3 : 3 * chans + 4, :chans]


def flipped(body, count):
    def run(*refs):
        return body(*refs[:count][::-1], *refs[count:])

    return run


def exchange(sends, axis):
    count = lax.axis_size(axis)
    return [sends[0]] + [
        lax.ppermute(sends[s], axis, [(i, i ^ s) for i in range(count)]) for s in range(1, count)
    ]


def shards(volume, w_first, b_first, w_second, prior_logits, cotangent):
    chans, planes, rows, width = volume.shape
    disp = lax.axis_size("disp")
    space = lax.axis_size("space")
    cols = width // disp
    lanes = -(-(cols + 8) // 128) * 128
    dims = (planes, rows, chans, width, disp, space, cols, lanes)
    count = planes * disp
    n = planes * rows * chans

    own = jnp.transpose(volume, (1, 2, 0, 3)).reshape(planes, rows * chans, width)
    sends = call(
        functools.partial(split_body, dims),
        "split",
        [((n + 12 * planes, lanes), BF16, True)] * disp,
        own, prior_logits,
        scratch=[pltpu.VMEM((4 * planes, width), F32)],
    )
    pieces = exchange(sends, "disp")

    xr = rows + 8
    hr = rows + 6
    base1 = jnp.transpose(w_first, (2, 3, 0, 1, 4)).astype(F32)
    base1 = jnp.pad(base1, ((0, 0), (0, 0), (0, 0), (0, xr - 3), (0, 0))).reshape(3 * chans, 3 * xr * chans)
    base1 = jnp.pad(base1, ((0, 0), (0, -base1.shape[1] % 128)))
    base2 = jnp.transpose(w_second, (2, 0, 1, 3)).astype(F32)
    base2 = jnp.pad(base2, ((0, 0), (0, 0), (0, hr - 3), (0, 0))).reshape(3, 3 * hr * chans)
    base2 = jnp.pad(base2, ((0, 5), (0, -base2.shape[1] % 128)))
    base3 = jnp.transpose(w_second[::-1, ::-1], (2, 3, 0, 1)).astype(F32)
    base3 = jnp.pad(base3, ((0, 0), (0, 0), (0, 0), (0, 16 - 3))).reshape(3 * chans, 3 * 16)
    base3 = jnp.pad(base3, ((0, 0), (0, 128 - base3.shape[1])))
    base4 = jnp.transpose(w_first[::-1, ::-1], (2, 4, 0, 1, 3)).astype(F32)
    base4 = jnp.pad(base4, ((0, 0), (0, 0), (0, 0), (0, rows - 1), (0, 0))).reshape(
        3 * chans, 3 * (rows + 2) * chans
    )
    base4 = jnp.pad(base4, ((0, 0), (0, -base4.shape[1] % 128)))
    bands = call(
        functools.partial(bands_body, dims),
        "bands",
        (
            ((3 * hr * chans, 3 * xr * chans), BF16, True),
            ((3 * (rows + 4), 3 * hr * chans), BF16, True),
            ((3 * (rows + 2) * chans, 3 * 16), BF16, True),
            ((3 * rows * chans, 3 * (rows + 2) * chans), BF16, True),
            ((hr * chans, 2 * lanes), F32, True),
        ),
        base1, base2, base3, base4, b_first[None, :],
    )

    extra = -(-(6 * count + 6) // 16) * 16
    send_one, send_two, prior, cot = call(
        flipped(functools.partial(rows_body, dims), disp),
        "rows",
        (
            ((n * disp + extra, lanes), BF16, True),
            ((n * disp + extra, lanes), BF16, True),
            ((count, rows + 4, lanes), F32, True),
            ((rows + 4, lanes), F32, True),
        ),
        *pieces[::-1], cotangent,
        scratch=[pltpu.VMEM((extra, lanes), F32)],
    )
    z_one = lax.ppermute(send_one, "space", swap_pairs(space, 0))
    z_two = lax.ppermute(send_two, "space", swap_pairs(space, 1))

    tail = 3 * (3 * chans + 8) + 32
    backs = call(
        functools.partial(main_body, dims),
        "main",
        [((n + tail, lanes), BF16, True)] * disp,
        send_one, z_one, z_two, prior, cot, *bands,
        scratch=[
            pltpu.VMEM(((count + 3) * xr * chans, lanes), BF16),
            pltpu.VMEM(((count + 3) * hr * chans, lanes), BF16),
            pltpu.VMEM((count, (rows + 2) * chans, lanes), F32),
            pltpu.VMEM((count, rows + 4, lanes), F32),
            pltpu.VMEM((rows + 4, lanes), F32),
            pltpu.VMEM(((count + 2) * 16, lanes), BF16),
            pltpu.VMEM(((count + 2) * (rows + 2) * chans, lanes), BF16),
            pltpu.VMEM((n * disp, lanes), BF16),
        ],
    )
    backs = exchange(backs, "disp")
    (pay,) = call(
        flipped(functools.partial(sum_body, chans), disp),
        "sum",
        (((3 * chans + 8, lanes), F32, True),),
        *backs[::-1],
    )
    stages = radix_stages(space)
    for k, steps in enumerate(stages):
        parts = [pay] + [lax.ppermute(pay, "space", [(i, i ^ s) for i in range(space)]) for s in steps]
        if k < len(stages) - 1:
            pay = tree_sum(parts)

    volume_grad, disparity = call(
        functools.partial(join_body, dims),
        "join",
        (((chans, planes, rows, width), BF16, False), ((rows, width), F32, False)),
        *backs,
    )

    scale = 16.0 / math.sqrt(planes * disp * rows * space * width)
    first_sum, bias_sum, second_sum = call(
        functools.partial(finish_body, chans, scale),
        "finish",
        (
            ((3, 3, 3, chans, chans), F32, False),
            ((1, chans), F32, False),
            ((3, 3, 3, chans), F32, False),
        ),
        *parts,
    )
    return (volume_grad, first_sum, bias_sum[0], second_sum, disparity)


def solution(mesh):
    return jax.shard_map(
        shards,
        mesh=mesh,
        in_specs=(
            P(None, "disp", ("groups", "space"), None),
            P(),
            P(),
            P(),
            P("disp", ("groups", "space"), None),
            P(("groups", "space"), None),
        ),
        out_specs=(
            P(None, "disp", ("groups", "space"), None),
            P(None, None, None, "groups", None),
            P("groups"),
            P(None, None, None, "groups"),
            P(("groups", "space"), None),
        ),
        check_vma=False,
    )
```

time: 139 us -> 33.9 us (0.24)
  blocking collectives: 78.7 us -> 0 us
  local copies, waits for them, and re-layouts: 22.4 us -> 3.07 us
  matrix products: 6.02 us -> 0 us
  Pallas kernels: 0 us -> 4.79 us
  starting transfers between devices: 17.4 us -> 14.6 us
    psum x1 -> x0, blocking collectives: 61.6 us -> none  [shards(): lax.psum((first_grad * grad_scale, bias_grad * grad_scale, second_grad *...]
    all_gather x3 -> x0, blocking collectives: 17.1 us -> none  [combined_all(): everything = jax.tree.map(lambda part: lax.all_gather(part, axis), value)]
    unnamed x109 -> x13, local copies, waits for them, and re-layouts: 11.4 us -> 1.42 us
    dot_general x6 -> x0, matrix products: 6.02 us -> none  [the longest x2 4.42 us: kernel_grad(): jnp.einsum('odhw,kdhw->ok', out_grad, stacked, preferred_element_type=jnp...]
    squeeze x35 -> x0, local copies, waits for them, and re-layouts: 5.99 us -> none  [correlate(): kernel[a, b, c]]
    pallas_call x0 -> x7, Pallas kernels: none -> 4.79 us  [call(): pl.pallas_call(body, out_shape=tuple((pltpu.VMEM(shape, dtype) if inside...]
    ppermute x8 -> x11, starting transfers between devices: 17.4 us -> 14.6 us  [the longest x6 5.05 us: exchange(): lax.ppermute(sends[s], axis, [(i, i ^ s) for i in range(count)])]
    concatenate x10 -> x0, local copies, waits for them, and re-layouts: 2.56 us -> none  [the longest x5 2.08 us: tap_stack(): jnp.concatenate([padded[:, a:a + planes, b:b + rows, c:c + width] for a i...]
  transfers between devices with their start and end apart: 8 -> 11, of which waited for: 3 -> 8; matrix products, arithmetic and copies ran while one was open for 7% -> 3% of each run, Pallas kernels for 0% -> 3%
where the time goes in v4:
time: 33.9 us; the launch traced here: 33.7 us
  starting transfers between devices  14.6 us (43%)
  waiting for transfers between devices  10.4 us (31%)
  Pallas kernels  4.79 us (14%)
  local copies, waits for them, and re-layouts  3.07 us (9%)
  between operations  0.8 us (2%)
    ppermute x6, waiting for transfers between devices, exchange(): lax.ppermute(sends[s], axis, [(i, i ^ s) for i in range(count)])  6.02 us
    ppermute x6, starting transfers between devices, exchange(): lax.ppermute(sends[s], axis, [(i, i ^ s) for i in range(count)])  5.05 us
    pallas_call x7, Pallas kernels, call(): pl.pallas_call(body, out_shape=tuple((pltpu.VMEM(shape, dtype) if inside...  4.79 us
    ppermute x1, starting transfers between devices, shards(): z_one = lax.ppermute(send_one, 'space', swap_pairs(space, 0))  4.46 us
    ppermute x3, starting transfers between devices, shards(): lax.ppermute(pay, 'space', [(i, i ^ s) for i in range(space)])  4.45 us
    ppermute x1, waiting for transfers between devices, shards(): z_one = lax.ppermute(send_one, 'space', swap_pairs(space, 0))  2.59 us
    ppermute x3, waiting for transfers between devices, shards(): lax.ppermute(pay, 'space', [(i, i ^ s) for i in range(space)])  1.76 us
    unnamed x13, local copies, waits for them, and re-layouts  1.42 us
  transfers between devices with their start and end apart: 11, of which 8 were waited for; matrix products, arithmetic and copies ran while one was open for 3% of the time, Pallas kernels for 3%

profile of v4, /device:TPU:0, one launch (start us, length us, event | category | flops | bytes accessed | tf_op | source)
XLA Modules:
  0.0 33.7 jit_solution(5722688975296586524)
XLA Ops:
  0.6 0.9 %copy.26 = bf16[4,4,8,256]{3,2,1,0:T(8,128)(2,1)S(1)} copy(bf16[4,4,8,256]{3,1,0,2:T(4,128)(2,1)} %bitcast.17) | data formatting | bytes 131072 | tf_op jit(solution)/shard_map/transpose | solution.py:450
  1.5 0.2 split.1
  1.7 2.4 %collective-permute-start = (bf16[176,128]{1,0:T(8,128)(2,1)S(1)}, bf16[176,128]{1,0:T(8,128)(2,1)S(1)}, u32[]{:S(2)}, u32[]{:S(2)}) collective-permute-start(bf16[176,128]{1,0:T(8,128)(2,1)S(1)} %get-tuple-element.27), channel_id=1, source_target_pairs={{0,3},{1,2},{2,1},{3,0},{4,7},{5,6},{6,5},{7,4},{8,11},{9,10},{10,... | collective-permute-start | bytes 135176 | tf_op jit(solution)/shard_map/ppermute | solution.py:436
  4.2 0.6 %collective-permute-start.1 = (bf16[176,128]{1,0:T(8,128)(2,1)S(1)}, bf16[176,128]{1,0:T(8,128)(2,1)S(1)}, u32[]{:S(2)}, u32[]{:S(2)}) collective-permute-start(bf16[176,128]{1,0:T(8,128)(2,1)S(1)} %get-tuple-element.28), channel_id=1, source_target_pairs={{0,2},{1,3},{2,0},{3,1},{4,6},{5,7},{6,4},{7,5},{8,10},{9,11},{10,... | collective-permute-start | bytes 135176 | tf_op jit(solution)/shard_map/ppermute | solution.py:436
  4.9 0.1 reshape.34
  5.0 0.1 copy.21
  5.1 0.6 %copy-done.3 = bf16[3,3,3,8,8]{4,3,2,1,0:T(8,128)(2,1)S(1)} copy-done((bf16[3,3,3,8,8]{4,3,2,1,0:T(8,128)(2,1)S(1)}, bf16[3,3,3,8,8]{4,3,2,1,0:T(8,128)(2,1)}, u32[]{:S(2)}) %copy-start.3) | copy-done | bytes 3480
  5.7 0.1 copy.24
  5.8 0.1 reshape.33
  6.1 0.1 reshape.31
  6.2 2.2 %collective-permute-done.1.refs_1_ = bf16[176,128]{1,0:T(8,128)(2,1)S(1)} collective-permute-done((bf16[176,128]{1,0:T(8,128)(2,1)S(1)}, bf16[176,128]{1,0:T(8,128)(2,1)S(1)}, u32[]{:S(2)}, u32[]{:S(2)}) %collective-permute-start.1) | collective-permute-done | bytes 45088 | tf_op jit(solution)/shard_map/ppermute | solution.py:436
  8.4 0.1 rows.1
  8.5 0.7 %collective-permute-start.4 = (bf16[624,128]{1,0:T(8,128)(2,1)S(1)}, bf16[624,128]{1,0:T(8,128)(2,1)S(1)}, u32[]{:S(2)}, u32[]{:S(2)}) collective-permute-start(bf16[624,128]{1,0:T(8,128)(2,1)S(1)} %get-tuple-element.32), channel_id=1, source_target_pairs={{0,0},{4,8},{8,4},{12,12},{1,1},{5,9},{9,5},{13,13},{2,2},{6,10},{... | collective-permute-start | bytes 479240 | tf_op jit(solution)/shard_map/ppermute | solution.py:503
  9.2 4.5 %collective-permute-start.3 = (bf16[624,128]{1,0:T(8,128)(2,1)S(1)}, bf16[624,128]{1,0:T(8,128)(2,1)S(1)}, u32[]{:S(2)}, u32[]{:S(2)}) collective-permute-start(bf16[624,128]{1,0:T(8,128)(2,1)S(1)} %get-tuple-element.31.refs_0_), channel_id=1, source_target_pairs={{0,4},{4,0},{8,12},{12,8},{1,5},{5,1},{9,13},{13,9},{2,6},{6,2},{1... | collective-permute-start | bytes 479240 | tf_op jit(solution)/shard_map/ppermute | solution.py:502
  13.8 0.2 reshape.30
  14.0 0.6 %copy-done.2 = f32[8]{0:T(128)S(1)} copy-done((f32[8]{0:T(128)S(1)}, f32[8]{0:T(128)}, u32[]{:S(2)}) %copy-start.2) | copy-done | bytes 56
  14.7 0.2 bands.1
  14.9 2.6 %collective-permute-done.3.refs_1_ = bf16[624,128]{1,0:T(8,128)(2,1)S(1)} collective-permute-done((bf16[624,128]{1,0:T(8,128)(2,1)S(1)}, bf16[624,128]{1,0:T(8,128)(2,1)S(1)}, u32[]{:S(2)}, u32[]{:S(2)}) %collective-permute-start.3) | collective-permute-done | bytes 159776 | tf_op jit(solution)/shard_map/ppermute | solution.py:502
  17.5 2.7 %main.1 = (bf16[256,128]{1,0:T(8,128)(2,1)S(1)}, bf16[256,128]{1,0:T(8,128)(2,1)S(1)}, bf16[256,128]{1,0:T(8,128)(2,1)S(1)}, bf16[256,128]{1,0:T(8,128)(2,1)S(1)}) custom-call(bf16[624,128]{1,0:T(8,128)(2,1)S(1)} %get-tuple-element.31.refs_0_, bf16[624,128]{1,0:T(8,128)(2,1)S(1)} %collective-permute-done.3.refs_1_, ...), custom_call_target="tpu_custom_call" | custom-call | tf_op jit(solution)/shard_map/main/pallas_call | solution.py:54
  20.2 0.1 collective-permute-start.5
  20.3 1.6 %collective-permute-start.6 = (bf16[256,128]{1,0:T(8,128)(2,1)S(1)}, bf16[256,128]{1,0:T(8,128)(2,1)S(1)}, u32[]{:S(2)}, u32[]{:S(2)}) collective-permute-start(bf16[256,128]{1,0:T(8,128)(2,1)S(1)} %get-tuple-element.42), channel_id=1, source_target_pairs={{0,2},{1,3},{2,0},{3,1},{4,6},{5,7},{6,4},{7,5},{8,10},{9,11},{10,... | collective-permute-start | bytes 196616 | tf_op jit(solution)/shard_map/ppermute | solution.py:436
  21.9 0.3 collective-permute-start.7
  22.1 2.6 %collective-permute-done.6.refs_2_.refs_1_ = bf16[256,128]{1,0:T(8,128)(2,1)S(1)} collective-permute-done((bf16[256,128]{1,0:T(8,128)(2,1)S(1)}, bf16[256,128]{1,0:T(8,128)(2,1)S(1)}, u32[]{:S(2)}, u32[]{:S(2)}) %collective-permute-start.6) | collective-permute-done | bytes 65568 | tf_op jit(solution)/shard_map/ppermute | solution.py:436
  24.8 1.1 %collective-permute-done.7.refs_3_.refs_0_ = bf16[256,128]{1,0:T(8,128)(2,1)S(1)} collective-permute-done((bf16[256,128]{1,0:T(8,128)(2,1)S(1)}, bf16[256,128]{1,0:T(8,128)(2,1)S(1)}, u32[]{:S(2)}, u32[]{:S(2)}) %collective-permute-start.7) | collective-permute-done | bytes 65568 | tf_op jit(solution)/shard_map/ppermute | solution.py:436
  25.9 1.4 %collective-permute-start.10 = (f32[32,128]{1,0:T(8,128)S(1)}, f32[32,128]{1,0:T(8,128)S(1)}, u32[]{:S(2)}, u32[]{:S(2)}) collective-permute-start(f32[32,128]{1,0:T(8,128)S(1)} %sum.1.refs_0_), channel_id=1, source_target_pairs={{0,12},{4,8},{8,4},{12,0},{1,13},{5,9},{9,5},{13,1},{2,14},{6,10},... | collective-permute-start | bytes 49160 | tf_op jit(solution)/shard_map/ppermute | solution.py:531
  27.4 1.8 %collective-permute-start.9 = (f32[32,128]{1,0:T(8,128)S(1)}, f32[32,128]{1,0:T(8,128)S(1)}, u32[]{:S(2)}, u32[]{:S(2)}) collective-permute-start(f32[32,128]{1,0:T(8,128)S(1)} %sum.1.refs_0_), channel_id=1, source_target_pairs={{0,8},{4,12},{8,0},{12,4},{1,9},{5,13},{9,1},{13,5},{2,10},{6,14},... | collective-permute-start | bytes 49160 | tf_op jit(solution)/shard_map/ppermute | solution.py:531
  29.2 1.2 %collective-permute-start.8 = (f32[32,128]{1,0:T(8,128)S(1)}, f32[32,128]{1,0:T(8,128)S(1)}, u32[]{:S(2)}, u32[]{:S(2)}) collective-permute-start(f32[32,128]{1,0:T(8,128)S(1)} %sum.1.refs_0_), channel_id=1, source_target_pairs={{0,4},{4,0},{8,12},{12,8},{1,5},{5,1},{9,13},{13,9},{2,6},{6,2},{1... | collective-permute-start | bytes 49160 | tf_op jit(solution)/shard_map/ppermute | solution.py:531
  30.4 0.8 %join.1 = (bf16[8,4,4,256]{3,2,1,0:T(4,128)(2,1)}, f32[4,256]{1,0:T(4,128)}) custom-call(bf16[256,128]{1,0:T(8,128)(2,1)S(1)} %get-tuple-element.40.refs_0_.refs_3_, bf16[256,128]{1,0:T(8,128)(2,1)S(1)} %collective-permute-done.5.refs_1_.refs_2_, bf16[256,128]{1,0:T(8,128)(2,1)S(1)} %collective-permute-done.6.refs_2_.refs_1_, ...), custom_call_target="tpu_custom_call" | custom-call | tf_op jit(solution)/shard_map/join/pallas_call | solution.py:54
  31.2 0.4 %collective-permute-done.10.refs_3_ = f32[32,128]{1,0:T(8,128)S(1)} collective-permute-done((f32[32,128]{1,0:T(8,128)S(1)}, f32[32,128]{1,0:T(8,128)S(1)}, u32[]{:S(2)}, u32[]{:S(2)}) %collective-permute-start.10) | collective-permute-done | bytes 16416 | tf_op jit(solution)/shard_map/ppermute | solution.py:531
  31.6 0.4 %collective-permute-done.9.refs_2_ = f32[32,128]{1,0:T(8,128)S(1)} collective-permute-done((f32[32,128]{1,0:T(8,128)S(1)}, f32[32,128]{1,0:T(8,128)S(1)}, u32[]{:S(2)}, u32[]{:S(2)}) %collective-permute-start.9) | collective-permute-done | bytes 16416 | tf_op jit(solution)/shard_map/ppermute | solution.py:531
  32.0 0.9 %collective-permute-done.8.refs_1_ = f32[32,128]{1,0:T(8,128)S(1)} collective-permute-done((f32[32,128]{1,0:T(8,128)S(1)}, f32[32,128]{1,0:T(8,128)S(1)}, u32[]{:S(2)}, u32[]{:S(2)}) %collective-permute-start.8) | collective-permute-done | bytes 16416 | tf_op jit(solution)/shard_map/ppermute | solution.py:531
  32.9 0.8 %finish.1 = (f32[3,3,3,8,8]{4,3,2,1,0:T(8,128)}, f32[1,8]{1,0:T(1,128)}, f32[3,3,3,8]{3,2,1,0:T(4,128)}) custom-call(f32[32,128]{1,0:T(8,128)S(1)} %sum.1.refs_0_, f32[32,128]{1,0:T(8,128)S(1)} %collective-permute-done.8.refs_1_, f32[32,128]{1,0:T(8,128)S(1)} %collective-permute-done.9.refs_2_, f32[32,128]{1,0:T(8,128)S(1)} %collective-permute-done.10.refs_3_), custom_call_target="tpu_custom_call" | custom-call | tf_op jit(solution)/shard_map/finish/pallas_call | solution.py:54
  (26 shorter events, 0.4 us)
Async XLA Ops:
  0.6 0.9 %copy-start = (f32[4,4,256]{2,1,0:T(4,128)S(1)}, f32[4,4,256]{2,1,0:T(4,128)}, u32[]{:S(2)}) copy-start(f32[4,4,256]{2,1,0:T(4,128)} %prior_ref.1) | copy-start | bytes 49156
  1.5 3.3 %copy-start.4 = (bf16[3,3,3,8]{3,2,1,0:T(4,128)(2,1)S(1)}, bf16[3,3,3,8]{3,2,1,0:T(4,128)(2,1)}, u32[]{:S(2)}) copy-start(bf16[3,3,3,8]{3,2,1,0:T(4,128)(2,1)} %param.9) | copy-start | bytes 1300
  1.7 4.5 %collective-permute-start = (bf16[176,128]{1,0:T(8,128)(2,1)S(1)}, bf16[176,128]{1,0:T(8,128)(2,1)S(1)}, u32[]{:S(2)}, u32[]{:S(2)}) collective-permute-start(bf16[176,128]{1,0:T(8,128)(2,1)S(1)} %get-tuple-element.27), channel_id=1, source_target_pairs={{0,3},{1,2},{2,1},{3,0},{4,7},{5,6},{6,5},{7,4},{8,11},{9,10},{10,... | collective-permute-start | bytes 135176 | tf_op jit(solution)/shard_map/ppermute | solution.py:436
  4.2 4.2 %collective-permute-start.1 = (bf16[176,128]{1,0:T(8,128)(2,1)S(1)}, bf16[176,128]{1,0:T(8,128)(2,1)S(1)}, u32[]{:S(2)}, u32[]{:S(2)}) collective-permute-start(bf16[176,128]{1,0:T(8,128)(2,1)S(1)} %get-tuple-element.28), channel_id=1, source_target_pairs={{0,2},{1,3},{2,0},{3,1},{4,6},{5,7},{6,4},{7,5},{8,10},{9,11},{10,... | collective-permute-start | bytes 135176 | tf_op jit(solution)/shard_map/ppermute | solution.py:436
  4.8 3.6 %collective-permute-start.2 = (bf16[176,128]{1,0:T(8,128)(2,1)S(1)}, bf16[176,128]{1,0:T(8,128)(2,1)S(1)}, u32[]{:S(2)}, u32[]{:S(2)}) collective-permute-start(bf16[176,128]{1,0:T(8,128)(2,1)S(1)} %get-tuple-element.29), channel_id=1, source_target_pairs={{0,1},{1,0},{2,3},{3,2},{4,5},{5,4},{6,7},{7,6},{8,9},{9,8},{10,11... | collective-permute-start | bytes 135176 | tf_op jit(solution)/shard_map/ppermute | solution.py:436
  4.9 0.8 %copy-start.3 = (bf16[3,3,3,8,8]{4,3,2,1,0:T(8,128)(2,1)S(1)}, bf16[3,3,3,8,8]{4,3,2,1,0:T(8,128)(2,1)}, u32[]{:S(2)}) copy-start(bf16[3,3,3,8,8]{4,3,2,1,0:T(8,128)(2,1)} %param.7) | copy-start | bytes 10372
  6.0 2.4 %copy-start.1 = (f32[4,256]{1,0:T(4,128)S(1)}, f32[4,256]{1,0:T(4,128)}, u32[]{:S(2)}) copy-start(f32[4,256]{1,0:T(4,128)} %refs_4_.1) | copy-start | bytes 12292
  8.5 6.3 %collective-permute-start.4 = (bf16[624,128]{1,0:T(8,128)(2,1)S(1)}, bf16[624,128]{1,0:T(8,128)(2,1)S(1)}, u32[]{:S(2)}, u32[]{:S(2)}) collective-permute-start(bf16[624,128]{1,0:T(8,128)(2,1)S(1)} %get-tuple-element.32), channel_id=1, source_target_pairs={{0,0},{4,8},{8,4},{12,12},{1,1},{5,9},{9,5},{13,13},{2,2},{6,10},{... | collective-permute-start | bytes 479240 | tf_op jit(solution)/shard_map/ppermute | solution.py:503
  9.2 8.3 %collective-permute-start.3 = (bf16[624,128]{1,0:T(8,128)(2,1)S(1)}, bf16[624,128]{1,0:T(8,128)(2,1)S(1)}, u32[]{:S(2)}, u32[]{:S(2)}) collective-permute-start(bf16[624,128]{1,0:T(8,128)(2,1)S(1)} %get-tuple-element.31.refs_0_), channel_id=1, source_target_pairs={{0,4},{4,0},{8,12},{12,8},{1,5},{5,1},{9,13},{13,9},{2,6},{6,2},{1... | collective-permute-start | bytes 479240 | tf_op jit(solution)/shard_map/ppermute | solution.py:502
  14.0 0.7 %copy-start.2 = (f32[8]{0:T(128)S(1)}, f32[8]{0:T(128)}, u32[]{:S(2)}) copy-start(f32[8]{0:T(128)} %param.8) | copy-start | bytes 100
  20.2 1.9 %collective-permute-start.5 = (bf16[256,128]{1,0:T(8,128)(2,1)S(1)}, bf16[256,128]{1,0:T(8,128)(2,1)S(1)}, u32[]{:S(2)}, u32[]{:S(2)}) collective-permute-start(bf16[256,128]{1,0:T(8,128)(2,1)S(1)} %get-tuple-element.41), channel_id=1, source_target_pairs={{0,1},{1,0},{2,3},{3,2},{4,5},{5,4},{6,7},{7,6},{8,9},{9,8},{10,11... | collective-permute-start | bytes 196616 | tf_op jit(solution)/shard_map/ppermute | solution.py:436
  20.3 4.5 %collective-permute-start.6 = (bf16[256,128]{1,0:T(8,128)(2,1)S(1)}, bf16[256,128]{1,0:T(8,128)(2,1)S(1)}, u32[]{:S(2)}, u32[]{:S(2)}) collective-permute-start(bf16[256,128]{1,0:T(8,128)(2,1)S(1)} %get-tuple-element.42), channel_id=1, source_target_pairs={{0,2},{1,3},{2,0},{3,1},{4,6},{5,7},{6,4},{7,5},{8,10},{9,11},{10,... | collective-permute-start | bytes 196616 | tf_op jit(solution)/shard_map/ppermute | solution.py:436
  21.9 4.0 %collective-permute-start.7 = (bf16[256,128]{1,0:T(8,128)(2,1)S(1)}, bf16[256,128]{1,0:T(8,128)(2,1)S(1)}, u32[]{:S(2)}, u32[]{:S(2)}) collective-permute-start(bf16[256,128]{1,0:T(8,128)(2,1)S(1)} %get-tuple-element.43), channel_id=1, source_target_pairs={{0,3},{1,2},{2,1},{3,0},{4,7},{5,6},{6,5},{7,4},{8,11},{9,10},{10,... | collective-permute-start | bytes 196616 | tf_op jit(solution)/shard_map/ppermute | solution.py:436
  25.9 5.6 %collective-permute-start.10 = (f32[32,128]{1,0:T(8,128)S(1)}, f32[32,128]{1,0:T(8,128)S(1)}, u32[]{:S(2)}, u32[]{:S(2)}) collective-permute-start(f32[32,128]{1,0:T(8,128)S(1)} %sum.1.refs_0_), channel_id=1, source_target_pairs={{0,12},{4,8},{8,4},{12,0},{1,13},{5,9},{9,5},{13,1},{2,14},{6,10},... | collective-permute-start | bytes 49160 | tf_op jit(solution)/shard_map/ppermute | solution.py:531
  27.4 4.6 %collective-permute-start.9 = (f32[32,128]{1,0:T(8,128)S(1)}, f32[32,128]{1,0:T(8,128)S(1)}, u32[]{:S(2)}, u32[]{:S(2)}) collective-permute-start(f32[32,128]{1,0:T(8,128)S(1)} %sum.1.refs_0_), channel_id=1, source_target_pairs={{0,8},{4,12},{8,0},{12,4},{1,9},{5,13},{9,1},{13,5},{2,10},{6,14},... | collective-permute-start | bytes 49160 | tf_op jit(solution)/shard_map/ppermute | solution.py:531
  29.2 3.7 %collective-permute-start.8 = (f32[32,128]{1,0:T(8,128)S(1)}, f32[32,128]{1,0:T(8,128)S(1)}, u32[]{:S(2)}, u32[]{:S(2)}) collective-permute-start(f32[32,128]{1,0:T(8,128)S(1)} %sum.1.refs_0_), channel_id=1, source_target_pairs={{0,4},{4,0},{8,12},{12,8},{1,5},{5,1},{9,13},{13,9},{2,6},{6,2},{1... | collective-permute-start | bytes 49160 | tf_op jit(solution)/shard_map/ppermute | solution.py:531

commit v5 on v4

--- a/solution.py
+++ b/solution.py
@@ -72,9 +72,9 @@
     return lax.dot_general(a, b, (((1,), (1,)), ((), ())), preferred_element_type=F32)
 
 
-def terms(value):
+def terms(value, count=3):
     out = []
-    for _ in range(3):
+    for _ in range(count):
         term = value.astype(BF16).astype(F32)
         out.append(term)
         value = value - term
@@ -86,6 +86,34 @@
     moved = pltpu.roll(x, (width - start) % width, 1)[:, :size]
     column = start + lax.broadcasted_iota(jnp.int32, moved.shape, 1)
     return jnp.where((column >= 0) & (column < width), moved, 0.0)
+
+
+def lanes_of(x):
+    return lax.broadcasted_iota(jnp.int32, x.shape, 1)
+
+
+def pack(x):
+    n = x.shape[0]
+    far = pltpu.roll(x[n // 2 :], 64, 1)
+    out = [jnp.where(lanes_of(far) < 64, x[: n // 2], far)]
+    for t in range(-(-n // 128)):
+        rest = jnp.zeros((8, 128), F32)
+        lane = lanes_of(rest)
+        for k in range(16):
+            at = (t * 16 + k) * 8
+            if at < n:
+                moved = pltpu.roll(x[at : at + 8], (8 * k + 64) % 128, 1)
+                rest = jnp.where((lane >= 8 * k) & (lane < 8 * k + 8), moved, rest)
+        out.append(rest)
+    return out
+
+
+def unpack(main, rest, k):
+    n = main.shape[0]
+    value = main[8 * k : 8 * k + 8] if 8 * k < n else pltpu.roll(main[8 * k - n : 8 * k - n + 8], 64, 1)
+    moved = rest[8 * (k // 16) : 8 * (k // 16) + 8]
+    moved = pltpu.roll(moved, (64 - 8 * (k % 16)) % 128, 1)
+    return jnp.where(lanes_of(value) < 64, value, moved)
 
 
 def split_body(dims, own_ref, prior_ref, *refs):
@@ -99,55 +127,60 @@
             at = h * half + 2 * p
             wide_ref[at : at + 2] = prior_ref[p, 2 * h : 2 * h + 2]
     wide = wide_ref[...]
-    pieces = [own_ref[...].reshape(planes * rows * chans, width).astype(F32)]
+    n = planes * rows * chans
+    pieces = [own_ref[...].reshape(n, width).astype(F32)]
     for h in range(2):
         pieces += terms(wide[h * half : (h + 1) * half])
     whole = jnp.concatenate(pieces, axis=0)
     for s in range(disp):
         start = (di ^ s) * cols - 4
-        out_refs[s][...] = window(whole, start, lanes).astype(BF16)
+        moved = window(whole, start, lanes)
+        out_refs[s][...] = jnp.concatenate(pack(moved[:n]) + pack(moved[n:]), axis=0).astype(BF16)
 
 
 def rows_body(dims, *refs):
     planes, rows, chans, width, disp, space, cols, lanes = dims
     piece_refs = refs[:disp]
-    cot_in_ref, one_ref, two_ref, prior_ref, cot_ref, wide_ref = refs[disp:]
+    cot_in_ref, one_ref, two_ref, prior_ref, cot_ref, wide_ref, rest_ref = refs[disp:]
     di = lax.axis_index("disp")
     even = lax.axis_index("space") % 2 == 0
     n = planes * rows * chans
-    total = n * disp
-    half = 2 * planes
+    half = n // 2
+    group = 2 * planes
     cot = window(jnp.concatenate([cot_in_ref[...]] * 2, axis=0), di * cols - 4, lanes)[:rows]
     cot_ref[...] = jnp.zeros(cot_ref.shape, F32)
     cot_ref[2 : 2 + rows] = cot
+    fine = []
     for s in range(disp):
         g = di ^ s
-        block = piece_refs[s][:n]
-        at = pl.multiple_of(g * n, n)
-        one_ref[pl.ds(at, n)] = block
-        two_ref[pl.ds(at, n)] = block
-        prior = piece_refs[s][n:].astype(F32)
+        block = piece_refs[s][:half]
+        at = pl.multiple_of(g * half, half)
+        one_ref[pl.ds(at, half)] = block
+        two_ref[pl.ds(at, half)] = block
+        value = piece_refs[s][half:].astype(F32)
+        rest_ref[pl.ds(pl.multiple_of(g * 8, 8), 8)] = value[:8]
+        value = value[8:]
+        value = [unpack(value[: 3 * group], value[3 * group :], k) for k in range(6)]
+        fine.append(value)
         for h in range(2):
-            base = 3 * half * h
-            value = prior[base : base + half] + prior[base + half : base + 2 * half] + prior[base + 2 * half : base + 3 * half]
+            prior = value[3 * h] + value[3 * h + 1] + value[3 * h + 2]
             for p in range(planes):
-                prior_ref[g * planes + p, 2 + 2 * h : 4 + 2 * h] = value[2 * p : 2 * p + 2]
+                prior_ref[g * planes + p, 2 + 2 * h : 4 + 2 * h] = prior[2 * p : 2 * p + 2]
     for out_ref, down in ((one_ref, even), (two_ref, jnp.logical_not(even))):
 
         def put(h):
             for s in range(disp):
-                prior = piece_refs[s][n:].astype(F32)
-                at = pl.multiple_of((di ^ s) * 3 * half, 8)
-                wide_ref[pl.ds(at, 3 * half)] = prior[3 * half * h : 3 * half * (h + 1)]
+                at = pl.multiple_of((di ^ s) * 3 * group, 8)
+                wide_ref[pl.ds(at, 3 * group)] = jnp.concatenate(fine[s][3 * h : 3 * h + 3], axis=0)
             for t, term in enumerate(terms(cot_ref[2 + 2 * h : 4 + 2 * h])):
-                at = disp * 3 * half + 2 * t
+                at = disp * 3 * group + 2 * t
                 wide_ref[at : at + 2] = term
-            rest = disp * 3 * half + 6
+            rest = disp * 3 * group + 6
             wide_ref[rest:] = jnp.zeros((wide_ref.shape[0] - rest, lanes), F32)
 
         pl.when(down)(functools.partial(put, 1))
         pl.when(jnp.logical_not(down))(functools.partial(put, 0))
-        out_ref[total:] = wide_ref[...].astype(BF16)
+        out_ref[disp * half :] = jnp.concatenate([rest_ref[...]] + pack(wide_ref[...]), axis=0).astype(BF16)
 
 
 def bands_body(dims, base1_ref, base2_ref, base3_ref, base4_ref, bias_ref, band1_ref, band2_ref, band3_ref, band4_ref, col_ref):
@@ -195,6 +228,19 @@
     sr = 16
     two = 2 * lanes
 
+    def place_rows(src, row):
+        main = src[: n // 2].astype(F32)
+        rest = src[n // 2 : n // 2 + 8 * disp].astype(F32)
+        side = planes * block // 2
+        for k in range(count):
+            g = k // planes
+            p = k % planes
+            value = [
+                unpack(main[g * side : (g + 1) * side], rest[8 * g : 8 * g + 8], p * rows + r) for r in range(rows)
+            ]
+            at = (k + 1) * xr + row * chans
+            x_ref[at : at + block] = jnp.concatenate(value, axis=0).astype(BF16)
+
     x_ref[:xr] = jnp.zeros((xr, lanes), BF16)
     x_ref[(count + 1) * xr :] = jnp.zeros((2 * xr, lanes), BF16)
     h_ref[:hr] = jnp.zeros((hr, lanes), BF16)
@@ -202,34 +248,30 @@
     s_ref[...] = jnp.zeros(s_ref.shape, BF16)
     pg_ref[:gr] = jnp.zeros((gr, lanes), BF16)
     pg_ref[(count + 1) * gr :] = jnp.zeros((gr, lanes), BF16)
-    for k in range(count):
-        at = (k + 1) * xr + 4 * chans
-        x_ref[at : at + block] = own_ref[k * block : (k + 1) * block]
+    place_rows(own_ref, 4)
     prior_ref[...] = prior_in_ref[...]
     cot_ref[...] = cot_in_ref[...]
     half = 2 * planes
 
     def place(ok, first, one, other, row, at8):
         def put(src):
-            for k in range(count):
-                at = (k + 1) * xr + row * chans
-                if src is None:
-                    x_ref[at : at + 4 * chans] = jnp.zeros((4 * chans, lanes), BF16)
-                else:
-                    x_ref[at : at + 4 * chans] = src[k * block : k * block + 4 * chans]
             if src is None:
                 for k in range(count):
+                    at = (k + 1) * xr + row * chans
+                    x_ref[at : at + 4 * chans] = jnp.zeros((4 * chans, lanes), BF16)
                     prior_ref[k, at8 : at8 + 2] = jnp.zeros((2, lanes), F32)
                 cot_ref[at8 : at8 + 2] = jnp.zeros((2, lanes), F32)
                 return
-            extra = src[n:].astype(F32)
+            place_rows(src, row)
+            extra = src[n // 2 + 8 * disp :].astype(F32)
+            used = -(-(3 * half * disp + 6) // 16) * 16
+            value = [unpack(extra[: used // 2], extra[used // 2 :], k) for k in range(3 * disp + 1)]
             for g in range(disp):
-                base = g * 3 * half
-                value = extra[base : base + half] + extra[base + half : base + 2 * half] + extra[base + 2 * half : base + 3 * half]
+                prior = value[3 * g] + value[3 * g + 1] + value[3 * g + 2]
                 for p in range(planes):
-                    prior_ref[g * planes + p, at8 : at8 + 2] = value[2 * p : 2 * p + 2]
-            base = disp * 3 * half
-            cot_ref[at8 : at8 + 2] = extra[base : base + 2] + extra[base + 2 : base + 4] + extra[base + 4 : base + 6]
+                    prior_ref[g * planes + p, at8 : at8 + 2] = prior[2 * p : 2 * p + 2]
+            cot = value[3 * disp]
+            cot_ref[at8 : at8 + 2] = cot[:2] + cot[2:4] + cot[4:6]
 
         pl.when(ok & first)(lambda: put(one))
         pl.when(ok & jnp.logical_not(first))(lambda: put(other))
@@ -354,15 +396,25 @@
     second = jnp.where(row_in == 3, bias_sum, second)
     payload = jnp.concatenate([packed(out1, inner), second], axis=0)
     shown = jnp.concatenate([disparity[2 : 2 + rows]] * 2, axis=0)
-    tail = jnp.concatenate(terms(payload) + terms(shown) + [jnp.zeros((8, lanes), F32)], axis=0).astype(BF16)
+    tail = jnp.concatenate(terms(payload, 2) + terms(shown, 2), axis=0).astype(BF16)
 
     band4 = band4_ref[...]
+    found = [None] * planes
     for p in range(0, count, 2):
         y = dot(band4, pair(pg_ref, p, gr, 3 * gr))
-        y = (y[block : 2 * block] + shift_down(y[:block]) + shift_up(y[2 * block :])).astype(BF16)
+        y = y[block : 2 * block] + shift_down(y[:block]) + shift_up(y[2 * block :])
         for q in range(2):
-            v_ref[(p + q) * block : (p + q + 1) * block] = y[:, q * lanes : (q + 1) * lanes]
-    size = planes * block
+            moved = y[:, q * lanes : (q + 1) * lanes]
+            k = p + q
+            found[k % planes] = moved
+        if (p + 2) % planes == 0:
+            near = jnp.concatenate(found[: planes // 2], axis=0)
+            far = jnp.concatenate(found[planes // 2 :], axis=0)
+            near = pltpu.roll(near, lanes - 4, 1)
+            far = pltpu.roll(far, 60, 1)
+            at = (p // planes) * (planes * block // 2)
+            v_ref[at : at + planes * block // 2] = jnp.where(lanes_of(near) < 64, near, far).astype(BF16)
+    size = planes * block // 2
     for s in range(disp):
         back_refs[s][:size] = v_ref[pl.ds(pl.multiple_of((di ^ s) * size, size), size)]
         back_refs[s][size:] = tail
@@ -373,9 +425,9 @@
     k = 3 * chans + 8
     sums = []
     for r in parts:
-        n = r.shape[0] - 3 * k - 32
+        n = r.shape[0] - 2 * k - 16
         value = r[n:].astype(F32)
-        sums.append(value[:k] + value[k : 2 * k] + value[2 * k : 3 * k])
+        sums.append(value[:k] + value[k : 2 * k])
     refs[-1][...] = tree_sum(sums)
 
 
@@ -385,17 +437,17 @@
     grad_ref, disp_ref = refs[disp:]
     di = lax.axis_index("disp")
     n = planes * rows * chans
-    k = 3 * (3 * chans + 8)
+    k = 2 * (3 * chans + 8)
     total = None
     for s in range(disp):
         j = di ^ s
-        shown = parts[s][n + k :].astype(F32)
-        shown = shown[:8] + shown[8:16] + shown[16:24]
-        value = jnp.concatenate([parts[s][:n].astype(F32), shown], axis=0)
-        lane = lax.broadcasted_iota(jnp.int32, value.shape, 1)
-        value = jnp.where((lane >= 4) & (lane < 4 + cols), value, 0.0)
+        shown = parts[s][n // 2 + k :].astype(F32)
+        shown = pltpu.roll(shown[:8] + shown[8:], lanes - 4, 1)
+        main = parts[s][: n // 2].astype(F32)
+        value = jnp.concatenate([main, pltpu.roll(main, 64, 1), shown], axis=0)
+        value = jnp.where(lanes_of(value) < cols, value, 0.0)
         value = jnp.concatenate([value, jnp.zeros((value.shape[0], width - lanes), F32)], axis=1)
-        value = pltpu.roll(value, (j * cols - 4 + width) % width, 1)
+        value = pltpu.roll(value, j * cols, 1)
         total = value if total is None else total + value
     disp_ref[...] = total[n : n + rows]
     grad = total[:n].astype(BF16)
@@ -451,7 +503,7 @@
     sends = call(
         functools.partial(split_body, dims),
         "split",
-        [((n + 12 * planes, lanes), BF16, True)] * disp,
+        [((n // 2 + 8 + 6 * planes + 8, lanes), BF16, True)] * disp,
         own, prior_logits,
         scratch=[pltpu.VMEM((4 * planes, width), F32)],
     )
@@ -487,26 +539,27 @@
     )
 
     extra = -(-(6 * count + 6) // 16) * 16
+    sent = (n // 2 + 8) * disp + extra // 2 + 8 * -(-extra // 128)
     send_one, send_two, prior, cot = call(
         flipped(functools.partial(rows_body, dims), disp),
         "rows",
         (
-            ((n * disp + extra, lanes), BF16, True),
-            ((n * disp + extra, lanes), BF16, True),
+            ((sent, lanes), BF16, True),
+            ((sent, lanes), BF16, True),
             ((count, rows + 4, lanes), F32, True),
             ((rows + 4, lanes), F32, True),
         ),
         *pieces[::-1], cotangent,
-        scratch=[pltpu.VMEM((extra, lanes), F32)],
+        scratch=[pltpu.VMEM((extra, lanes), F32), pltpu.VMEM((8 * disp, lanes), F32)],
     )
     z_one = lax.ppermute(send_one, "space", swap_pairs(space, 0))
     z_two = lax.ppermute(send_two, "space", swap_pairs(space, 1))
 
-    tail = 3 * (3 * chans + 8) + 32
+    tail = 2 * (3 * chans + 8) + 16
     backs = call(
         functools.partial(main_body, dims),
         "main",
-        [((n + tail, lanes), BF16, True)] * disp,
+        [((n // 2 + tail, lanes), BF16, True)] * disp,
         send_one, z_one, z_two, prior, cot, *bands,
         scratch=[
             pltpu.VMEM(((count + 3) * xr * chans, lanes), BF16),
@@ -516,7 +569,7 @@
             pltpu.VMEM((rows + 4, lanes), F32),
             pltpu.VMEM(((count + 2) * 16, lanes), BF16),
             pltpu.VMEM(((count + 2) * (rows + 2) * chans, lanes), BF16),
-            pltpu.VMEM((n * disp, lanes), BF16),
+            pltpu.VMEM((n // 2 * disp, lanes), BF16),
         ],
     )
     backs = exchange(backs, "disp")

time: 33.9 us -> 32.3 us (0.953)
  waiting for transfers between devices: 10.4 us -> 8 us
  Pallas kernels: 4.79 us -> 5.52 us
    ppermute x6, waiting for transfers between devices: 6.02 us -> 4.17 us  [exchange(): lax.ppermute(sends[s], axis, [(i, i ^ s) for i in range(count)])]
    ppermute x1, waiting for transfers between devices: 2.59 us -> 1.63 us  [shards(): z_one = lax.ppermute(send_one, 'space', swap_pairs(space, 0))]
    pallas_call x7, Pallas kernels: 4.79 us -> 5.52 us  [call(): pl.pallas_call(body, out_shape=tuple((pltpu.VMEM(shape, dtype) if inside...]
    ppermute x3, waiting for transfers between devices: 1.76 us -> 2.2 us  [shards(): lax.ppermute(pay, 'space', [(i, i ^ s) for i in range(space)])]
  transfers between devices with their start and end apart: 11 -> 11, of which waited for: 8 -> 7; matrix products, arithmetic and copies ran while one was open for 3% -> 3% of each run, Pallas kernels for 3% -> 3%
where the time goes in v5:
time: 32.3 us; the launch traced here: 32.1 us
  starting transfers between devices  14.6 us (45%)
  waiting for transfers between devices  8 us (25%)
  Pallas kernels  5.52 us (17%)
  local copies, waits for them, and re-layouts  3.08 us (10%)
  between operations  0.81 us (3%)
    pallas_call x7, Pallas kernels, call(): pl.pallas_call(body, out_shape=tuple((pltpu.VMEM(shape, dtype) if inside...  5.52 us
    ppermute x6, starting transfers between devices, exchange(): lax.ppermute(sends[s], axis, [(i, i ^ s) for i in range(count)])  5.05 us
    ppermute x1, starting transfers between devices, shards(): z_one = lax.ppermute(send_one, 'space', swap_pairs(space, 0))  4.46 us
    ppermute x3, starting transfers between devices, shards(): lax.ppermute(pay, 'space', [(i, i ^ s) for i in range(space)])  4.45 us
    ppermute x6, waiting for transfers between devices, exchange(): lax.ppermute(sends[s], axis, [(i, i ^ s) for i in range(count)])  4.17 us
    ppermute x3, waiting for transfers between devices, shards(): lax.ppermute(pay, 'space', [(i, i ^ s) for i in range(space)])  2.2 us
    ppermute x1, waiting for transfers between devices, shards(): z_one = lax.ppermute(send_one, 'space', swap_pairs(space, 0))  1.63 us
    unnamed x13, local copies, waits for them, and re-layouts  1.42 us
  transfers between devices with their start and end apart: 11, of which 7 were waited for; matrix products, arithmetic and copies ran while one was open for 3% of the time, Pallas kernels for 3%

profile of v5, /device:TPU:0, one launch (start us, length us, event | category | flops | bytes accessed | tf_op | source)
XLA Modules:
  0.0 32.1 jit_solution(7047705835474177190)
XLA Ops:
  0.6 0.9 %copy.26 = bf16[4,4,8,256]{3,2,1,0:T(8,128)(2,1)S(1)} copy(bf16[4,4,8,256]{3,1,0,2:T(4,128)(2,1)} %bitcast.17) | data formatting | bytes 131072 | tf_op jit(solution)/shard_map/transpose | solution.py:502
  1.5 0.4 %split.1 = (bf16[104,128]{1,0:T(8,128)(2,1)S(1)}, bf16[104,128]{1,0:T(8,128)(2,1)S(1)}, bf16[104,128]{1,0:T(8,128)(2,1)S(1)}, bf16[104,128]{1,0:T(8,128)(2,1)S(1)}) custom-call(bf16[4,32,256]{2,1,0:T(8,128)(2,1)S(1)} %bitcast.14, f32[4,4,256]{2,1,0:T(4,128)S(1)} %copy-done), custom_call_target="tpu_custom_call" | custom-call | tf_op jit(solution)/shard_map/split/pallas_call | solution.py:54
  2.0 2.4 %collective-permute-start = (bf16[104,128]{1,0:T(8,128)(2,1)S(1)}, bf16[104,128]{1,0:T(8,128)(2,1)S(1)}, u32[]{:S(2)}, u32[]{:S(2)}) collective-permute-start(bf16[104,128]{1,0:T(8,128)(2,1)S(1)} %get-tuple-element.27), channel_id=1, source_target_pairs={{0,3},{1,2},{2,1},{3,0},{4,7},{5,6},{6,5},{7,4},{8,11},{9,10},{10,... | collective-permute-start | bytes 79880 | tf_op jit(solution)/shard_map/ppermute | solution.py:488
  4.4 0.6 %collective-permute-start.1 = (bf16[104,128]{1,0:T(8,128)(2,1)S(1)}, bf16[104,128]{1,0:T(8,128)(2,1)S(1)}, u32[]{:S(2)}, u32[]{:S(2)}) collective-permute-start(bf16[104,128]{1,0:T(8,128)(2,1)S(1)} %get-tuple-element.28), channel_id=1, source_target_pairs={{0,2},{1,3},{2,0},{3,1},{4,6},{5,7},{6,4},{7,5},{8,10},{9,11},{10,... | collective-permute-start | bytes 79880 | tf_op jit(solution)/shard_map/ppermute | solution.py:488
  5.2 0.1 reshape.34
  5.2 0.1 copy.21
  5.3 0.6 %copy-done.3 = bf16[3,3,3,8,8]{4,3,2,1,0:T(8,128)(2,1)S(1)} copy-done((bf16[3,3,3,8,8]{4,3,2,1,0:T(8,128)(2,1)S(1)}, bf16[3,3,3,8,8]{4,3,2,1,0:T(8,128)(2,1)}, u32[]{:S(2)}) %copy-start.3) | copy-done | bytes 3480
  5.9 0.1 copy.24
  6.1 0.1 reshape.33
  6.4 0.2 reshape.30
  6.7 0.1 reshape.31
  6.8 1.5 %collective-permute-done.1.refs_1_ = bf16[104,128]{1,0:T(8,128)(2,1)S(1)} collective-permute-done((bf16[104,128]{1,0:T(8,128)(2,1)S(1)}, bf16[104,128]{1,0:T(8,128)(2,1)S(1)}, u32[]{:S(2)}, u32[]{:S(2)}) %collective-permute-start.1) | collective-permute-done | bytes 26656 | tf_op jit(solution)/shard_map/ppermute | solution.py:488
  8.3 0.3 rows.1
  8.6 0.7 %collective-permute-start.4 = (bf16[352,128]{1,0:T(8,128)(2,1)S(1)}, bf16[352,128]{1,0:T(8,128)(2,1)S(1)}, u32[]{:S(2)}, u32[]{:S(2)}) collective-permute-start(bf16[352,128]{1,0:T(8,128)(2,1)S(1)} %get-tuple-element.32), channel_id=1, source_target_pairs={{0,0},{4,8},{8,4},{12,12},{1,1},{5,9},{9,5},{13,13},{2,2},{6,10},{... | collective-permute-start | bytes 270344 | tf_op jit(solution)/shard_map/ppermute | solution.py:556
  9.3 4.5 %collective-permute-start.3 = (bf16[352,128]{1,0:T(8,128)(2,1)S(1)}, bf16[352,128]{1,0:T(8,128)(2,1)S(1)}, u32[]{:S(2)}, u32[]{:S(2)}) collective-permute-start(bf16[352,128]{1,0:T(8,128)(2,1)S(1)} %get-tuple-element.31.refs_0_), channel_id=1, source_target_pairs={{0,4},{4,0},{8,12},{12,8},{1,5},{5,1},{9,13},{13,9},{2,6},{6,2},{1... | collective-permute-start | bytes 270344 | tf_op jit(solution)/shard_map/ppermute | solution.py:555
  13.7 0.7 %copy-done.2 = f32[8]{0:T(128)S(1)} copy-done((f32[8]{0:T(128)S(1)}, f32[8]{0:T(128)}, u32[]{:S(2)}) %copy-start.2) | copy-done | bytes 56
  14.4 0.2 bands.1
  14.6 1.6 %collective-permute-done.3.refs_1_ = bf16[352,128]{1,0:T(8,128)(2,1)S(1)} collective-permute-done((bf16[352,128]{1,0:T(8,128)(2,1)S(1)}, bf16[352,128]{1,0:T(8,128)(2,1)S(1)}, u32[]{:S(2)}, u32[]{:S(2)}) %collective-permute-start.3) | collective-permute-done | bytes 90144 | tf_op jit(solution)/shard_map/ppermute | solution.py:555
  16.2 3.0 %main.1 = (bf16[144,128]{1,0:T(8,128)(2,1)S(1)}, bf16[144,128]{1,0:T(8,128)(2,1)S(1)}, bf16[144,128]{1,0:T(8,128)(2,1)S(1)}, bf16[144,128]{1,0:T(8,128)(2,1)S(1)}) custom-call(bf16[352,128]{1,0:T(8,128)(2,1)S(1)} %get-tuple-element.31.refs_0_, bf16[352,128]{1,0:T(8,128)(2,1)S(1)} %collective-permute-done.3.refs_1_, ...), custom_call_target="tpu_custom_call" | custom-call | tf_op jit(solution)/shard_map/main/pallas_call | solution.py:54
  19.2 0.1 collective-permute-start.5
  19.3 1.0 %collective-permute-start.6 = (bf16[144,128]{1,0:T(8,128)(2,1)S(1)}, bf16[144,128]{1,0:T(8,128)(2,1)S(1)}, u32[]{:S(2)}, u32[]{:S(2)}) collective-permute-start(bf16[144,128]{1,0:T(8,128)(2,1)S(1)} %get-tuple-element.42), channel_id=1, source_target_pairs={{0,2},{1,3},{2,0},{3,1},{4,6},{5,7},{6,4},{7,5},{8,10},{9,11},{10,... | collective-permute-start | bytes 110600 | tf_op jit(solution)/shard_map/ppermute | solution.py:488
  20.3 0.9 %collective-permute-start.7 = (bf16[144,128]{1,0:T(8,128)(2,1)S(1)}, bf16[144,128]{1,0:T(8,128)(2,1)S(1)}, u32[]{:S(2)}, u32[]{:S(2)}) collective-permute-start(bf16[144,128]{1,0:T(8,128)(2,1)S(1)} %get-tuple-element.43), channel_id=1, source_target_pairs={{0,3},{1,2},{2,1},{3,0},{4,7},{5,6},{6,5},{7,4},{8,11},{9,10},{10,... | collective-permute-start | bytes 110600 | tf_op jit(solution)/shard_map/ppermute | solution.py:488
  21.2 2.2 %collective-permute-done.6.refs_2_.refs_1_ = bf16[144,128]{1,0:T(8,128)(2,1)S(1)} collective-permute-done((bf16[144,128]{1,0:T(8,128)(2,1)S(1)}, bf16[144,128]{1,0:T(8,128)(2,1)S(1)}, u32[]{:S(2)}, u32[]{:S(2)}) %collective-permute-start.6) | collective-permute-done | bytes 36896 | tf_op jit(solution)/shard_map/ppermute | solution.py:488
  23.4 0.4 %collective-permute-done.7.refs_3_.refs_0_ = bf16[144,128]{1,0:T(8,128)(2,1)S(1)} collective-permute-done((bf16[144,128]{1,0:T(8,128)(2,1)S(1)}, bf16[144,128]{1,0:T(8,128)(2,1)S(1)}, u32[]{:S(2)}, u32[]{:S(2)}) %collective-permute-start.7) | collective-permute-done | bytes 36896 | tf_op jit(solution)/shard_map/ppermute | solution.py:488
  23.8 1.4 %collective-permute-start.10 = (f32[32,128]{1,0:T(8,128)S(1)}, f32[32,128]{1,0:T(8,128)S(1)}, u32[]{:S(2)}, u32[]{:S(2)}) collective-permute-start(f32[32,128]{1,0:T(8,128)S(1)} %sum.1.refs_0_), channel_id=1, source_target_pairs={{0,12},{4,8},{8,4},{12,0},{1,13},{5,9},{9,5},{13,1},{2,14},{6,10},... | collective-permute-start | bytes 49160 | tf_op jit(solution)/shard_map/ppermute | solution.py:584
  25.3 2.3 %collective-permute-start.9 = (f32[32,128]{1,0:T(8,128)S(1)}, f32[32,128]{1,0:T(8,128)S(1)}, u32[]{:S(2)}, u32[]{:S(2)}) collective-permute-start(f32[32,128]{1,0:T(8,128)S(1)} %sum.1.refs_0_), channel_id=1, source_target_pairs={{0,8},{4,12},{8,0},{12,4},{1,9},{5,13},{9,1},{13,5},{2,10},{6,14},... | collective-permute-start | bytes 49160 | tf_op jit(solution)/shard_map/ppermute | solution.py:584
  27.6 0.7 %collective-permute-start.8 = (f32[32,128]{1,0:T(8,128)S(1)}, f32[32,128]{1,0:T(8,128)S(1)}, u32[]{:S(2)}, u32[]{:S(2)}) collective-permute-start(f32[32,128]{1,0:T(8,128)S(1)} %sum.1.refs_0_), channel_id=1, source_target_pairs={{0,4},{4,0},{8,12},{12,8},{1,5},{5,1},{9,13},{13,9},{2,6},{6,2},{1... | collective-permute-start | bytes 49160 | tf_op jit(solution)/shard_map/ppermute | solution.py:584
  28.3 0.8 %join.1 = (bf16[8,4,4,256]{3,2,1,0:T(4,128)(2,1)}, f32[4,256]{1,0:T(4,128)}) custom-call(bf16[144,128]{1,0:T(8,128)(2,1)S(1)} %get-tuple-element.40.refs_0_.refs_3_, bf16[144,128]{1,0:T(8,128)(2,1)S(1)} %collective-permute-done.5.refs_1_.refs_2_, bf16[144,128]{1,0:T(8,128)(2,1)S(1)} %collective-permute-done.6.refs_2_.refs_1_, ...), custom_call_target="tpu_custom_call" | custom-call | tf_op jit(solution)/shard_map/join/pallas_call | solution.py:54
  29.1 0.5 %collective-permute-done.10.refs_3_ = f32[32,128]{1,0:T(8,128)S(1)} collective-permute-done((f32[32,128]{1,0:T(8,128)S(1)}, f32[32,128]{1,0:T(8,128)S(1)}, u32[]{:S(2)}, u32[]{:S(2)}) %collective-permute-start.10) | collective-permute-done | bytes 16416 | tf_op jit(solution)/shard_map/ppermute | solution.py:584
  29.6 0.3 %collective-permute-done.9.refs_2_ = f32[32,128]{1,0:T(8,128)S(1)} collective-permute-done((f32[32,128]{1,0:T(8,128)S(1)}, f32[32,128]{1,0:T(8,128)S(1)}, u32[]{:S(2)}, u32[]{:S(2)}) %collective-permute-start.9) | collective-permute-done | bytes 16416 | tf_op jit(solution)/shard_map/ppermute | solution.py:584
  29.9 1.4 %collective-permute-done.8.refs_1_ = f32[32,128]{1,0:T(8,128)S(1)} collective-permute-done((f32[32,128]{1,0:T(8,128)S(1)}, f32[32,128]{1,0:T(8,128)S(1)}, u32[]{:S(2)}, u32[]{:S(2)}) %collective-permute-start.8) | collective-permute-done | bytes 16416 | tf_op jit(solution)/shard_map/ppermute | solution.py:584
  31.3 0.8 %finish.1 = (f32[3,3,3,8,8]{4,3,2,1,0:T(8,128)}, f32[1,8]{1,0:T(1,128)}, f32[3,3,3,8]{3,2,1,0:T(4,128)}) custom-call(f32[32,128]{1,0:T(8,128)S(1)} %sum.1.refs_0_, f32[32,128]{1,0:T(8,128)S(1)} %collective-permute-done.8.refs_1_, f32[32,128]{1,0:T(8,128)S(1)} %collective-permute-done.9.refs_2_, f32[32,128]{1,0:T(8,128)S(1)} %collective-permute-done.10.refs_3_), custom_call_target="tpu_custom_call" | custom-call | tf_op jit(solution)/shard_map/finish/pallas_call | solution.py:54
  (26 shorter events, 0.3 us)
Async XLA Ops:
  0.6 0.9 %copy-start = (f32[4,4,256]{2,1,0:T(4,128)S(1)}, f32[4,4,256]{2,1,0:T(4,128)}, u32[]{:S(2)}) copy-start(f32[4,4,256]{2,1,0:T(4,128)} %prior_ref.1) | copy-start | bytes 49156
  1.5 3.6 %copy-start.4 = (bf16[3,3,3,8]{3,2,1,0:T(4,128)(2,1)S(1)}, bf16[3,3,3,8]{3,2,1,0:T(4,128)(2,1)}, u32[]{:S(2)}) copy-start(bf16[3,3,3,8]{3,2,1,0:T(4,128)(2,1)} %param.9) | copy-start | bytes 1300
  2.0 4.8 %collective-permute-start = (bf16[104,128]{1,0:T(8,128)(2,1)S(1)}, bf16[104,128]{1,0:T(8,128)(2,1)S(1)}, u32[]{:S(2)}, u32[]{:S(2)}) collective-permute-start(bf16[104,128]{1,0:T(8,128)(2,1)S(1)} %get-tuple-element.27), channel_id=1, source_target_pairs={{0,3},{1,2},{2,1},{3,0},{4,7},{5,6},{6,5},{7,4},{8,11},{9,10},{10,... | collective-permute-start | bytes 79880 | tf_op jit(solution)/shard_map/ppermute | solution.py:488
  4.4 3.8 %collective-permute-start.1 = (bf16[104,128]{1,0:T(8,128)(2,1)S(1)}, bf16[104,128]{1,0:T(8,128)(2,1)S(1)}, u32[]{:S(2)}, u32[]{:S(2)}) collective-permute-start(bf16[104,128]{1,0:T(8,128)(2,1)S(1)} %get-tuple-element.28), channel_id=1, source_target_pairs={{0,2},{1,3},{2,0},{3,1},{4,6},{5,7},{6,4},{7,5},{8,10},{9,11},{10,... | collective-permute-start | bytes 79880 | tf_op jit(solution)/shard_map/ppermute | solution.py:488
  5.1 3.2 %collective-permute-start.2 = (bf16[104,128]{1,0:T(8,128)(2,1)S(1)}, bf16[104,128]{1,0:T(8,128)(2,1)S(1)}, u32[]{:S(2)}, u32[]{:S(2)}) collective-permute-start(bf16[104,128]{1,0:T(8,128)(2,1)S(1)} %get-tuple-element.29), channel_id=1, source_target_pairs={{0,1},{1,0},{2,3},{3,2},{4,5},{5,4},{6,7},{7,6},{8,9},{9,8},{10,11... | collective-permute-start | bytes 79880 | tf_op jit(solution)/shard_map/ppermute | solution.py:488
  5.1 0.8 %copy-start.3 = (bf16[3,3,3,8,8]{4,3,2,1,0:T(8,128)(2,1)S(1)}, bf16[3,3,3,8,8]{4,3,2,1,0:T(8,128)(2,1)}, u32[]{:S(2)}) copy-start(bf16[3,3,3,8,8]{4,3,2,1,0:T(8,128)(2,1)} %param.7) | copy-start | bytes 10372
  6.6 1.6 %copy-start.1 = (f32[4,256]{1,0:T(4,128)S(1)}, f32[4,256]{1,0:T(4,128)}, u32[]{:S(2)}) copy-start(f32[4,256]{1,0:T(4,128)} %refs_4_.1) | copy-start | bytes 12292
  8.6 6.0 %collective-permute-start.4 = (bf16[352,128]{1,0:T(8,128)(2,1)S(1)}, bf16[352,128]{1,0:T(8,128)(2,1)S(1)}, u32[]{:S(2)}, u32[]{:S(2)}) collective-permute-start(bf16[352,128]{1,0:T(8,128)(2,1)S(1)} %get-tuple-element.32), channel_id=1, source_target_pairs={{0,0},{4,8},{8,4},{12,12},{1,1},{5,9},{9,5},{13,13},{2,2},{6,10},{... | collective-permute-start | bytes 270344 | tf_op jit(solution)/shard_map/ppermute | solution.py:556
  9.3 7.0 %collective-permute-start.3 = (bf16[352,128]{1,0:T(8,128)(2,1)S(1)}, bf16[352,128]{1,0:T(8,128)(2,1)S(1)}, u32[]{:S(2)}, u32[]{:S(2)}) collective-permute-start(bf16[352,128]{1,0:T(8,128)(2,1)S(1)} %get-tuple-element.31.refs_0_), channel_id=1, source_target_pairs={{0,4},{4,0},{8,12},{12,8},{1,5},{5,1},{9,13},{13,9},{2,6},{6,2},{1... | collective-permute-start | bytes 270344 | tf_op jit(solution)/shard_map/ppermute | solution.py:555
  13.7 0.7 %copy-start.2 = (f32[8]{0:T(128)S(1)}, f32[8]{0:T(128)}, u32[]{:S(2)}) copy-start(f32[8]{0:T(128)} %param.8) | copy-start | bytes 100
  19.2 1.9 %collective-permute-start.5 = (bf16[144,128]{1,0:T(8,128)(2,1)S(1)}, bf16[144,128]{1,0:T(8,128)(2,1)S(1)}, u32[]{:S(2)}, u32[]{:S(2)}) collective-permute-start(bf16[144,128]{1,0:T(8,128)(2,1)S(1)} %get-tuple-element.41), channel_id=1, source_target_pairs={{0,1},{1,0},{2,3},{3,2},{4,5},{5,4},{6,7},{7,6},{8,9},{9,8},{10,11... | collective-permute-start | bytes 110600 | tf_op jit(solution)/shard_map/ppermute | solution.py:488
  19.3 4.1 %collective-permute-start.6 = (bf16[144,128]{1,0:T(8,128)(2,1)S(1)}, bf16[144,128]{1,0:T(8,128)(2,1)S(1)}, u32[]{:S(2)}, u32[]{:S(2)}) collective-permute-start(bf16[144,128]{1,0:T(8,128)(2,1)S(1)} %get-tuple-element.42), channel_id=1, source_target_pairs={{0,2},{1,3},{2,0},{3,1},{4,6},{5,7},{6,4},{7,5},{8,10},{9,11},{10,... | collective-permute-start | bytes 110600 | tf_op jit(solution)/shard_map/ppermute | solution.py:488
  20.3 3.5 %collective-permute-start.7 = (bf16[144,128]{1,0:T(8,128)(2,1)S(1)}, bf16[144,128]{1,0:T(8,128)(2,1)S(1)}, u32[]{:S(2)}, u32[]{:S(2)}) collective-permute-start(bf16[144,128]{1,0:T(8,128)(2,1)S(1)} %get-tuple-element.43), channel_id=1, source_target_pairs={{0,3},{1,2},{2,1},{3,0},{4,7},{5,6},{6,5},{7,4},{8,11},{9,10},{10,... | collective-permute-start | bytes 110600 | tf_op jit(solution)/shard_map/ppermute | solution.py:488
  23.8 5.7 %collective-permute-start.10 = (f32[32,128]{1,0:T(8,128)S(1)}, f32[32,128]{1,0:T(8,128)S(1)}, u32[]{:S(2)}, u32[]{:S(2)}) collective-permute-start(f32[32,128]{1,0:T(8,128)S(1)} %sum.1.refs_0_), channel_id=1, source_target_pairs={{0,12},{4,8},{8,4},{12,0},{1,13},{5,9},{9,5},{13,1},{2,14},{6,10},... | collective-permute-start | bytes 49160 | tf_op jit(solution)/shard_map/ppermute | solution.py:584
  25.3 4.7 %collective-permute-start.9 = (f32[32,128]{1,0:T(8,128)S(1)}, f32[32,128]{1,0:T(8,128)S(1)}, u32[]{:S(2)}, u32[]{:S(2)}) collective-permute-start(f32[32,128]{1,0:T(8,128)S(1)} %sum.1.refs_0_), channel_id=1, source_target_pairs={{0,8},{4,12},{8,0},{12,4},{1,9},{5,13},{9,1},{13,5},{2,10},{6,14},... | collective-permute-start | bytes 49160 | tf_op jit(solution)/shard_map/ppermute | solution.py:584
  27.6 3.7 %collective-permute-start.8 = (f32[32,128]{1,0:T(8,128)S(1)}, f32[32,128]{1,0:T(8,128)S(1)}, u32[]{:S(2)}, u32[]{:S(2)}) collective-permute-start(f32[32,128]{1,0:T(8,128)S(1)} %sum.1.refs_0_), channel_id=1, source_target_pairs={{0,4},{4,0},{8,12},{12,8},{1,5},{5,1},{9,13},{13,9},{2,6},{6,2},{1... | collective-permute-start | bytes 49160 | tf_op jit(solution)/shard_map/ppermute | solution.py:584

commit v6 on v5

--- a/solution.py
+++ b/solution.py
@@ -49,8 +49,9 @@
     return x if amount == 0 else pltpu.roll(x, amount, 1)
 
 
-def call(body, name, outs, *operands, scratch=()):
-    operands = [pltpu.with_memory_space_constraint(x, pltpu.VMEM) for x in operands]
+def call(body, name, outs, *operands, scratch=(), inside=True):
+    if inside:
+        operands = [pltpu.with_memory_space_constraint(x, pltpu.VMEM) for x in operands]
     return pl.pallas_call(
         body,
         out_shape=tuple(
@@ -116,26 +117,33 @@
     return jnp.where(lanes_of(value) < 64, value, moved)
 
 
-def split_body(dims, own_ref, prior_ref, *refs):
+def split_body(dims, volume_ref, prior_ref, *refs):
     planes, rows, chans, width, disp, space, cols, lanes = dims
     out_refs = refs[:disp]
-    wide_ref = refs[disp]
+    wide_ref, found_ref = refs[disp : disp + 2]
+    own_refs = refs[disp + 2 :]
     di = lax.axis_index("disp")
-    half = 2 * planes
+    group = 2 * planes
+    n = planes * rows * chans
+    for i in range(chans):
+        value = volume_ref[i].astype(F32)
+        for p in range(planes):
+            for j, ref in enumerate(own_refs):
+                ref[pl.ds(p * rows * chans + i, rows, stride=chans)] = value[p][:, j * 128 : (j + 1) * 128]
     for h in range(2):
         for p in range(planes):
-            at = h * half + 2 * p
+            at = h * group + 2 * p
             wide_ref[at : at + 2] = prior_ref[p, 2 * h : 2 * h + 2]
     wide = wide_ref[...]
-    n = planes * rows * chans
-    pieces = [own_ref[...].reshape(n, width).astype(F32)]
+    pieces = [jnp.concatenate([ref[...] for ref in own_refs], axis=1)]
     for h in range(2):
-        pieces += terms(wide[h * half : (h + 1) * half])
+        pieces += terms(wide[h * group : (h + 1) * group])
     whole = jnp.concatenate(pieces, axis=0)
+    for t in range(disp):
+        moved = window(whole, t * cols - 4, lanes)
+        found_ref[t] = jnp.concatenate(pack(moved[:n]) + pack(moved[n:]), axis=0).astype(BF16)
     for s in range(disp):
-        start = (di ^ s) * cols - 4
-        moved = window(whole, start, lanes)
-        out_refs[s][...] = jnp.concatenate(pack(moved[:n]) + pack(moved[n:]), axis=0).astype(BF16)
+        out_refs[s][...] = found_ref[di ^ s]
 
 
 def rows_body(dims, *refs):
@@ -194,7 +202,7 @@
                 pieces.append(right(piece, step * r))
         return jnp.concatenate(pieces, axis=0)[:, :used].astype(BF16)
 
-    band1_ref[...] = band(base1_ref[...], chans, rows + 6, chans, band1_ref.shape[1])
+    band1_ref[...] = band(base1_ref[...], chans, rows + 2, chans, band1_ref.shape[1])
     band2_ref[...] = band(base2_ref[...], 1, rows + 4, chans, band2_ref.shape[1])
     band3_ref[...] = band(base3_ref[...], chans, rows + 2, 1, band3_ref.shape[1])
     band4 = band(base4_ref[...], chans, rows, chans, band4_ref.shape[1])
@@ -289,10 +297,23 @@
     inside = ((row_at >= 0) & (row_at < space * rows) & (column >= 0) & (column < width)).astype(F32)
     band1 = band1_ref[...]
     bias = col_ref[...]
+    yr = (rows + 2) * chans
+    wr = (rows + 4) * chans
     for p in range(0, count, 2):
-        y = dot(band1, pair(x_ref, p, xr, 3 * xr))
-        pre = y[hr : 2 * hr] + shift_up(y[:hr]) + shift_down(y[2 * hr :]) + bias
-        sig = jax.nn.sigmoid(pre)
+        pre = []
+        for at in (0, 4 * chans):
+            rhs = [
+                jnp.concatenate(
+                    [x_ref[(p + q + a) * xr + at : (p + q + a) * xr + at + wr] for a in range(3)], axis=0
+                )
+                for q in range(2)
+            ]
+            y = dot(band1, jnp.concatenate(rhs, axis=1))
+            skip = at // 2
+            y = [y[c * yr + skip : (c + 1) * yr] for c in range(3)]
+            pre.append(y[1] + shift_up(y[0]) + shift_down(y[2]))
+        pre = jnp.concatenate(pre, axis=0) + bias
+        sig = 0.5 * jnp.tanh(0.5 * pre) + 0.5
         hidden = (pre * sig * inside).astype(BF16)
         slope = (sig * (1.0 + pre * (1.0 - sig)) * inside)[2 * chans : hr - 2 * chans]
         for q in range(2):
@@ -356,18 +377,19 @@
     for p in range(0, count, 2):
         rhs = []
         for q in range(2):
-            at = [(p + q + a) * xr + 2 * chans for a in range(4)]
+            at = [(p + q + a) * xr + 2 * chans for a in range(3)]
             rhs.append(jnp.concatenate([x_ref[k : k + inner] for k in at], axis=0))
         part = dot_t(left1[p // 2], jnp.concatenate(rhs, axis=1))
         acc1 = part if acc1 is None else acc1 + part
         lhs = jnp.concatenate([left2[p], left2[p + 1]], axis=1)
-        part = dot_t(lhs, pair(h_ref, p, hr, 4 * hr))
+        part = dot_t(lhs, pair(h_ref, p, hr, 3 * hr))
         acc2 = part if acc2 is None else acc2 + part
 
+    acc1 = jnp.concatenate([acc1, jnp.zeros((acc1.shape[0], -acc1.shape[1] % 128), F32)], axis=1)
+    acc2 = jnp.concatenate([acc2, jnp.zeros((acc2.shape[0], -acc2.shape[1] % 128), F32)], axis=1)
     out1 = jnp.zeros((3 * chans, acc1.shape[1]), F32)
     for r in range(rows):
         out1 = out1 + left(acc1[3 * chans * r : 3 * chans * (r + 1)], chans * (r + 1))
-    acc2 = acc2[:, :256]
     row_in = lax.broadcasted_iota(jnp.int32, acc2.shape, 0) % lr
     out2 = jnp.zeros(acc2.shape, F32)
     for r in range(2, 2 + rows):
@@ -499,20 +521,26 @@
     count = planes * disp
     n = planes * rows * chans
 
-    own = jnp.transpose(volume, (1, 2, 0, 3)).reshape(planes, rows * chans, width)
+    piece = n // 2 + 8 + 6 * planes + 8
     sends = call(
         functools.partial(split_body, dims),
         "split",
-        [((n // 2 + 8 + 6 * planes + 8, lanes), BF16, True)] * disp,
-        own, prior_logits,
-        scratch=[pltpu.VMEM((4 * planes, width), F32)],
+        [((piece, lanes), BF16, True)] * disp,
+        volume, prior_logits,
+        inside=False,
+        scratch=[
+            pltpu.VMEM((4 * planes, width), F32),
+            pltpu.VMEM((disp, piece, lanes), BF16),
+        ]
+        + [pltpu.VMEM((n, 128), F32)] * (width // 128),
     )
     pieces = exchange(sends, "disp")
 
     xr = rows + 8
     hr = rows + 6
     base1 = jnp.transpose(w_first, (2, 3, 0, 1, 4)).astype(F32)
-    base1 = jnp.pad(base1, ((0, 0), (0, 0), (0, 0), (0, xr - 3), (0, 0))).reshape(3 * chans, 3 * xr * chans)
+    base1 = jnp.pad(base1, ((0, 0), (0, 0), (0, 0), (0, rows + 1), (0, 0)))
+    base1 = base1.reshape(3 * chans, 3 * (rows + 4) * chans)
     base1 = jnp.pad(base1, ((0, 0), (0, -base1.shape[1] % 128)))
     base2 = jnp.transpose(w_second, (2, 0, 1, 3)).astype(F32)
     base2 = jnp.pad(base2, ((0, 0), (0, 0), (0, hr - 3), (0, 0))).reshape(3, 3 * hr * chans)
@@ -529,7 +557,7 @@
         functools.partial(bands_body, dims),
         "bands",
         (
-            ((3 * hr * chans, 3 * xr * chans), BF16, True),
+            ((3 * (rows + 2) * chans, 3 * (rows + 4) * chans), BF16, True),
             ((3 * (rows + 4), 3 * hr * chans), BF16, True),
             ((3 * (rows + 2) * chans, 3 * 16), BF16, True),
             ((3 * rows * chans, 3 * (rows + 2) * chans), BF16, True),
@@ -586,10 +614,10 @@
             pay = tree_sum(parts)
 
     volume_grad, disparity = call(
-        functools.partial(join_body, dims),
+        flipped(functools.partial(join_body, dims), disp),
         "join",
         (((chans, planes, rows, width), BF16, False), ((rows, width), F32, False)),
-        *backs,
+        *backs[::-1],
     )
 
     scale = 16.0 / math.sqrt(planes * disp * rows * space * width)

time: 32.3 us -> 31.6 us (0.978)
  local copies, waits for them, and re-layouts: 3.08 us -> 2.1 us
  Pallas kernels: 5.52 us -> 5.97 us
    transpose x1 -> x0, local copies, waits for them, and re-layouts: 0.87 us -> none  [shards(): jnp.transpose(volume, (1, 2, 0, 3)).reshape(planes, rows * chans, width)]
    pallas_call x7, Pallas kernels: 5.52 us -> 5.97 us  [call(): pl.pallas_call(body, out_shape=tuple((pltpu.VMEM(shape, dtype) if inside...]
    unnamed x13 -> x11, local copies, waits for them, and re-layouts: 1.42 us -> 1.42 us
where the time goes in v6:
time: 31.6 us; the launch traced here: 31.4 us
  starting transfers between devices  14.6 us (46%)
  waiting for transfers between devices  7.88 us (25%)
  Pallas kernels  5.97 us (19%)
  local copies, waits for them, and re-layouts  2.1 us (7%)
  between operations  0.79 us (2%)
    pallas_call x7, Pallas kernels, call(): pl.pallas_call(body, out_shape=tuple((pltpu.VMEM(shape, dtype) if inside...  5.97 us
    ppermute x6, starting transfers between devices, exchange(): lax.ppermute(sends[s], axis, [(i, i ^ s) for i in range(count)])  5.04 us
    ppermute x1, starting transfers between devices, shards(): z_one = lax.ppermute(send_one, 'space', swap_pairs(space, 0))  4.46 us
    ppermute x3, starting transfers between devices, shards(): lax.ppermute(pay, 'space', [(i, i ^ s) for i in range(space)])  4.45 us
    ppermute x6, waiting for transfers between devices, exchange(): lax.ppermute(sends[s], axis, [(i, i ^ s) for i in range(count)])  4.19 us
    ppermute x3, waiting for transfers between devices, shards(): lax.ppermute(pay, 'space', [(i, i ^ s) for i in range(space)])  2.06 us
    ppermute x1, waiting for transfers between devices, shards(): z_one = lax.ppermute(send_one, 'space', swap_pairs(space, 0))  1.63 us
    unnamed x11, local copies, waits for them, and re-layouts  1.42 us
  transfers between devices with their start and end apart: 11, of which 7 were waited for; matrix products, arithmetic and copies ran while one was open for 3% of the time, Pallas kernels for 3%

profile of v6, /device:TPU:0, one launch (start us, length us, event | category | flops | bytes accessed | tf_op | source)
XLA Modules:
  0.0 31.4 jit_solution(7084858632304599017)
XLA Ops:
  0.6 1.1 %split.1 = (bf16[104,128]{1,0:T(8,128)(2,1)S(1)}, bf16[104,128]{1,0:T(8,128)(2,1)S(1)}, bf16[104,128]{1,0:T(8,128)(2,1)S(1)}, bf16[104,128]{1,0:T(8,128)(2,1)S(1)}) custom-call(bf16[8,4,4,256]{3,2,1,0:T(4,128)(2,1)} %volume_ref.1, f32[4,4,256]{2,1,0:T(4,128)} %prior_ref.1), custom_call_target="tpu_custom_call" | custom-call | tf_op jit(solution)/shard_map/split/pallas_call | solution.py:55
  1.8 2.4 %collective-permute-start = (bf16[104,128]{1,0:T(8,128)(2,1)S(1)}, bf16[104,128]{1,0:T(8,128)(2,1)S(1)}, u32[]{:S(2)}, u32[]{:S(2)}) collective-permute-start(bf16[104,128]{1,0:T(8,128)(2,1)S(1)} %get-tuple-element.27), channel_id=1, source_target_pairs={{0,3},{1,2},{2,1},{3,0},{4,7},{5,6},{6,5},{7,4},{8,11},{9,10},{10,... | collective-permute-start | bytes 79880 | tf_op jit(solution)/shard_map/ppermute | solution.py:510
  4.2 0.6 %collective-permute-start.1 = (bf16[104,128]{1,0:T(8,128)(2,1)S(1)}, bf16[104,128]{1,0:T(8,128)(2,1)S(1)}, u32[]{:S(2)}, u32[]{:S(2)}) collective-permute-start(bf16[104,128]{1,0:T(8,128)(2,1)S(1)} %get-tuple-element.28), channel_id=1, source_target_pairs={{0,2},{1,3},{2,0},{3,1},{4,6},{5,7},{6,4},{7,5},{8,10},{9,11},{10,... | collective-permute-start | bytes 79880 | tf_op jit(solution)/shard_map/ppermute | solution.py:510
  4.9 0.0 collective-permute-start.2
  5.0 0.1 reshape.30
  5.1 0.1 copy.19
  5.1 0.6 %copy-done.2 = bf16[3,3,3,8,8]{4,3,2,1,0:T(8,128)(2,1)S(1)} copy-done((bf16[3,3,3,8,8]{4,3,2,1,0:T(8,128)(2,1)S(1)}, bf16[3,3,3,8,8]{4,3,2,1,0:T(8,128)(2,1)}, u32[]{:S(2)}) %copy-start.2) | copy-done | bytes 3480
  5.7 0.1 copy.22
  5.9 0.1 reshape.29
  6.1 0.1 reshape.26
  6.3 0.1 reshape.27
  6.5 1.6 %collective-permute-done.1.refs_1_ = bf16[104,128]{1,0:T(8,128)(2,1)S(1)} collective-permute-done((bf16[104,128]{1,0:T(8,128)(2,1)S(1)}, bf16[104,128]{1,0:T(8,128)(2,1)S(1)}, u32[]{:S(2)}, u32[]{:S(2)}) %collective-permute-start.1) | collective-permute-done | bytes 26656 | tf_op jit(solution)/shard_map/ppermute | solution.py:510
  8.1 0.3 rows.1
  8.4 0.7 %collective-permute-start.4 = (bf16[352,128]{1,0:T(8,128)(2,1)S(1)}, bf16[352,128]{1,0:T(8,128)(2,1)S(1)}, u32[]{:S(2)}, u32[]{:S(2)}) collective-permute-start(bf16[352,128]{1,0:T(8,128)(2,1)S(1)} %get-tuple-element.32), channel_id=1, source_target_pairs={{0,0},{4,8},{8,4},{12,12},{1,1},{5,9},{9,5},{13,13},{2,2},{6,10},{... | collective-permute-start | bytes 270344 | tf_op jit(solution)/shard_map/ppermute | solution.py:584
  9.1 4.5 %collective-permute-start.3 = (bf16[352,128]{1,0:T(8,128)(2,1)S(1)}, bf16[352,128]{1,0:T(8,128)(2,1)S(1)}, u32[]{:S(2)}, u32[]{:S(2)}) collective-permute-start(bf16[352,128]{1,0:T(8,128)(2,1)S(1)} %get-tuple-element.31.refs_0_), channel_id=1, source_target_pairs={{0,4},{4,0},{8,12},{12,8},{1,5},{5,1},{9,13},{13,9},{2,6},{6,2},{1... | collective-permute-start | bytes 270344 | tf_op jit(solution)/shard_map/ppermute | solution.py:583
  13.5 0.7 %copy-done.1 = f32[8]{0:T(128)S(1)} copy-done((f32[8]{0:T(128)S(1)}, f32[8]{0:T(128)}, u32[]{:S(2)}) %copy-start.1) | copy-done | bytes 56
  14.2 0.2 bands.1
  14.4 1.6 %collective-permute-done.3.refs_1_ = bf16[352,128]{1,0:T(8,128)(2,1)S(1)} collective-permute-done((bf16[352,128]{1,0:T(8,128)(2,1)S(1)}, bf16[352,128]{1,0:T(8,128)(2,1)S(1)}, u32[]{:S(2)}, u32[]{:S(2)}) %collective-permute-start.3) | collective-permute-done | bytes 90144 | tf_op jit(solution)/shard_map/ppermute | solution.py:583
  16.0 2.8 %main.1 = (bf16[144,128]{1,0:T(8,128)(2,1)S(1)}, bf16[144,128]{1,0:T(8,128)(2,1)S(1)}, bf16[144,128]{1,0:T(8,128)(2,1)S(1)}, bf16[144,128]{1,0:T(8,128)(2,1)S(1)}) custom-call(bf16[352,128]{1,0:T(8,128)(2,1)S(1)} %get-tuple-element.31.refs_0_, bf16[352,128]{1,0:T(8,128)(2,1)S(1)} %collective-permute-done.3.refs_1_, ...), custom_call_target="tpu_custom_call" | custom-call | tf_op jit(solution)/shard_map/main/pallas_call | solution.py:55
  18.8 0.1 collective-permute-start.5
  18.9 1.0 %collective-permute-start.6 = (bf16[144,128]{1,0:T(8,128)(2,1)S(1)}, bf16[144,128]{1,0:T(8,128)(2,1)S(1)}, u32[]{:S(2)}, u32[]{:S(2)}) collective-permute-start(bf16[144,128]{1,0:T(8,128)(2,1)S(1)} %get-tuple-element.41), channel_id=1, source_target_pairs={{0,2},{1,3},{2,0},{3,1},{4,6},{5,7},{6,4},{7,5},{8,10},{9,11},{10,... | collective-permute-start | bytes 110600 | tf_op jit(solution)/shard_map/ppermute | solution.py:510
  19.9 0.9 %collective-permute-start.7 = (bf16[144,128]{1,0:T(8,128)(2,1)S(1)}, bf16[144,128]{1,0:T(8,128)(2,1)S(1)}, u32[]{:S(2)}, u32[]{:S(2)}) collective-permute-start(bf16[144,128]{1,0:T(8,128)(2,1)S(1)} %get-tuple-element.42), channel_id=1, source_target_pairs={{0,1},{1,0},{2,3},{3,2},{4,5},{5,4},{6,7},{7,6},{8,9},{9,8},{10,11... | collective-permute-start | bytes 110600 | tf_op jit(solution)/shard_map/ppermute | solution.py:510
  20.7 1.5 %collective-permute-done.5.refs_0_ = bf16[144,128]{1,0:T(8,128)(2,1)S(1)} collective-permute-done((bf16[144,128]{1,0:T(8,128)(2,1)S(1)}, bf16[144,128]{1,0:T(8,128)(2,1)S(1)}, u32[]{:S(2)}, u32[]{:S(2)}) %collective-permute-start.5) | collective-permute-done | bytes 36896 | tf_op jit(solution)/shard_map/ppermute | solution.py:510
  22.2 1.0 %collective-permute-done.6.refs_1_ = bf16[144,128]{1,0:T(8,128)(2,1)S(1)} collective-permute-done((bf16[144,128]{1,0:T(8,128)(2,1)S(1)}, bf16[144,128]{1,0:T(8,128)(2,1)S(1)}, u32[]{:S(2)}, u32[]{:S(2)}) %collective-permute-start.6) | collective-permute-done | bytes 36896 | tf_op jit(solution)/shard_map/ppermute | solution.py:510
  23.3 1.4 %collective-permute-start.10 = (f32[32,128]{1,0:T(8,128)S(1)}, f32[32,128]{1,0:T(8,128)S(1)}, u32[]{:S(2)}, u32[]{:S(2)}) collective-permute-start(f32[32,128]{1,0:T(8,128)S(1)} %sum.1.refs_0_), channel_id=1, source_target_pairs={{0,12},{4,8},{8,4},{12,0},{1,13},{5,9},{9,5},{13,1},{2,14},{6,10},... | collective-permute-start | bytes 49160 | tf_op jit(solution)/shard_map/ppermute | solution.py:612
  24.7 2.2 %collective-permute-start.9 = (f32[32,128]{1,0:T(8,128)S(1)}, f32[32,128]{1,0:T(8,128)S(1)}, u32[]{:S(2)}, u32[]{:S(2)}) collective-permute-start(f32[32,128]{1,0:T(8,128)S(1)} %sum.1.refs_0_), channel_id=1, source_target_pairs={{0,8},{4,12},{8,0},{12,4},{1,9},{5,13},{9,1},{13,5},{2,10},{6,14},... | collective-permute-start | bytes 49160 | tf_op jit(solution)/shard_map/ppermute | solution.py:612
  26.9 0.9 %collective-permute-start.8 = (f32[32,128]{1,0:T(8,128)S(1)}, f32[32,128]{1,0:T(8,128)S(1)}, u32[]{:S(2)}, u32[]{:S(2)}) collective-permute-start(f32[32,128]{1,0:T(8,128)S(1)} %sum.1.refs_0_), channel_id=1, source_target_pairs={{0,4},{4,0},{8,12},{12,8},{1,5},{5,1},{9,13},{13,9},{2,6},{6,2},{1... | collective-permute-start | bytes 49160 | tf_op jit(solution)/shard_map/ppermute | solution.py:612
  27.8 0.8 %join.1 = (bf16[8,4,4,256]{3,2,1,0:T(4,128)(2,1)}, f32[4,256]{1,0:T(4,128)}) custom-call(bf16[144,128]{1,0:T(8,128)(2,1)S(1)} %collective-permute-done.5.refs_0_, bf16[144,128]{1,0:T(8,128)(2,1)S(1)} %collective-permute-done.6.refs_1_, bf16[144,128]{1,0:T(8,128)(2,1)S(1)} %collective-permute-done.7.refs_2_, bf16[144,128]{1,0:T(8,128)(2,1)S(1)} %get-tuple-element.43.refs_3_), custom_call_target="tpu_custom_call" | custom-call | tf_op jit(solution)/shard_map/join/pallas_call | solution.py:55
  28.6 0.4 %collective-permute-done.10.refs_3_ = f32[32,128]{1,0:T(8,128)S(1)} collective-permute-done((f32[32,128]{1,0:T(8,128)S(1)}, f32[32,128]{1,0:T(8,128)S(1)}, u32[]{:S(2)}, u32[]{:S(2)}) %collective-permute-start.10) | collective-permute-done | bytes 16416 | tf_op jit(solution)/shard_map/ppermute | solution.py:612
  28.9 0.4 %collective-permute-done.9.refs_2_ = f32[32,128]{1,0:T(8,128)S(1)} collective-permute-done((f32[32,128]{1,0:T(8,128)S(1)}, f32[32,128]{1,0:T(8,128)S(1)}, u32[]{:S(2)}, u32[]{:S(2)}) %collective-permute-start.9) | collective-permute-done | bytes 16416 | tf_op jit(solution)/shard_map/ppermute | solution.py:612
  29.4 1.3 %collective-permute-done.8.refs_1_ = f32[32,128]{1,0:T(8,128)S(1)} collective-permute-done((f32[32,128]{1,0:T(8,128)S(1)}, f32[32,128]{1,0:T(8,128)S(1)}, u32[]{:S(2)}, u32[]{:S(2)}) %collective-permute-start.8) | collective-permute-done | bytes 16416 | tf_op jit(solution)/shard_map/ppermute | solution.py:612
  30.6 0.8 %finish.1 = (f32[3,3,3,8,8]{4,3,2,1,0:T(8,128)}, f32[1,8]{1,0:T(1,128)}, f32[3,3,3,8]{3,2,1,0:T(4,128)}) custom-call(f32[32,128]{1,0:T(8,128)S(1)} %sum.1.refs_0_, f32[32,128]{1,0:T(8,128)S(1)} %collective-permute-done.8.refs_1_, f32[32,128]{1,0:T(8,128)S(1)} %collective-permute-done.9.refs_2_, f32[32,128]{1,0:T(8,128)S(1)} %collective-permute-done.10.refs_3_), custom_call_target="tpu_custom_call" | custom-call | tf_op jit(solution)/shard_map/finish/pallas_call | solution.py:55
  (22 shorter events, 0.2 us)
Async XLA Ops:
  0.6 4.3 %copy-start.3 = (bf16[3,3,3,8]{3,2,1,0:T(4,128)(2,1)S(1)}, bf16[3,3,3,8]{3,2,1,0:T(4,128)(2,1)}, u32[]{:S(2)}) copy-start(bf16[3,3,3,8]{3,2,1,0:T(4,128)(2,1)} %param.9) | copy-start | bytes 1300
  1.8 4.7 %collective-permute-start = (bf16[104,128]{1,0:T(8,128)(2,1)S(1)}, bf16[104,128]{1,0:T(8,128)(2,1)S(1)}, u32[]{:S(2)}, u32[]{:S(2)}) collective-permute-start(bf16[104,128]{1,0:T(8,128)(2,1)S(1)} %get-tuple-element.27), channel_id=1, source_target_pairs={{0,3},{1,2},{2,1},{3,0},{4,7},{5,6},{6,5},{7,4},{8,11},{9,10},{10,... | collective-permute-start | bytes 79880 | tf_op jit(solution)/shard_map/ppermute | solution.py:510
  4.2 3.8 %collective-permute-start.1 = (bf16[104,128]{1,0:T(8,128)(2,1)S(1)}, bf16[104,128]{1,0:T(8,128)(2,1)S(1)}, u32[]{:S(2)}, u32[]{:S(2)}) collective-permute-start(bf16[104,128]{1,0:T(8,128)(2,1)S(1)} %get-tuple-element.28), channel_id=1, source_target_pairs={{0,2},{1,3},{2,0},{3,1},{4,6},{5,7},{6,4},{7,5},{8,10},{9,11},{10,... | collective-permute-start | bytes 79880 | tf_op jit(solution)/shard_map/ppermute | solution.py:510
  4.9 3.2 %collective-permute-start.2 = (bf16[104,128]{1,0:T(8,128)(2,1)S(1)}, bf16[104,128]{1,0:T(8,128)(2,1)S(1)}, u32[]{:S(2)}, u32[]{:S(2)}) collective-permute-start(bf16[104,128]{1,0:T(8,128)(2,1)S(1)} %get-tuple-element.29), channel_id=1, source_target_pairs={{0,1},{1,0},{2,3},{3,2},{4,5},{5,4},{6,7},{7,6},{8,9},{9,8},{10,11... | collective-permute-start | bytes 79880 | tf_op jit(solution)/shard_map/ppermute | solution.py:510
  4.9 0.8 %copy-start.2 = (bf16[3,3,3,8,8]{4,3,2,1,0:T(8,128)(2,1)S(1)}, bf16[3,3,3,8,8]{4,3,2,1,0:T(8,128)(2,1)}, u32[]{:S(2)}) copy-start(bf16[3,3,3,8,8]{4,3,2,1,0:T(8,128)(2,1)} %param.7) | copy-start | bytes 10372
  6.3 1.8 %copy-start = (f32[4,256]{1,0:T(4,128)S(1)}, f32[4,256]{1,0:T(4,128)}, u32[]{:S(2)}) copy-start(f32[4,256]{1,0:T(4,128)} %refs_4_.1) | copy-start | bytes 12292
  8.4 6.0 %collective-permute-start.4 = (bf16[352,128]{1,0:T(8,128)(2,1)S(1)}, bf16[352,128]{1,0:T(8,128)(2,1)S(1)}, u32[]{:S(2)}, u32[]{:S(2)}) collective-permute-start(bf16[352,128]{1,0:T(8,128)(2,1)S(1)} %get-tuple-element.32), channel_id=1, source_target_pairs={{0,0},{4,8},{8,4},{12,12},{1,1},{5,9},{9,5},{13,13},{2,2},{6,10},{... | collective-permute-start | bytes 270344 | tf_op jit(solution)/shard_map/ppermute | solution.py:584
  9.1 7.0 %collective-permute-start.3 = (bf16[352,128]{1,0:T(8,128)(2,1)S(1)}, bf16[352,128]{1,0:T(8,128)(2,1)S(1)}, u32[]{:S(2)}, u32[]{:S(2)}) collective-permute-start(bf16[352,128]{1,0:T(8,128)(2,1)S(1)} %get-tuple-element.31.refs_0_), channel_id=1, source_target_pairs={{0,4},{4,0},{8,12},{12,8},{1,5},{5,1},{9,13},{13,9},{2,6},{6,2},{1... | collective-permute-start | bytes 270344 | tf_op jit(solution)/shard_map/ppermute | solution.py:583
  13.5 0.7 %copy-start.1 = (f32[8]{0:T(128)S(1)}, f32[8]{0:T(128)}, u32[]{:S(2)}) copy-start(f32[8]{0:T(128)} %param.8) | copy-start | bytes 100
  18.8 3.4 %collective-permute-start.5 = (bf16[144,128]{1,0:T(8,128)(2,1)S(1)}, bf16[144,128]{1,0:T(8,128)(2,1)S(1)}, u32[]{:S(2)}, u32[]{:S(2)}) collective-permute-start(bf16[144,128]{1,0:T(8,128)(2,1)S(1)} %get-tuple-element.40), channel_id=1, source_target_pairs={{0,3},{1,2},{2,1},{3,0},{4,7},{5,6},{6,5},{7,4},{8,11},{9,10},{10,... | collective-permute-start | bytes 110600 | tf_op jit(solution)/shard_map/ppermute | solution.py:510
  18.9 4.4 %collective-permute-start.6 = (bf16[144,128]{1,0:T(8,128)(2,1)S(1)}, bf16[144,128]{1,0:T(8,128)(2,1)S(1)}, u32[]{:S(2)}, u32[]{:S(2)}) collective-permute-start(bf16[144,128]{1,0:T(8,128)(2,1)S(1)} %get-tuple-element.41), channel_id=1, source_target_pairs={{0,2},{1,3},{2,0},{3,1},{4,6},{5,7},{6,4},{7,5},{8,10},{9,11},{10,... | collective-permute-start | bytes 110600 | tf_op jit(solution)/shard_map/ppermute | solution.py:510
  19.9 3.4 %collective-permute-start.7 = (bf16[144,128]{1,0:T(8,128)(2,1)S(1)}, bf16[144,128]{1,0:T(8,128)(2,1)S(1)}, u32[]{:S(2)}, u32[]{:S(2)}) collective-permute-start(bf16[144,128]{1,0:T(8,128)(2,1)S(1)} %get-tuple-element.42), channel_id=1, source_target_pairs={{0,1},{1,0},{2,3},{3,2},{4,5},{5,4},{6,7},{7,6},{8,9},{9,8},{10,11... | collective-permute-start | bytes 110600 | tf_op jit(solution)/shard_map/ppermute | solution.py:510
  23.3 5.7 %collective-permute-start.10 = (f32[32,128]{1,0:T(8,128)S(1)}, f32[32,128]{1,0:T(8,128)S(1)}, u32[]{:S(2)}, u32[]{:S(2)}) collective-permute-start(f32[32,128]{1,0:T(8,128)S(1)} %sum.1.refs_0_), channel_id=1, source_target_pairs={{0,12},{4,8},{8,4},{12,0},{1,13},{5,9},{9,5},{13,1},{2,14},{6,10},... | collective-permute-start | bytes 49160 | tf_op jit(solution)/shard_map/ppermute | solution.py:612
  24.7 4.6 %collective-permute-start.9 = (f32[32,128]{1,0:T(8,128)S(1)}, f32[32,128]{1,0:T(8,128)S(1)}, u32[]{:S(2)}, u32[]{:S(2)}) collective-permute-start(f32[32,128]{1,0:T(8,128)S(1)} %sum.1.refs_0_), channel_id=1, source_target_pairs={{0,8},{4,12},{8,0},{12,4},{1,9},{5,13},{9,1},{13,5},{2,10},{6,14},... | collective-permute-start | bytes 49160 | tf_op jit(solution)/shard_map/ppermute | solution.py:612
  26.9 3.7 %collective-permute-start.8 = (f32[32,128]{1,0:T(8,128)S(1)}, f32[32,128]{1,0:T(8,128)S(1)}, u32[]{:S(2)}, u32[]{:S(2)}) collective-permute-start(f32[32,128]{1,0:T(8,128)S(1)} %sum.1.refs_0_), channel_id=1, source_target_pairs={{0,4},{4,0},{8,12},{12,8},{1,5},{5,1},{9,13},{13,9},{2,6},{6,2},{1... | collective-permute-start | bytes 49160 | tf_op jit(solution)/shard_map/ppermute | solution.py:612

commit v7 on v6

--- a/solution.py
+++ b/solution.py
@@ -372,51 +372,46 @@
         left1.append(jnp.concatenate(pieces, axis=0).astype(BF16))
 
     inner = (rows + 4) * chans
-    acc1 = None
-    acc2 = None
+    acc = None
     for p in range(0, count, 2):
-        rhs = []
+        far = []
         for q in range(2):
-            at = [(p + q + a) * xr + 2 * chans for a in range(3)]
-            rhs.append(jnp.concatenate([x_ref[k : k + inner] for k in at], axis=0))
-        part = dot_t(left1[p // 2], jnp.concatenate(rhs, axis=1))
-        acc1 = part if acc1 is None else acc1 + part
-        lhs = jnp.concatenate([left2[p], left2[p + 1]], axis=1)
-        part = dot_t(lhs, pair(h_ref, p, hr, 3 * hr))
-        acc2 = part if acc2 is None else acc2 + part
-
-    acc1 = jnp.concatenate([acc1, jnp.zeros((acc1.shape[0], -acc1.shape[1] % 128), F32)], axis=1)
-    acc2 = jnp.concatenate([acc2, jnp.zeros((acc2.shape[0], -acc2.shape[1] % 128), F32)], axis=1)
-    out1 = jnp.zeros((3 * chans, acc1.shape[1]), F32)
-    for r in range(rows):
-        out1 = out1 + left(acc1[3 * chans * r : 3 * chans * (r + 1)], chans * (r + 1))
-    row_in = lax.broadcasted_iota(jnp.int32, acc2.shape, 0) % lr
-    out2 = jnp.zeros(acc2.shape, F32)
-    for r in range(2, 2 + rows):
-        out2 = out2 + jnp.where(row_in == r, left(acc2, chans * r), 0.0)
-    out2 = jnp.concatenate(
-        [jnp.sum(out2[c * lr : (c + 1) * lr], axis=0, keepdims=True) for c in range(3)]
-        + [jnp.zeros((5, out2.shape[1]), F32)],
-        axis=0,
-    )
+            k = p + q
+            far.append(
+                jnp.concatenate(
+                    [x_ref[(k + a) * xr + 2 * chans : (k + a) * xr + 2 * chans + inner] for a in range(3)]
+                    + [h_ref[k * hr : (k + 3) * hr]],
+                    axis=0,
+                )
+            )
+        side = jnp.concatenate([left2[p], left2[p + 1]], axis=1)
+        side = jnp.concatenate([left1[p // 2], side, jnp.zeros((128 - 15 * chans, two), BF16)], axis=0)
+        part = dot_t(jnp.concatenate(far, axis=1), side)
+        acc = part if acc is None else acc + part
+
+    def turned(at, amount):
+        return pltpu.roll(acc[at : at + chans], amount % 128, 1)
+
     tap = 3 * chans
-
-    def packed(out, pitch):
-        lane_p = lax.broadcasted_iota(jnp.int32, (out.shape[0], lanes), 1)
-        total = jnp.zeros((out.shape[0], lanes), F32)
-        for a in range(3):
-            moved = left(out, a * (pitch - tap))[:, :lanes]
-            total = jnp.where((lane_p >= a * tap) & (lane_p < (a + 1) * tap), moved, total)
-        return total
-
+    blocks = [jnp.zeros((chans, 128), F32), jnp.zeros((chans, 128), F32)]
+    lane_p = lax.broadcasted_iota(jnp.int32, (chans, 128), 1)
+    for k in range(9):
+        a, b = k // 3, k % 3
+        to = tap * (k % 5)
+        value = sum(turned(a * inner + (r + b + 1) * chans, to - tap * r) for r in range(rows))
+        blocks[k // 5] = jnp.where((lane_p >= to) & (lane_p < to + tap), value, blocks[k // 5])
+        base = 3 * inner + a * hr
+        used = rows * tap
+        if k < 8:
+            value = sum(turned(base + (r + b) * chans, 96 + k - used - r) for r in range(2, 2 + rows))
+            blocks[1] = jnp.where((lane_p >= 96) & (lane_p < 120) & (lane_p % 8 == k), value, blocks[1])
+        else:
+            for c in range(3):
+                value = sum(turned(base + (r + b) * chans, 120 + c - used - lr * c - r) for r in range(2, 2 + rows))
+                blocks[0] = jnp.where(lane_p == 120 + c, value, blocks[0])
     bias_sum = jnp.sum(bias_sum, axis=1, keepdims=True)
-    sub = lax.broadcasted_iota(jnp.int32, (chans, lanes), 0)
-    lane_b = lax.broadcasted_iota(jnp.int32, (chans, lanes), 1)
-    bias_sum = jnp.sum(jnp.where(sub == lane_b, bias_sum, 0.0), axis=0, keepdims=True)
-    second = packed(out2, hr)
-    row_in = lax.broadcasted_iota(jnp.int32, second.shape, 0)
-    second = jnp.where(row_in == 3, bias_sum, second)
-    payload = jnp.concatenate([packed(out1, inner), second], axis=0)
+    blocks[1] = jnp.where(lane_p == 120, bias_sum, blocks[1])
+    payload = jnp.concatenate(blocks, axis=0)
     shown = jnp.concatenate([disparity[2 : 2 + rows]] * 2, axis=0)
     tail = jnp.concatenate(terms(payload, 2) + terms(shown, 2), axis=0).astype(BF16)
 
@@ -444,7 +439,7 @@
 
 def sum_body(chans, *refs):
     parts = refs[:-1]
-    k = 3 * chans + 8
+    k = 2 * chans
     sums = []
     for r in parts:
         n = r.shape[0] - 2 * k - 16
@@ -459,7 +454,7 @@
     grad_ref, disp_ref = refs[disp:]
     di = lax.axis_index("disp")
     n = planes * rows * chans
-    k = 2 * (3 * chans + 8)
+    k = 4 * chans
     total = None
     for s in range(disp):
         j = di ^ s
@@ -488,13 +483,15 @@
 def finish_body(chans, scale, *refs):
     gw_ref, gb_ref, gs_ref = refs[-3:]
     total = tree_sum([r[...] for r in refs[:-3]]) * scale
-    for a in range(3):
-        for b in range(3):
-            at = (a * 3 + b) * chans
-            for c in range(3):
-                gw_ref[a, b, c] = total[c * chans : (c + 1) * chans, at : at + chans]
-            gs_ref[a, b] = total[3 * chans : 3 * chans + 3, at : at + chans]
-    gb_ref[...] = total[3 * chans + 3 : 3 * chans + 4, :chans]
+    flat = [jnp.transpose(total[:chans]), jnp.transpose(total[chans:])]
+    for k in range(9):
+        a, b = k // 3, k % 3
+        for c in range(3):
+            at = 3 * chans * (k % 5) + chans * c
+            gw_ref[a, b, c] = flat[k // 5][at : at + chans]
+            at = 96 + k + 8 * c if k < 8 else 120 + c
+            gs_ref[a, b, c : c + 1] = flat[1 if k < 8 else 0][at : at + 1]
+    gb_ref[...] = flat[1][120:121]
 
 
 def flipped(body, count):
@@ -583,7 +580,7 @@
     z_one = lax.ppermute(send_one, "space", swap_pairs(space, 0))
     z_two = lax.ppermute(send_two, "space", swap_pairs(space, 1))
 
-    tail = 2 * (3 * chans + 8) + 16
+    tail = 4 * chans + 16
     backs = call(
         functools.partial(main_body, dims),
         "main",
@@ -604,7 +601,7 @@
     (pay,) = call(
         flipped(functools.partial(sum_body, chans), disp),
         "sum",
-        (((3 * chans + 8, lanes), F32, True),),
+        (((2 * chans, lanes), F32, True),),
         *backs[::-1],
     )
     stages = radix_stages(space)

time: 31.6 us -> 31.1 us (0.984)
  no operation moved by 1% of the time
where the time goes in v7:
time: 31.1 us; the launch traced here: 30.9 us
  starting transfers between devices  14.6 us (47%)
  waiting for transfers between devices  7.62 us (25%)
  Pallas kernels  5.73 us (18%)
  local copies, waits for them, and re-layouts  2.1 us (7%)
  between operations  0.79 us (3%)
    pallas_call x7, Pallas kernels, call(): pl.pallas_call(body, out_shape=tuple((pltpu.VMEM(shape, dtype) if inside...  5.73 us
    ppermute x6, starting transfers between devices, exchange(): lax.ppermute(sends[s], axis, [(i, i ^ s) for i in range(count)])  5.04 us
    ppermute x1, starting transfers between devices, shards(): z_one = lax.ppermute(send_one, 'space', swap_pairs(space, 0))  4.46 us
    ppermute x3, starting transfers between devices, shards(): lax.ppermute(pay, 'space', [(i, i ^ s) for i in range(space)])  4.45 us
    ppermute x6, waiting for transfers between devices, exchange(): lax.ppermute(sends[s], axis, [(i, i ^ s) for i in range(count)])  4.02 us
    ppermute x3, waiting for transfers between devices, shards(): lax.ppermute(pay, 'space', [(i, i ^ s) for i in range(space)])  1.97 us
    ppermute x1, waiting for transfers between devices, shards(): z_one = lax.ppermute(send_one, 'space', swap_pairs(space, 0))  1.63 us
    unnamed x11, local copies, waits for them, and re-layouts  1.42 us
  transfers between devices with their start and end apart: 11, of which 7 were waited for; matrix products, arithmetic and copies ran while one was open for 3% of the time, Pallas kernels for 3%

profile of v7, /device:TPU:0, one launch (start us, length us, event | category | flops | bytes accessed | tf_op | source)
XLA Modules:
  0.0 30.9 jit_solution(1772937206645549987)
XLA Ops:
  0.6 1.1 %split.1 = (bf16[104,128]{1,0:T(8,128)(2,1)S(1)}, bf16[104,128]{1,0:T(8,128)(2,1)S(1)}, bf16[104,128]{1,0:T(8,128)(2,1)S(1)}, bf16[104,128]{1,0:T(8,128)(2,1)S(1)}) custom-call(bf16[8,4,4,256]{3,2,1,0:T(4,128)(2,1)} %volume_ref.1, f32[4,4,256]{2,1,0:T(4,128)} %prior_ref.1), custom_call_target="tpu_custom_call" | custom-call | tf_op jit(solution)/shard_map/split/pallas_call | solution.py:55
  1.8 2.4 %collective-permute-start = (bf16[104,128]{1,0:T(8,128)(2,1)S(1)}, bf16[104,128]{1,0:T(8,128)(2,1)S(1)}, u32[]{:S(2)}, u32[]{:S(2)}) collective-permute-start(bf16[104,128]{1,0:T(8,128)(2,1)S(1)} %get-tuple-element.27), channel_id=1, source_target_pairs={{0,3},{1,2},{2,1},{3,0},{4,7},{5,6},{6,5},{7,4},{8,11},{9,10},{10,... | collective-permute-start | bytes 79880 | tf_op jit(solution)/shard_map/ppermute | solution.py:507
  4.2 0.6 %collective-permute-start.1 = (bf16[104,128]{1,0:T(8,128)(2,1)S(1)}, bf16[104,128]{1,0:T(8,128)(2,1)S(1)}, u32[]{:S(2)}, u32[]{:S(2)}) collective-permute-start(bf16[104,128]{1,0:T(8,128)(2,1)S(1)} %get-tuple-element.28), channel_id=1, source_target_pairs={{0,2},{1,3},{2,0},{3,1},{4,6},{5,7},{6,4},{7,5},{8,10},{9,11},{10,... | collective-permute-start | bytes 79880 | tf_op jit(solution)/shard_map/ppermute | solution.py:507
  4.9 0.0 collective-permute-start.2
  5.0 0.1 reshape.30
  5.1 0.1 copy.19
  5.1 0.6 %copy-done.2 = bf16[3,3,3,8,8]{4,3,2,1,0:T(8,128)(2,1)S(1)} copy-done((bf16[3,3,3,8,8]{4,3,2,1,0:T(8,128)(2,1)S(1)}, bf16[3,3,3,8,8]{4,3,2,1,0:T(8,128)(2,1)}, u32[]{:S(2)}) %copy-start.2) | copy-done | bytes 3480
  5.7 0.1 copy.22
  5.9 0.1 reshape.29
  6.1 0.1 reshape.26
  6.3 0.1 reshape.27
  6.5 1.6 %collective-permute-done.1.refs_1_ = bf16[104,128]{1,0:T(8,128)(2,1)S(1)} collective-permute-done((bf16[104,128]{1,0:T(8,128)(2,1)S(1)}, bf16[104,128]{1,0:T(8,128)(2,1)S(1)}, u32[]{:S(2)}, u32[]{:S(2)}) %collective-permute-start.1) | collective-permute-done | bytes 26656 | tf_op jit(solution)/shard_map/ppermute | solution.py:507
  8.1 0.3 rows.1
  8.4 0.7 %collective-permute-start.4 = (bf16[352,128]{1,0:T(8,128)(2,1)S(1)}, bf16[352,128]{1,0:T(8,128)(2,1)S(1)}, u32[]{:S(2)}, u32[]{:S(2)}) collective-permute-start(bf16[352,128]{1,0:T(8,128)(2,1)S(1)} %get-tuple-element.32), channel_id=1, source_target_pairs={{0,0},{4,8},{8,4},{12,12},{1,1},{5,9},{9,5},{13,13},{2,2},{6,10},{... | collective-permute-start | bytes 270344 | tf_op jit(solution)/shard_map/ppermute | solution.py:581
  9.1 4.5 %collective-permute-start.3 = (bf16[352,128]{1,0:T(8,128)(2,1)S(1)}, bf16[352,128]{1,0:T(8,128)(2,1)S(1)}, u32[]{:S(2)}, u32[]{:S(2)}) collective-permute-start(bf16[352,128]{1,0:T(8,128)(2,1)S(1)} %get-tuple-element.31.refs_0_), channel_id=1, source_target_pairs={{0,4},{4,0},{8,12},{12,8},{1,5},{5,1},{9,13},{13,9},{2,6},{6,2},{1... | collective-permute-start | bytes 270344 | tf_op jit(solution)/shard_map/ppermute | solution.py:580
  13.5 0.7 %copy-done.1 = f32[8]{0:T(128)S(1)} copy-done((f32[8]{0:T(128)S(1)}, f32[8]{0:T(128)}, u32[]{:S(2)}) %copy-start.1) | copy-done | bytes 56
  14.2 0.2 bands.1
  14.4 1.6 %collective-permute-done.3.refs_1_ = bf16[352,128]{1,0:T(8,128)(2,1)S(1)} collective-permute-done((bf16[352,128]{1,0:T(8,128)(2,1)S(1)}, bf16[352,128]{1,0:T(8,128)(2,1)S(1)}, u32[]{:S(2)}, u32[]{:S(2)}) %collective-permute-start.3) | collective-permute-done | bytes 90144 | tf_op jit(solution)/shard_map/ppermute | solution.py:580
  16.0 2.5 %main.1 = (bf16[112,128]{1,0:T(8,128)(2,1)S(1)}, bf16[112,128]{1,0:T(8,128)(2,1)S(1)}, bf16[112,128]{1,0:T(8,128)(2,1)S(1)}, bf16[112,128]{1,0:T(8,128)(2,1)S(1)}) custom-call(bf16[352,128]{1,0:T(8,128)(2,1)S(1)} %get-tuple-element.31.refs_0_, bf16[352,128]{1,0:T(8,128)(2,1)S(1)} %collective-permute-done.3.refs_1_, ...), custom_call_target="tpu_custom_call" | custom-call | tf_op jit(solution)/shard_map/main/pallas_call | solution.py:55
  18.5 0.1 collective-permute-start.5
  18.6 1.0 %collective-permute-start.6 = (bf16[112,128]{1,0:T(8,128)(2,1)S(1)}, bf16[112,128]{1,0:T(8,128)(2,1)S(1)}, u32[]{:S(2)}, u32[]{:S(2)}) collective-permute-start(bf16[112,128]{1,0:T(8,128)(2,1)S(1)} %get-tuple-element.41), channel_id=1, source_target_pairs={{0,2},{1,3},{2,0},{3,1},{4,6},{5,7},{6,4},{7,5},{8,10},{9,11},{10,... | collective-permute-start | bytes 86024 | tf_op jit(solution)/shard_map/ppermute | solution.py:507
  19.6 0.9 %collective-permute-start.7 = (bf16[112,128]{1,0:T(8,128)(2,1)S(1)}, bf16[112,128]{1,0:T(8,128)(2,1)S(1)}, u32[]{:S(2)}, u32[]{:S(2)}) collective-permute-start(bf16[112,128]{1,0:T(8,128)(2,1)S(1)} %get-tuple-element.42), channel_id=1, source_target_pairs={{0,1},{1,0},{2,3},{3,2},{4,5},{5,4},{6,7},{7,6},{8,9},{9,8},{10,11... | collective-permute-start | bytes 86024 | tf_op jit(solution)/shard_map/ppermute | solution.py:507
  20.5 1.4 %collective-permute-done.5.refs_0_ = bf16[112,128]{1,0:T(8,128)(2,1)S(1)} collective-permute-done((bf16[112,128]{1,0:T(8,128)(2,1)S(1)}, bf16[112,128]{1,0:T(8,128)(2,1)S(1)}, u32[]{:S(2)}, u32[]{:S(2)}) %collective-permute-start.5) | collective-permute-done | bytes 28704 | tf_op jit(solution)/shard_map/ppermute | solution.py:507
  21.9 0.9 %collective-permute-done.6.refs_1_ = bf16[112,128]{1,0:T(8,128)(2,1)S(1)} collective-permute-done((bf16[112,128]{1,0:T(8,128)(2,1)S(1)}, bf16[112,128]{1,0:T(8,128)(2,1)S(1)}, u32[]{:S(2)}, u32[]{:S(2)}) %collective-permute-start.6) | collective-permute-done | bytes 28704 | tf_op jit(solution)/shard_map/ppermute | solution.py:507
  22.9 1.4 %collective-permute-start.10 = (f32[16,128]{1,0:T(8,128)S(1)}, f32[16,128]{1,0:T(8,128)S(1)}, u32[]{:S(2)}, u32[]{:S(2)}) collective-permute-start(f32[16,128]{1,0:T(8,128)S(1)} %sum.1.refs_0_), channel_id=1, source_target_pairs={{0,12},{4,8},{8,4},{12,0},{1,13},{5,9},{9,5},{13,1},{2,14},{6,10},... | collective-permute-start | bytes 24584 | tf_op jit(solution)/shard_map/ppermute | solution.py:609
  24.3 2.2 %collective-permute-start.9 = (f32[16,128]{1,0:T(8,128)S(1)}, f32[16,128]{1,0:T(8,128)S(1)}, u32[]{:S(2)}, u32[]{:S(2)}) collective-permute-start(f32[16,128]{1,0:T(8,128)S(1)} %sum.1.refs_0_), channel_id=1, source_target_pairs={{0,8},{4,12},{8,0},{12,4},{1,9},{5,13},{9,1},{13,5},{2,10},{6,14},... | collective-permute-start | bytes 24584 | tf_op jit(solution)/shard_map/ppermute | solution.py:609
  26.4 0.9 %collective-permute-start.8 = (f32[16,128]{1,0:T(8,128)S(1)}, f32[16,128]{1,0:T(8,128)S(1)}, u32[]{:S(2)}, u32[]{:S(2)}) collective-permute-start(f32[16,128]{1,0:T(8,128)S(1)} %sum.1.refs_0_), channel_id=1, source_target_pairs={{0,4},{4,0},{8,12},{12,8},{1,5},{5,1},{9,13},{13,9},{2,6},{6,2},{1... | collective-permute-start | bytes 24584 | tf_op jit(solution)/shard_map/ppermute | solution.py:609
  27.3 0.8 %join.1 = (bf16[8,4,4,256]{3,2,1,0:T(4,128)(2,1)}, f32[4,256]{1,0:T(4,128)}) custom-call(bf16[112,128]{1,0:T(8,128)(2,1)S(1)} %collective-permute-done.5.refs_0_, bf16[112,128]{1,0:T(8,128)(2,1)S(1)} %collective-permute-done.6.refs_1_, bf16[112,128]{1,0:T(8,128)(2,1)S(1)} %collective-permute-done.7.refs_2_, bf16[112,128]{1,0:T(8,128)(2,1)S(1)} %get-tuple-element.43.refs_3_), custom_call_target="tpu_custom_call" | custom-call | tf_op jit(solution)/shard_map/join/pallas_call | solution.py:55
  28.1 0.2 collective-permute-done.10.refs_3_
  28.4 0.4 %collective-permute-done.9.refs_2_ = f32[16,128]{1,0:T(8,128)S(1)} collective-permute-done((f32[16,128]{1,0:T(8,128)S(1)}, f32[16,128]{1,0:T(8,128)S(1)}, u32[]{:S(2)}, u32[]{:S(2)}) %collective-permute-start.9) | collective-permute-done | bytes 8224 | tf_op jit(solution)/shard_map/ppermute | solution.py:609
  28.8 1.3 %collective-permute-done.8.refs_1_ = f32[16,128]{1,0:T(8,128)S(1)} collective-permute-done((f32[16,128]{1,0:T(8,128)S(1)}, f32[16,128]{1,0:T(8,128)S(1)}, u32[]{:S(2)}, u32[]{:S(2)}) %collective-permute-start.8) | collective-permute-done | bytes 8224 | tf_op jit(solution)/shard_map/ppermute | solution.py:609
  30.1 0.8 %finish.1 = (f32[3,3,3,8,8]{4,3,2,1,0:T(8,128)}, f32[1,8]{1,0:T(1,128)}, f32[3,3,3,8]{3,2,1,0:T(4,128)}) custom-call(f32[16,128]{1,0:T(8,128)S(1)} %sum.1.refs_0_, f32[16,128]{1,0:T(8,128)S(1)} %collective-permute-done.8.refs_1_, f32[16,128]{1,0:T(8,128)S(1)} %collective-permute-done.9.refs_2_, f32[16,128]{1,0:T(8,128)S(1)} %collective-permute-done.10.refs_3_), custom_call_target="tpu_custom_call" | custom-call | tf_op jit(solution)/shard_map/finish/pallas_call | solution.py:55
  (22 shorter events, 0.2 us)
Async XLA Ops:
  0.6 4.3 %copy-start.3 = (bf16[3,3,3,8]{3,2,1,0:T(4,128)(2,1)S(1)}, bf16[3,3,3,8]{3,2,1,0:T(4,128)(2,1)}, u32[]{:S(2)}) copy-start(bf16[3,3,3,8]{3,2,1,0:T(4,128)(2,1)} %param.9) | copy-start | bytes 1300
  1.8 4.7 %collective-permute-start = (bf16[104,128]{1,0:T(8,128)(2,1)S(1)}, bf16[104,128]{1,0:T(8,128)(2,1)S(1)}, u32[]{:S(2)}, u32[]{:S(2)}) collective-permute-start(bf16[104,128]{1,0:T(8,128)(2,1)S(1)} %get-tuple-element.27), channel_id=1, source_target_pairs={{0,3},{1,2},{2,1},{3,0},{4,7},{5,6},{6,5},{7,4},{8,11},{9,10},{10,... | collective-permute-start | bytes 79880 | tf_op jit(solution)/shard_map/ppermute | solution.py:507
  4.2 3.8 %collective-permute-start.1 = (bf16[104,128]{1,0:T(8,128)(2,1)S(1)}, bf16[104,128]{1,0:T(8,128)(2,1)S(1)}, u32[]{:S(2)}, u32[]{:S(2)}) collective-permute-start(bf16[104,128]{1,0:T(8,128)(2,1)S(1)} %get-tuple-element.28), channel_id=1, source_target_pairs={{0,2},{1,3},{2,0},{3,1},{4,6},{5,7},{6,4},{7,5},{8,10},{9,11},{10,... | collective-permute-start | bytes 79880 | tf_op jit(solution)/shard_map/ppermute | solution.py:507
  4.9 3.2 %collective-permute-start.2 = (bf16[104,128]{1,0:T(8,128)(2,1)S(1)}, bf16[104,128]{1,0:T(8,128)(2,1)S(1)}, u32[]{:S(2)}, u32[]{:S(2)}) collective-permute-start(bf16[104,128]{1,0:T(8,128)(2,1)S(1)} %get-tuple-element.29), channel_id=1, source_target_pairs={{0,1},{1,0},{2,3},{3,2},{4,5},{5,4},{6,7},{7,6},{8,9},{9,8},{10,11... | collective-permute-start | bytes 79880 | tf_op jit(solution)/shard_map/ppermute | solution.py:507
  4.9 0.8 %copy-start.2 = (bf16[3,3,3,8,8]{4,3,2,1,0:T(8,128)(2,1)S(1)}, bf16[3,3,3,8,8]{4,3,2,1,0:T(8,128)(2,1)}, u32[]{:S(2)}) copy-start(bf16[3,3,3,8,8]{4,3,2,1,0:T(8,128)(2,1)} %param.7) | copy-start | bytes 10372
  6.3 1.8 %copy-start = (f32[4,256]{1,0:T(4,128)S(1)}, f32[4,256]{1,0:T(4,128)}, u32[]{:S(2)}) copy-start(f32[4,256]{1,0:T(4,128)} %refs_4_.1) | copy-start | bytes 12292
  8.4 6.0 %collective-permute-start.4 = (bf16[352,128]{1,0:T(8,128)(2,1)S(1)}, bf16[352,128]{1,0:T(8,128)(2,1)S(1)}, u32[]{:S(2)}, u32[]{:S(2)}) collective-permute-start(bf16[352,128]{1,0:T(8,128)(2,1)S(1)} %get-tuple-element.32), channel_id=1, source_target_pairs={{0,0},{4,8},{8,4},{12,12},{1,1},{5,9},{9,5},{13,13},{2,2},{6,10},{... | collective-permute-start | bytes 270344 | tf_op jit(solution)/shard_map/ppermute | solution.py:581
  9.1 7.0 %collective-permute-start.3 = (bf16[352,128]{1,0:T(8,128)(2,1)S(1)}, bf16[352,128]{1,0:T(8,128)(2,1)S(1)}, u32[]{:S(2)}, u32[]{:S(2)}) collective-permute-start(bf16[352,128]{1,0:T(8,128)(2,1)S(1)} %get-tuple-element.31.refs_0_), channel_id=1, source_target_pairs={{0,4},{4,0},{8,12},{12,8},{1,5},{5,1},{9,13},{13,9},{2,6},{6,2},{1... | collective-permute-start | bytes 270344 | tf_op jit(solution)/shard_map/ppermute | solution.py:580
  13.5 0.7 %copy-start.1 = (f32[8]{0:T(128)S(1)}, f32[8]{0:T(128)}, u32[]{:S(2)}) copy-start(f32[8]{0:T(128)} %param.8) | copy-start | bytes 100
  18.5 3.4 %collective-permute-start.5 = (bf16[112,128]{1,0:T(8,128)(2,1)S(1)}, bf16[112,128]{1,0:T(8,128)(2,1)S(1)}, u32[]{:S(2)}, u32[]{:S(2)}) collective-permute-start(bf16[112,128]{1,0:T(8,128)(2,1)S(1)} %get-tuple-element.40), channel_id=1, source_target_pairs={{0,3},{1,2},{2,1},{3,0},{4,7},{5,6},{6,5},{7,4},{8,11},{9,10},{10,... | collective-permute-start | bytes 86024 | tf_op jit(solution)/shard_map/ppermute | solution.py:507
  18.6 4.2 %collective-permute-start.6 = (bf16[112,128]{1,0:T(8,128)(2,1)S(1)}, bf16[112,128]{1,0:T(8,128)(2,1)S(1)}, u32[]{:S(2)}, u32[]{:S(2)}) collective-permute-start(bf16[112,128]{1,0:T(8,128)(2,1)S(1)} %get-tuple-element.41), channel_id=1, source_target_pairs={{0,2},{1,3},{2,0},{3,1},{4,6},{5,7},{6,4},{7,5},{8,10},{9,11},{10,... | collective-permute-start | bytes 86024 | tf_op jit(solution)/shard_map/ppermute | solution.py:507
  19.6 3.2 %collective-permute-start.7 = (bf16[112,128]{1,0:T(8,128)(2,1)S(1)}, bf16[112,128]{1,0:T(8,128)(2,1)S(1)}, u32[]{:S(2)}, u32[]{:S(2)}) collective-permute-start(bf16[112,128]{1,0:T(8,128)(2,1)S(1)} %get-tuple-element.42), channel_id=1, source_target_pairs={{0,1},{1,0},{2,3},{3,2},{4,5},{5,4},{6,7},{7,6},{8,9},{9,8},{10,11... | collective-permute-start | bytes 86024 | tf_op jit(solution)/shard_map/ppermute | solution.py:507
  22.9 5.5 %collective-permute-start.10 = (f32[16,128]{1,0:T(8,128)S(1)}, f32[16,128]{1,0:T(8,128)S(1)}, u32[]{:S(2)}, u32[]{:S(2)}) collective-permute-start(f32[16,128]{1,0:T(8,128)S(1)} %sum.1.refs_0_), channel_id=1, source_target_pairs={{0,12},{4,8},{8,4},{12,0},{1,13},{5,9},{9,5},{13,1},{2,14},{6,10},... | collective-permute-start | bytes 24584 | tf_op jit(solution)/shard_map/ppermute | solution.py:609
  24.3 4.5 %collective-permute-start.9 = (f32[16,128]{1,0:T(8,128)S(1)}, f32[16,128]{1,0:T(8,128)S(1)}, u32[]{:S(2)}, u32[]{:S(2)}) collective-permute-start(f32[16,128]{1,0:T(8,128)S(1)} %sum.1.refs_0_), channel_id=1, source_target_pairs={{0,8},{4,12},{8,0},{12,4},{1,9},{5,13},{9,1},{13,5},{2,10},{6,14},... | collective-permute-start | bytes 24584 | tf_op jit(solution)/shard_map/ppermute | solution.py:609
  26.4 3.7 %collective-permute-start.8 = (f32[16,128]{1,0:T(8,128)S(1)}, f32[16,128]{1,0:T(8,128)S(1)}, u32[]{:S(2)}, u32[]{:S(2)}) collective-permute-start(f32[16,128]{1,0:T(8,128)S(1)} %sum.1.refs_0_), channel_id=1, source_target_pairs={{0,4},{4,0},{8,12},{12,8},{1,5},{5,1},{9,13},{13,9},{2,6},{6,2},{1... | collective-permute-start | bytes 24584 | tf_op jit(solution)/shard_map/ppermute | solution.py:609

commit v8 on v7

--- a/solution.py
+++ b/solution.py
@@ -149,15 +149,13 @@
 def rows_body(dims, *refs):
     planes, rows, chans, width, disp, space, cols, lanes = dims
     piece_refs = refs[:disp]
-    cot_in_ref, one_ref, two_ref, prior_ref, cot_ref, wide_ref, rest_ref = refs[disp:]
+    cot_in_ref, one_ref, two_ref, wide_ref, rest_ref = refs[disp:]
     di = lax.axis_index("disp")
     even = lax.axis_index("space") % 2 == 0
     n = planes * rows * chans
     half = n // 2
     group = 2 * planes
     cot = window(jnp.concatenate([cot_in_ref[...]] * 2, axis=0), di * cols - 4, lanes)[:rows]
-    cot_ref[...] = jnp.zeros(cot_ref.shape, F32)
-    cot_ref[2 : 2 + rows] = cot
     fine = []
     for s in range(disp):
         g = di ^ s
@@ -170,25 +168,50 @@
         value = value[8:]
         value = [unpack(value[: 3 * group], value[3 * group :], k) for k in range(6)]
         fine.append(value)
+    for out_ref, down in ((one_ref, even), (two_ref, jnp.logical_not(even))):
+
+        def put(h):
+            for s in range(disp):
+                at = pl.multiple_of((di ^ s) * 3 * group, 8)
+                wide_ref[pl.ds(at, 3 * group)] = jnp.concatenate(fine[s][3 * h : 3 * h + 3], axis=0)
+            for t, term in enumerate(terms(cot[2 * h : 2 * h + 2])):
+                at = disp * 3 * group + 2 * t
+                wide_ref[at : at + 2] = term
+            rest = disp * 3 * group + 6
+            wide_ref[rest:] = jnp.zeros((wide_ref.shape[0] - rest, lanes), F32)
+
+        pl.when(down)(functools.partial(put, 1))
+        pl.when(jnp.logical_not(down))(functools.partial(put, 0))
+        out_ref[disp * half :] = jnp.concatenate([rest_ref[...]] + pack(wide_ref[...]), axis=0).astype(BF16)
+
+
+def mine_body(dims, *refs):
+    planes, rows, chans, width, disp, space, cols, lanes = dims
+    piece_refs = refs[:disp]
+    cot_in_ref, x_ref, prior_ref, cot_ref = refs[disp:]
+    di = lax.axis_index("disp")
+    block = rows * chans
+    half = planes * block // 2
+    group = 2 * planes
+    prior_ref[...] = jnp.zeros(prior_ref.shape, F32)
+    cot_ref[...] = jnp.zeros(cot_ref.shape, F32)
+    cot = jnp.concatenate([cot_in_ref[...]] * 2, axis=0)
+    cot_ref[2 : 2 + rows] = window(cot, di * cols - 4, lanes)[:rows]
+    x_ref[:block] = jnp.zeros((block, lanes), BF16)
+    x_ref[x_ref.shape[0] - block :] = jnp.zeros((block, lanes), BF16)
+    for s in range(disp):
+        g = di ^ s
+        main = piece_refs[s][:half].astype(F32)
+        rest = piece_refs[s][half:].astype(F32)
+        for p in range(planes):
+            value = [unpack(main, rest[:8], p * rows + r) for r in range(rows)]
+            at = pl.multiple_of((g * planes + p + 1) * block, block)
+            x_ref[pl.ds(at, block)] = jnp.concatenate(value, axis=0).astype(BF16)
+        value = [unpack(rest[8 : 8 + 3 * group], rest[8 + 3 * group :], k) for k in range(6)]
         for h in range(2):
             prior = value[3 * h] + value[3 * h + 1] + value[3 * h + 2]
             for p in range(planes):
                 prior_ref[g * planes + p, 2 + 2 * h : 4 + 2 * h] = prior[2 * p : 2 * p + 2]
-    for out_ref, down in ((one_ref, even), (two_ref, jnp.logical_not(even))):
-
-        def put(h):
-            for s in range(disp):
-                at = pl.multiple_of((di ^ s) * 3 * group, 8)
-                wide_ref[pl.ds(at, 3 * group)] = jnp.concatenate(fine[s][3 * h : 3 * h + 3], axis=0)
-            for t, term in enumerate(terms(cot_ref[2 + 2 * h : 4 + 2 * h])):
-                at = disp * 3 * group + 2 * t
-                wide_ref[at : at + 2] = term
-            rest = disp * 3 * group + 6
-            wide_ref[rest:] = jnp.zeros((wide_ref.shape[0] - rest, lanes), F32)
-
-        pl.when(down)(functools.partial(put, 1))
-        pl.when(jnp.logical_not(down))(functools.partial(put, 0))
-        out_ref[disp * half :] = jnp.concatenate([rest_ref[...]] + pack(wide_ref[...]), axis=0).astype(BF16)
 
 
 def bands_body(dims, base1_ref, base2_ref, base3_ref, base4_ref, bias_ref, band1_ref, band2_ref, band3_ref, band4_ref, col_ref):
@@ -220,23 +243,22 @@
 
 def main_body(dims, *refs):
     planes, rows, chans, width, disp, space, cols, lanes = dims
-    own_ref, za_ref, zb_ref, prior_in_ref, cot_in_ref, band1_ref, band2_ref, band3_ref, band4_ref, col_ref = refs[:10]
+    xo_ref, za_ref, zb_ref, prior_in_ref, cot_in_ref, band1_ref, band2_ref, band3_ref, band4_ref, col_ref = refs[:10]
     back_refs = refs[10 : 10 + disp]
-    x_ref, h_ref, slope_ref, prior_ref, cot_ref, s_ref, pg_ref, v_ref = refs[10 + disp :]
+    xu_ref, xd_ref, h_ref, slope_ref, prior_ref, cot_ref, s_ref, pg_ref, v_ref = refs[10 + disp :]
     zi = lax.axis_index("space")
     di = lax.axis_index("disp")
     z_even = zi % 2 == 0
     count = planes * disp
     n = count * rows * chans
     block = rows * chans
-    xr = (rows + 8) * chans
     hr = (rows + 6) * chans
     gr = (rows + 2) * chans
     lr = rows + 4
     sr = 16
     two = 2 * lanes
 
-    def place_rows(src, row):
+    def place_rows(src, ref):
         main = src[: n // 2].astype(F32)
         rest = src[n // 2 : n // 2 + 8 * disp].astype(F32)
         side = planes * block // 2
@@ -246,31 +268,29 @@
             value = [
                 unpack(main[g * side : (g + 1) * side], rest[8 * g : 8 * g + 8], p * rows + r) for r in range(rows)
             ]
-            at = (k + 1) * xr + row * chans
-            x_ref[at : at + block] = jnp.concatenate(value, axis=0).astype(BF16)
-
-    x_ref[:xr] = jnp.zeros((xr, lanes), BF16)
-    x_ref[(count + 1) * xr :] = jnp.zeros((2 * xr, lanes), BF16)
+            ref[(k + 1) * block : (k + 2) * block] = jnp.concatenate(value, axis=0).astype(BF16)
+
+    for ref in (xu_ref, xd_ref):
+        ref[:block] = jnp.zeros((block, lanes), BF16)
+        ref[(count + 1) * block :] = jnp.zeros((block, lanes), BF16)
     h_ref[:hr] = jnp.zeros((hr, lanes), BF16)
-    h_ref[(count + 1) * hr :] = jnp.zeros((2 * hr, lanes), BF16)
+    h_ref[(count + 1) * hr :] = jnp.zeros((hr, lanes), BF16)
     s_ref[...] = jnp.zeros(s_ref.shape, BF16)
     pg_ref[:gr] = jnp.zeros((gr, lanes), BF16)
     pg_ref[(count + 1) * gr :] = jnp.zeros((gr, lanes), BF16)
-    place_rows(own_ref, 4)
     prior_ref[...] = prior_in_ref[...]
     cot_ref[...] = cot_in_ref[...]
     half = 2 * planes
 
-    def place(ok, first, one, other, row, at8):
+    def place(ok, first, one, other, ref, at8):
         def put(src):
             if src is None:
+                ref[...] = jnp.zeros(ref.shape, BF16)
                 for k in range(count):
-                    at = (k + 1) * xr + row * chans
-                    x_ref[at : at + 4 * chans] = jnp.zeros((4 * chans, lanes), BF16)
                     prior_ref[k, at8 : at8 + 2] = jnp.zeros((2, lanes), F32)
                 cot_ref[at8 : at8 + 2] = jnp.zeros((2, lanes), F32)
                 return
-            place_rows(src, row)
+            place_rows(src, ref)
             extra = src[n // 2 + 8 * disp :].astype(F32)
             used = -(-(3 * half * disp + 6) // 16) * 16
             value = [unpack(extra[: used // 2], extra[used // 2 :], k) for k in range(3 * disp + 1)]
@@ -285,8 +305,8 @@
         pl.when(ok & jnp.logical_not(first))(lambda: put(other))
         pl.when(jnp.logical_not(ok))(lambda: put(None))
 
-    place(zi > 0, z_even, zb_ref, za_ref, 0, 0)
-    place(zi < space - 1, z_even, za_ref, zb_ref, 4 + rows, 2 + rows)
+    place(zi > 0, z_even, zb_ref, za_ref, xu_ref, 0)
+    place(zi < space - 1, z_even, za_ref, zb_ref, xd_ref, 2 + rows)
 
     def pair(ref, p, size, taken):
         return jnp.concatenate([ref[p * size : p * size + taken], ref[(p + 1) * size : (p + 1) * size + taken]], axis=1)
@@ -298,16 +318,15 @@
     band1 = band1_ref[...]
     bias = col_ref[...]
     yr = (rows + 2) * chans
-    wr = (rows + 4) * chans
     for p in range(0, count, 2):
         pre = []
-        for at in (0, 4 * chans):
-            rhs = [
-                jnp.concatenate(
-                    [x_ref[(p + q + a) * xr + at : (p + q + a) * xr + at + wr] for a in range(3)], axis=0
-                )
-                for q in range(2)
-            ]
+        for at, (near, far) in ((0, (xu_ref, xo_ref)), (4 * chans, (xo_ref, xd_ref))):
+            rhs = []
+            for q in range(2):
+                parts = []
+                for k in range(p + q, p + q + 3):
+                    parts += [near[k * block : (k + 1) * block], far[k * block : (k + 1) * block]]
+                rhs.append(jnp.concatenate(parts, axis=0))
             y = dot(band1, jnp.concatenate(rhs, axis=1))
             skip = at // 2
             y = [y[c * yr + skip : (c + 1) * yr] for c in range(3)]
@@ -377,13 +396,14 @@
         far = []
         for q in range(2):
             k = p + q
-            far.append(
-                jnp.concatenate(
-                    [x_ref[(k + a) * xr + 2 * chans : (k + a) * xr + 2 * chans + inner] for a in range(3)]
-                    + [h_ref[k * hr : (k + 3) * hr]],
-                    axis=0,
-                )
-            )
+            parts = []
+            for at in range(k * block, (k + 3) * block, block):
+                parts += [
+                    xu_ref[at + 2 * chans : at + block],
+                    xo_ref[at : at + block],
+                    xd_ref[at : at + block - 2 * chans],
+                ]
+            far.append(jnp.concatenate(parts + [h_ref[k * hr : (k + 3) * hr]], axis=0))
         side = jnp.concatenate([left2[p], left2[p + 1]], axis=1)
         side = jnp.concatenate([left1[p // 2], side, jnp.zeros((128 - 15 * chans, two), BF16)], axis=0)
         part = dot_t(jnp.concatenate(far, axis=1), side)
@@ -533,7 +553,6 @@
     )
     pieces = exchange(sends, "disp")
 
-    xr = rows + 8
     hr = rows + 6
     base1 = jnp.transpose(w_first, (2, 3, 0, 1, 4)).astype(F32)
     base1 = jnp.pad(base1, ((0, 0), (0, 0), (0, 0), (0, rows + 1), (0, 0)))
@@ -565,17 +584,22 @@
 
     extra = -(-(6 * count + 6) // 16) * 16
     sent = (n // 2 + 8) * disp + extra // 2 + 8 * -(-extra // 128)
-    send_one, send_two, prior, cot = call(
+    send_one, send_two = call(
         flipped(functools.partial(rows_body, dims), disp),
         "rows",
+        (((sent, lanes), BF16, True), ((sent, lanes), BF16, True)),
+        *pieces[::-1], cotangent,
+        scratch=[pltpu.VMEM((extra, lanes), F32), pltpu.VMEM((8 * disp, lanes), F32)],
+    )
+    mine = call(
+        flipped(functools.partial(mine_body, dims), disp),
+        "mine",
         (
-            ((sent, lanes), BF16, True),
-            ((sent, lanes), BF16, True),
+            (((count + 2) * rows * chans, lanes), BF16, True),
             ((count, rows + 4, lanes), F32, True),
             ((rows + 4, lanes), F32, True),
         ),
         *pieces[::-1], cotangent,
-        scratch=[pltpu.VMEM((extra, lanes), F32), pltpu.VMEM((8 * disp, lanes), F32)],
     )
     z_one = lax.ppermute(send_one, "space", swap_pairs(space, 0))
     z_two = lax.ppermute(send_two, "space", swap_pairs(space, 1))
@@ -585,10 +609,11 @@
         functools.partial(main_body, dims),
         "main",
         [((n // 2 + tail, lanes), BF16, True)] * disp,
-        send_one, z_one, z_two, prior, cot, *bands,
+        mine[0], z_one, z_two, *mine[1:], *bands,
         scratch=[
-            pltpu.VMEM(((count + 3) * xr * chans, lanes), BF16),
-            pltpu.VMEM(((count + 3) * hr * chans, lanes), BF16),
+            pltpu.VMEM(((count + 2) * rows * chans, lanes), BF16),
+            pltpu.VMEM(((count + 2) * rows * chans, lanes), BF16),
+            pltpu.VMEM(((count + 2) * hr * chans, lanes), BF16),
             pltpu.VMEM((count, (rows + 2) * chans, lanes), F32),
             pltpu.VMEM((count, rows + 4, lanes), F32),
             pltpu.VMEM((rows + 4, lanes), F32),

time: 31.1 us -> 30.6 us (0.984)
  starting transfers between devices: 14.6 us -> 14 us
    ppermute x1, starting transfers between devices: 4.46 us -> 1.64 us  [shards(): z_one = lax.ppermute(send_one, 'space', swap_pairs(space, 0))]
    ppermute x3, starting transfers between devices: 4.45 us -> 6.71 us  [shards(): lax.ppermute(pay, 'space', [(i, i ^ s) for i in range(space)])]
    ppermute x3, waiting for transfers between devices: 1.97 us -> 2.37 us  [shards(): lax.ppermute(pay, 'space', [(i, i ^ s) for i in range(space)])]
    ppermute x1, waiting for transfers between devices: 1.63 us -> 1.26 us  [shards(): z_one = lax.ppermute(send_one, 'space', swap_pairs(space, 0))]
    pallas_call x7 -> x8, Pallas kernels: 5.73 us -> 5.79 us  [call(): pl.pallas_call(body, out_shape=tuple((pltpu.VMEM(shape, dtype) if inside...]
  transfers between devices with their start and end apart: 11 -> 11, of which waited for: 7 -> 6; matrix products, arithmetic and copies ran while one was open for 3% -> 3% of each run, Pallas kernels for 3% -> 4%
where the time goes in v8:
time: 30.6 us; the launch traced here: 30.4 us
  starting transfers between devices  14 us (46%)
  waiting for transfers between devices  7.63 us (25%)
  Pallas kernels  5.79 us (19%)
  local copies, waits for them, and re-layouts  2.1 us (7%)
  between operations  0.8 us (3%)
    ppermute x3, starting transfers between devices, shards(): lax.ppermute(pay, 'space', [(i, i ^ s) for i in range(space)])  6.71 us
    pallas_call x8, Pallas kernels, call(): pl.pallas_call(body, out_shape=tuple((pltpu.VMEM(shape, dtype) if inside...  5.79 us
    ppermute x6, starting transfers between devices, exchange(): lax.ppermute(sends[s], axis, [(i, i ^ s) for i in range(count)])  5.04 us
    ppermute x6, waiting for transfers between devices, exchange(): lax.ppermute(sends[s], axis, [(i, i ^ s) for i in range(count)])  4 us
    ppermute x3, waiting for transfers between devices, shards(): lax.ppermute(pay, 'space', [(i, i ^ s) for i in range(space)])  2.37 us
    ppermute x1, starting transfers between devices, shards(): z_one = lax.ppermute(send_one, 'space', swap_pairs(space, 0))  1.64 us
    unnamed x11, local copies, waits for them, and re-layouts  1.41 us
    ppermute x1, waiting for transfers between devices, shards(): z_one = lax.ppermute(send_one, 'space', swap_pairs(space, 0))  1.26 us
  transfers between devices with their start and end apart: 11, of which 6 were waited for; matrix products, arithmetic and copies ran while one was open for 3% of the time, Pallas kernels for 4%

profile of v8, /device:TPU:0, one launch (start us, length us, event | category | flops | bytes accessed | tf_op | source)
XLA Modules:
  0.0 30.4 jit_solution(5139433384882603297)
XLA Ops:
  0.6 1.1 %split.1 = (bf16[104,128]{1,0:T(8,128)(2,1)S(1)}, bf16[104,128]{1,0:T(8,128)(2,1)S(1)}, bf16[104,128]{1,0:T(8,128)(2,1)S(1)}, bf16[104,128]{1,0:T(8,128)(2,1)S(1)}) custom-call(bf16[8,4,4,256]{3,2,1,0:T(4,128)(2,1)} %volume_ref.1, f32[4,4,256]{2,1,0:T(4,128)} %prior_ref.1), custom_call_target="tpu_custom_call" | custom-call | tf_op jit(solution)/shard_map/split/pallas_call | solution.py:55
  1.8 2.4 %collective-permute-start = (bf16[104,128]{1,0:T(8,128)(2,1)S(1)}, bf16[104,128]{1,0:T(8,128)(2,1)S(1)}, u32[]{:S(2)}, u32[]{:S(2)}) collective-permute-start(bf16[104,128]{1,0:T(8,128)(2,1)S(1)} %get-tuple-element.28), channel_id=1, source_target_pairs={{0,3},{1,2},{2,1},{3,0},{4,7},{5,6},{6,5},{7,4},{8,11},{9,10},{10,... | collective-permute-start | bytes 79880 | tf_op jit(solution)/shard_map/ppermute | solution.py:527
  4.2 0.6 %collective-permute-start.1 = (bf16[104,128]{1,0:T(8,128)(2,1)S(1)}, bf16[104,128]{1,0:T(8,128)(2,1)S(1)}, u32[]{:S(2)}, u32[]{:S(2)}) collective-permute-start(bf16[104,128]{1,0:T(8,128)(2,1)S(1)} %get-tuple-element.29), channel_id=1, source_target_pairs={{0,2},{1,3},{2,0},{3,1},{4,6},{5,7},{6,4},{7,5},{8,10},{9,11},{10,... | collective-permute-start | bytes 79880 | tf_op jit(solution)/shard_map/ppermute | solution.py:527
  4.9 0.0 collective-permute-start.2
  5.0 0.1 reshape.30
  5.1 0.1 copy.19
  5.1 0.6 %copy-done.2 = bf16[3,3,3,8,8]{4,3,2,1,0:T(8,128)(2,1)S(1)} copy-done((bf16[3,3,3,8,8]{4,3,2,1,0:T(8,128)(2,1)S(1)}, bf16[3,3,3,8,8]{4,3,2,1,0:T(8,128)(2,1)}, u32[]{:S(2)}) %copy-start.2) | copy-done | bytes 3480
  5.7 0.1 copy.22
  5.9 0.1 reshape.29
  6.1 0.1 reshape.26
  6.3 0.1 reshape.27
  6.5 1.6 %collective-permute-done.1.refs_1_ = bf16[104,128]{1,0:T(8,128)(2,1)S(1)} collective-permute-done((bf16[104,128]{1,0:T(8,128)(2,1)S(1)}, bf16[104,128]{1,0:T(8,128)(2,1)S(1)}, u32[]{:S(2)}, u32[]{:S(2)}) %collective-permute-start.1) | collective-permute-done | bytes 26656 | tf_op jit(solution)/shard_map/ppermute | solution.py:527
  8.1 0.3 %rows.1 = (bf16[352,128]{1,0:T(8,128)(2,1)S(1)}, bf16[352,128]{1,0:T(8,128)(2,1)S(1)}) custom-call(bf16[104,128]{1,0:T(8,128)(2,1)S(1)} %collective-permute-done.refs_0_, bf16[104,128]{1,0:T(8,128)(2,1)S(1)} %collective-permute-done.1.refs_1_, bf16[104,128]{1,0:T(8,128)(2,1)S(1)} %collective-permute-done.2.refs_2_, ...), custom_call_target="tpu_custom_call" | custom-call | tf_op jit(solution)/shard_map/rows/pallas_call | solution.py:55
  8.4 1.6 %collective-permute-start.3 = (bf16[352,128]{1,0:T(8,128)(2,1)S(1)}, bf16[352,128]{1,0:T(8,128)(2,1)S(1)}, u32[]{:S(2)}, u32[]{:S(2)}) collective-permute-start(bf16[352,128]{1,0:T(8,128)(2,1)S(1)} %get-tuple-element.33), channel_id=1, source_target_pairs={{0,4},{4,0},{8,12},{12,8},{1,5},{5,1},{9,13},{13,9},{2,6},{6,2},{1... | collective-permute-start | bytes 270344 | tf_op jit(solution)/shard_map/ppermute | solution.py:604
  10.0 0.7 %collective-permute-start.4 = (bf16[352,128]{1,0:T(8,128)(2,1)S(1)}, bf16[352,128]{1,0:T(8,128)(2,1)S(1)}, u32[]{:S(2)}, u32[]{:S(2)}) collective-permute-start(bf16[352,128]{1,0:T(8,128)(2,1)S(1)} %get-tuple-element.34), channel_id=1, source_target_pairs={{0,0},{4,8},{8,4},{12,12},{1,1},{5,9},{9,5},{13,13},{2,2},{6,10},{... | collective-permute-start | bytes 270344 | tf_op jit(solution)/shard_map/ppermute | solution.py:605
  10.7 0.6 %copy-done.1 = f32[8]{0:T(128)S(1)} copy-done((f32[8]{0:T(128)S(1)}, f32[8]{0:T(128)}, u32[]{:S(2)}) %copy-start.1) | copy-done | bytes 56
  11.4 0.2 bands.1
  11.6 0.1 mine.1
  11.7 1.3 %collective-permute-done.3.refs_1_ = bf16[352,128]{1,0:T(8,128)(2,1)S(1)} collective-permute-done((bf16[352,128]{1,0:T(8,128)(2,1)S(1)}, bf16[352,128]{1,0:T(8,128)(2,1)S(1)}, u32[]{:S(2)}, u32[]{:S(2)}) %collective-permute-start.3) | collective-permute-done | bytes 90144 | tf_op jit(solution)/shard_map/ppermute | solution.py:604
  13.0 2.4 %main.1 = (bf16[112,128]{1,0:T(8,128)(2,1)S(1)}, bf16[112,128]{1,0:T(8,128)(2,1)S(1)}, bf16[112,128]{1,0:T(8,128)(2,1)S(1)}, bf16[112,128]{1,0:T(8,128)(2,1)S(1)}) custom-call(bf16[576,128]{1,0:T(8,128)(2,1)S(1)} %get-tuple-element.32.refs_0_, bf16[352,128]{1,0:T(8,128)(2,1)S(1)} %collective-permute-done.3.refs_1_, ...), custom_call_target="tpu_custom_call" | custom-call | tf_op jit(solution)/shard_map/main/pallas_call | solution.py:55
  15.4 0.1 collective-permute-start.5
  15.5 1.0 %collective-permute-start.6 = (bf16[112,128]{1,0:T(8,128)(2,1)S(1)}, bf16[112,128]{1,0:T(8,128)(2,1)S(1)}, u32[]{:S(2)}, u32[]{:S(2)}) collective-permute-start(bf16[112,128]{1,0:T(8,128)(2,1)S(1)} %get-tuple-element.43), channel_id=1, source_target_pairs={{0,2},{1,3},{2,0},{3,1},{4,6},{5,7},{6,4},{7,5},{8,10},{9,11},{10,... | collective-permute-start | bytes 86024 | tf_op jit(solution)/shard_map/ppermute | solution.py:527
  16.5 0.9 %collective-permute-start.7 = (bf16[112,128]{1,0:T(8,128)(2,1)S(1)}, bf16[112,128]{1,0:T(8,128)(2,1)S(1)}, u32[]{:S(2)}, u32[]{:S(2)}) collective-permute-start(bf16[112,128]{1,0:T(8,128)(2,1)S(1)} %get-tuple-element.44), channel_id=1, source_target_pairs={{0,1},{1,0},{2,3},{3,2},{4,5},{5,4},{6,7},{7,6},{8,9},{9,8},{10,11... | collective-permute-start | bytes 86024 | tf_op jit(solution)/shard_map/ppermute | solution.py:527
  17.3 1.4 %collective-permute-done.5.refs_0_ = bf16[112,128]{1,0:T(8,128)(2,1)S(1)} collective-permute-done((bf16[112,128]{1,0:T(8,128)(2,1)S(1)}, bf16[112,128]{1,0:T(8,128)(2,1)S(1)}, u32[]{:S(2)}, u32[]{:S(2)}) %collective-permute-start.5) | collective-permute-done | bytes 28704 | tf_op jit(solution)/shard_map/ppermute | solution.py:527
  18.8 0.9 %collective-permute-done.6.refs_1_ = bf16[112,128]{1,0:T(8,128)(2,1)S(1)} collective-permute-done((bf16[112,128]{1,0:T(8,128)(2,1)S(1)}, bf16[112,128]{1,0:T(8,128)(2,1)S(1)}, u32[]{:S(2)}, u32[]{:S(2)}) %collective-permute-start.6) | collective-permute-done | bytes 28704 | tf_op jit(solution)/shard_map/ppermute | solution.py:527
  19.7 3.7 %collective-permute-start.10 = (f32[16,128]{1,0:T(8,128)S(1)}, f32[16,128]{1,0:T(8,128)S(1)}, u32[]{:S(2)}, u32[]{:S(2)}) collective-permute-start(f32[16,128]{1,0:T(8,128)S(1)} %sum.1.refs_0_), channel_id=1, source_target_pairs={{0,12},{4,8},{8,4},{12,0},{1,13},{5,9},{9,5},{13,1},{2,14},{6,10},... | collective-permute-start | bytes 24584 | tf_op jit(solution)/shard_map/ppermute | solution.py:634
  23.4 2.6 %collective-permute-start.9 = (f32[16,128]{1,0:T(8,128)S(1)}, f32[16,128]{1,0:T(8,128)S(1)}, u32[]{:S(2)}, u32[]{:S(2)}) collective-permute-start(f32[16,128]{1,0:T(8,128)S(1)} %sum.1.refs_0_), channel_id=1, source_target_pairs={{0,8},{4,12},{8,0},{12,4},{1,9},{5,13},{9,1},{13,5},{2,10},{6,14},... | collective-permute-start | bytes 24584 | tf_op jit(solution)/shard_map/ppermute | solution.py:634
  25.9 0.5 %collective-permute-start.8 = (f32[16,128]{1,0:T(8,128)S(1)}, f32[16,128]{1,0:T(8,128)S(1)}, u32[]{:S(2)}, u32[]{:S(2)}) collective-permute-start(f32[16,128]{1,0:T(8,128)S(1)} %sum.1.refs_0_), channel_id=1, source_target_pairs={{0,4},{4,0},{8,12},{12,8},{1,5},{5,1},{9,13},{13,9},{2,6},{6,2},{1... | collective-permute-start | bytes 24584 | tf_op jit(solution)/shard_map/ppermute | solution.py:634
  26.4 0.8 %join.1 = (bf16[8,4,4,256]{3,2,1,0:T(4,128)(2,1)}, f32[4,256]{1,0:T(4,128)}) custom-call(bf16[112,128]{1,0:T(8,128)(2,1)S(1)} %collective-permute-done.5.refs_0_, bf16[112,128]{1,0:T(8,128)(2,1)S(1)} %collective-permute-done.6.refs_1_, bf16[112,128]{1,0:T(8,128)(2,1)S(1)} %collective-permute-done.7.refs_2_, bf16[112,128]{1,0:T(8,128)(2,1)S(1)} %get-tuple-element.45.refs_3_), custom_call_target="tpu_custom_call" | custom-call | tf_op jit(solution)/shard_map/join/pallas_call | solution.py:55
  27.2 0.7 %collective-permute-done.9.refs_2_ = f32[16,128]{1,0:T(8,128)S(1)} collective-permute-done((f32[16,128]{1,0:T(8,128)S(1)}, f32[16,128]{1,0:T(8,128)S(1)}, u32[]{:S(2)}, u32[]{:S(2)}) %collective-permute-start.9) | collective-permute-done | bytes 8224 | tf_op jit(solution)/shard_map/ppermute | solution.py:634
  27.9 1.7 %collective-permute-done.8.refs_1_ = f32[16,128]{1,0:T(8,128)S(1)} collective-permute-done((f32[16,128]{1,0:T(8,128)S(1)}, f32[16,128]{1,0:T(8,128)S(1)}, u32[]{:S(2)}, u32[]{:S(2)}) %collective-permute-start.8) | collective-permute-done | bytes 8224 | tf_op jit(solution)/shard_map/ppermute | solution.py:634
  29.6 0.8 %finish.1 = (f32[3,3,3,8,8]{4,3,2,1,0:T(8,128)}, f32[1,8]{1,0:T(1,128)}, f32[3,3,3,8]{3,2,1,0:T(4,128)}) custom-call(f32[16,128]{1,0:T(8,128)S(1)} %sum.1.refs_0_, f32[16,128]{1,0:T(8,128)S(1)} %collective-permute-done.8.refs_1_, f32[16,128]{1,0:T(8,128)S(1)} %collective-permute-done.9.refs_2_, f32[16,128]{1,0:T(8,128)S(1)} %collective-permute-done.10.refs_3_), custom_call_target="tpu_custom_call" | custom-call | tf_op jit(solution)/shard_map/finish/pallas_call | solution.py:55
  (23 shorter events, 0.2 us)
Async XLA Ops:
  0.6 4.3 %copy-start.3 = (bf16[3,3,3,8]{3,2,1,0:T(4,128)(2,1)S(1)}, bf16[3,3,3,8]{3,2,1,0:T(4,128)(2,1)}, u32[]{:S(2)}) copy-start(bf16[3,3,3,8]{3,2,1,0:T(4,128)(2,1)} %param.9) | copy-start | bytes 1300
  1.8 4.7 %collective-permute-start = (bf16[104,128]{1,0:T(8,128)(2,1)S(1)}, bf16[104,128]{1,0:T(8,128)(2,1)S(1)}, u32[]{:S(2)}, u32[]{:S(2)}) collective-permute-start(bf16[104,128]{1,0:T(8,128)(2,1)S(1)} %get-tuple-element.28), channel_id=1, source_target_pairs={{0,3},{1,2},{2,1},{3,0},{4,7},{5,6},{6,5},{7,4},{8,11},{9,10},{10,... | collective-permute-start | bytes 79880 | tf_op jit(solution)/shard_map/ppermute | solution.py:527
  4.2 3.8 %collective-permute-start.1 = (bf16[104,128]{1,0:T(8,128)(2,1)S(1)}, bf16[104,128]{1,0:T(8,128)(2,1)S(1)}, u32[]{:S(2)}, u32[]{:S(2)}) collective-permute-start(bf16[104,128]{1,0:T(8,128)(2,1)S(1)} %get-tuple-element.29), channel_id=1, source_target_pairs={{0,2},{1,3},{2,0},{3,1},{4,6},{5,7},{6,4},{7,5},{8,10},{9,11},{10,... | collective-permute-start | bytes 79880 | tf_op jit(solution)/shard_map/ppermute | solution.py:527
  4.9 3.2 %collective-permute-start.2 = (bf16[104,128]{1,0:T(8,128)(2,1)S(1)}, bf16[104,128]{1,0:T(8,128)(2,1)S(1)}, u32[]{:S(2)}, u32[]{:S(2)}) collective-permute-start(bf16[104,128]{1,0:T(8,128)(2,1)S(1)} %get-tuple-element.30), channel_id=1, source_target_pairs={{0,1},{1,0},{2,3},{3,2},{4,5},{5,4},{6,7},{7,6},{8,9},{9,8},{10,11... | collective-permute-start | bytes 79880 | tf_op jit(solution)/shard_map/ppermute | solution.py:527
  4.9 0.8 %copy-start.2 = (bf16[3,3,3,8,8]{4,3,2,1,0:T(8,128)(2,1)S(1)}, bf16[3,3,3,8,8]{4,3,2,1,0:T(8,128)(2,1)}, u32[]{:S(2)}) copy-start(bf16[3,3,3,8,8]{4,3,2,1,0:T(8,128)(2,1)} %param.7) | copy-start | bytes 10372
  6.3 1.8 %copy-start = (f32[4,256]{1,0:T(4,128)S(1)}, f32[4,256]{1,0:T(4,128)}, u32[]{:S(2)}) copy-start(f32[4,256]{1,0:T(4,128)} %refs_4_.3) | copy-start | bytes 12292
  8.4 4.6 %collective-permute-start.3 = (bf16[352,128]{1,0:T(8,128)(2,1)S(1)}, bf16[352,128]{1,0:T(8,128)(2,1)S(1)}, u32[]{:S(2)}, u32[]{:S(2)}) collective-permute-start(bf16[352,128]{1,0:T(8,128)(2,1)S(1)} %get-tuple-element.33), channel_id=1, source_target_pairs={{0,4},{4,0},{8,12},{12,8},{1,5},{5,1},{9,13},{13,9},{2,6},{6,2},{1... | collective-permute-start | bytes 270344 | tf_op jit(solution)/shard_map/ppermute | solution.py:604
  10.0 3.0 %collective-permute-start.4 = (bf16[352,128]{1,0:T(8,128)(2,1)S(1)}, bf16[352,128]{1,0:T(8,128)(2,1)S(1)}, u32[]{:S(2)}, u32[]{:S(2)}) collective-permute-start(bf16[352,128]{1,0:T(8,128)(2,1)S(1)} %get-tuple-element.34), channel_id=1, source_target_pairs={{0,0},{4,8},{8,4},{12,12},{1,1},{5,9},{9,5},{13,13},{2,2},{6,10},{... | collective-permute-start | bytes 270344 | tf_op jit(solution)/shard_map/ppermute | solution.py:605
  10.7 0.7 %copy-start.1 = (f32[8]{0:T(128)S(1)}, f32[8]{0:T(128)}, u32[]{:S(2)}) copy-start(f32[8]{0:T(128)} %param.8) | copy-start | bytes 100
  15.4 3.4 %collective-permute-start.5 = (bf16[112,128]{1,0:T(8,128)(2,1)S(1)}, bf16[112,128]{1,0:T(8,128)(2,1)S(1)}, u32[]{:S(2)}, u32[]{:S(2)}) collective-permute-start(bf16[112,128]{1,0:T(8,128)(2,1)S(1)} %get-tuple-element.42), channel_id=1, source_target_pairs={{0,3},{1,2},{2,1},{3,0},{4,7},{5,6},{6,5},{7,4},{8,11},{9,10},{10,... | collective-permute-start | bytes 86024 | tf_op jit(solution)/shard_map/ppermute | solution.py:527
  15.5 4.2 %collective-permute-start.6 = (bf16[112,128]{1,0:T(8,128)(2,1)S(1)}, bf16[112,128]{1,0:T(8,128)(2,1)S(1)}, u32[]{:S(2)}, u32[]{:S(2)}) collective-permute-start(bf16[112,128]{1,0:T(8,128)(2,1)S(1)} %get-tuple-element.43), channel_id=1, source_target_pairs={{0,2},{1,3},{2,0},{3,1},{4,6},{5,7},{6,4},{7,5},{8,10},{9,11},{10,... | collective-permute-start | bytes 86024 | tf_op jit(solution)/shard_map/ppermute | solution.py:527
  16.5 3.2 %collective-permute-start.7 = (bf16[112,128]{1,0:T(8,128)(2,1)S(1)}, bf16[112,128]{1,0:T(8,128)(2,1)S(1)}, u32[]{:S(2)}, u32[]{:S(2)}) collective-permute-start(bf16[112,128]{1,0:T(8,128)(2,1)S(1)} %get-tuple-element.44), channel_id=1, source_target_pairs={{0,1},{1,0},{2,3},{3,2},{4,5},{5,4},{6,7},{7,6},{8,9},{9,8},{10,11... | collective-permute-start | bytes 86024 | tf_op jit(solution)/shard_map/ppermute | solution.py:527
  19.7 7.5 %collective-permute-start.10 = (f32[16,128]{1,0:T(8,128)S(1)}, f32[16,128]{1,0:T(8,128)S(1)}, u32[]{:S(2)}, u32[]{:S(2)}) collective-permute-start(f32[16,128]{1,0:T(8,128)S(1)} %sum.1.refs_0_), channel_id=1, source_target_pairs={{0,12},{4,8},{8,4},{12,0},{1,13},{5,9},{9,5},{13,1},{2,14},{6,10},... | collective-permute-start | bytes 24584 | tf_op jit(solution)/shard_map/ppermute | solution.py:634
  23.4 4.5 %collective-permute-start.9 = (f32[16,128]{1,0:T(8,128)S(1)}, f32[16,128]{1,0:T(8,128)S(1)}, u32[]{:S(2)}, u32[]{:S(2)}) collective-permute-start(f32[16,128]{1,0:T(8,128)S(1)} %sum.1.refs_0_), channel_id=1, source_target_pairs={{0,8},{4,12},{8,0},{12,4},{1,9},{5,13},{9,1},{13,5},{2,10},{6,14},... | collective-permute-start | bytes 24584 | tf_op jit(solution)/shard_map/ppermute | solution.py:634
  25.9 3.7 %collective-permute-start.8 = (f32[16,128]{1,0:T(8,128)S(1)}, f32[16,128]{1,0:T(8,128)S(1)}, u32[]{:S(2)}, u32[]{:S(2)}) collective-permute-start(f32[16,128]{1,0:T(8,128)S(1)} %sum.1.refs_0_), channel_id=1, source_target_pairs={{0,4},{4,0},{8,12},{12,8},{1,5},{5,1},{9,13},{13,9},{2,6},{6,2},{1... | collective-permute-start | bytes 24584 | tf_op jit(solution)/shard_map/ppermute | solution.py:634

commit v9 on v8

--- a/solution.py
+++ b/solution.py
@@ -149,7 +149,7 @@
 def rows_body(dims, *refs):
     planes, rows, chans, width, disp, space, cols, lanes = dims
     piece_refs = refs[:disp]
-    cot_in_ref, one_ref, two_ref, wide_ref, rest_ref = refs[disp:]
+    cot_in_ref, one_ref, two_ref, wide_ref = refs[disp:]
     di = lax.axis_index("disp")
     even = lax.axis_index("space") % 2 == 0
     n = planes * rows * chans
@@ -157,32 +157,24 @@
     group = 2 * planes
     cot = window(jnp.concatenate([cot_in_ref[...]] * 2, axis=0), di * cols - 4, lanes)[:rows]
     fine = []
+    rests = []
     for s in range(disp):
-        g = di ^ s
         block = piece_refs[s][:half]
-        at = pl.multiple_of(g * half, half)
-        one_ref[pl.ds(at, half)] = block
-        two_ref[pl.ds(at, half)] = block
+        one_ref[s * half : (s + 1) * half] = block
+        two_ref[s * half : (s + 1) * half] = block
         value = piece_refs[s][half:].astype(F32)
-        rest_ref[pl.ds(pl.multiple_of(g * 8, 8), 8)] = value[:8]
+        rests.append(value[:8])
         value = value[8:]
-        value = [unpack(value[: 3 * group], value[3 * group :], k) for k in range(6)]
-        fine.append(value)
-    for out_ref, down in ((one_ref, even), (two_ref, jnp.logical_not(even))):
-
-        def put(h):
-            for s in range(disp):
-                at = pl.multiple_of((di ^ s) * 3 * group, 8)
-                wide_ref[pl.ds(at, 3 * group)] = jnp.concatenate(fine[s][3 * h : 3 * h + 3], axis=0)
-            for t, term in enumerate(terms(cot[2 * h : 2 * h + 2])):
-                at = disp * 3 * group + 2 * t
-                wide_ref[at : at + 2] = term
-            rest = disp * 3 * group + 6
-            wide_ref[rest:] = jnp.zeros((wide_ref.shape[0] - rest, lanes), F32)
-
-        pl.when(down)(functools.partial(put, 1))
-        pl.when(jnp.logical_not(down))(functools.partial(put, 0))
-        out_ref[disp * half :] = jnp.concatenate([rest_ref[...]] + pack(wide_ref[...]), axis=0).astype(BF16)
+        fine.append([unpack(value[: 3 * group], value[3 * group :], k) for k in range(6)])
+    wide_ref[...] = jnp.zeros(wide_ref.shape, F32)
+    ends = []
+    for h in range(2):
+        for t, term in enumerate(terms(cot[2 * h : 2 * h + 2])):
+            wide_ref[h, 2 * t : 2 * t + 2] = term
+        parts = [fine[s][3 * h + t] for s in range(disp) for t in range(3)]
+        ends.append(jnp.concatenate(rests + pack(jnp.concatenate(parts + [wide_ref[h]], axis=0)), axis=0))
+    one_ref[disp * half :] = jnp.where(even, ends[1], ends[0]).astype(BF16)
+    two_ref[disp * half :] = jnp.where(even, ends[0], ends[1]).astype(BF16)
 
 
 def mine_body(dims, *refs):
@@ -263,12 +255,13 @@
         rest = src[n // 2 : n // 2 + 8 * disp].astype(F32)
         side = planes * block // 2
         for k in range(count):
-            g = k // planes
+            s = k // planes
             p = k % planes
             value = [
-                unpack(main[g * side : (g + 1) * side], rest[8 * g : 8 * g + 8], p * rows + r) for r in range(rows)
+                unpack(main[s * side : (s + 1) * side], rest[8 * s : 8 * s + 8], p * rows + r) for r in range(rows)
             ]
-            ref[(k + 1) * block : (k + 2) * block] = jnp.concatenate(value, axis=0).astype(BF16)
+            at = pl.multiple_of(((di ^ s) * planes + p + 1) * block, block)
+            ref[pl.ds(at, block)] = jnp.concatenate(value, axis=0).astype(BF16)
 
     for ref in (xu_ref, xd_ref):
         ref[:block] = jnp.zeros((block, lanes), BF16)
@@ -294,10 +287,10 @@
             extra = src[n // 2 + 8 * disp :].astype(F32)
             used = -(-(3 * half * disp + 6) // 16) * 16
             value = [unpack(extra[: used // 2], extra[used // 2 :], k) for k in range(3 * disp + 1)]
-            for g in range(disp):
-                prior = value[3 * g] + value[3 * g + 1] + value[3 * g + 2]
+            for s in range(disp):
+                prior = value[3 * s] + value[3 * s + 1] + value[3 * s + 2]
                 for p in range(planes):
-                    prior_ref[g * planes + p, at8 : at8 + 2] = prior[2 * p : 2 * p + 2]
+                    prior_ref[(di ^ s) * planes + p, at8 : at8 + 2] = prior[2 * p : 2 * p + 2]
             cot = value[3 * disp]
             cot_ref[at8 : at8 + 2] = cot[:2] + cot[2:4] + cot[4:6]
 
@@ -433,7 +426,9 @@
     blocks[1] = jnp.where(lane_p == 120, bias_sum, blocks[1])
     payload = jnp.concatenate(blocks, axis=0)
     shown = jnp.concatenate([disparity[2 : 2 + rows]] * 2, axis=0)
-    tail = jnp.concatenate(terms(payload, 2) + terms(shown, 2), axis=0).astype(BF16)
+    shown = terms(shown, 2)
+    shown = jnp.where(lax.broadcasted_iota(jnp.int32, shown[0].shape, 0) < rows, shown[0], shown[1])
+    tail = jnp.concatenate(terms(payload, 2) + [shown], axis=0).astype(BF16)
 
     band4 = band4_ref[...]
     found = [None] * planes
@@ -462,7 +457,7 @@
     k = 2 * chans
     sums = []
     for r in parts:
-        n = r.shape[0] - 2 * k - 16
+        n = r.shape[0] - 2 * k - 8
         value = r[n:].astype(F32)
         sums.append(value[:k] + value[k : 2 * k])
     refs[-1][...] = tree_sum(sums)
@@ -479,7 +474,7 @@
     for s in range(disp):
         j = di ^ s
         shown = parts[s][n // 2 + k :].astype(F32)
-        shown = pltpu.roll(shown[:8] + shown[8:], lanes - 4, 1)
+        shown = pltpu.roll(shown + pltpu.roll(shown, rows, 0), lanes - 4, 1)
         main = parts[s][: n // 2].astype(F32)
         value = jnp.concatenate([main, pltpu.roll(main, 64, 1), shown], axis=0)
         value = jnp.where(lanes_of(value) < cols, value, 0.0)
@@ -589,7 +584,7 @@
         "rows",
         (((sent, lanes), BF16, True), ((sent, lanes), BF16, True)),
         *pieces[::-1], cotangent,
-        scratch=[pltpu.VMEM((extra, lanes), F32), pltpu.VMEM((8 * disp, lanes), F32)],
+        scratch=[pltpu.VMEM((2, extra - 6 * count, lanes), F32)],
     )
     mine = call(
         flipped(functools.partial(mine_body, dims), disp),
@@ -604,7 +599,7 @@
     z_one = lax.ppermute(send_one, "space", swap_pairs(space, 0))
     z_two = lax.ppermute(send_two, "space", swap_pairs(space, 1))
 
-    tail = 4 * chans + 16
+    tail = 4 * chans + 8
     backs = call(
         functools.partial(main_body, dims),
         "main",

time: 30.6 us -> 30.5 us (level)
  no operation moved by 1% of the time
where the time goes in v9:
time: 30.5 us; the launch traced here: 30.2 us
  starting transfers between devices  14 us (46%)
  waiting for transfers between devices  7.58 us (25%)
  Pallas kernels  5.68 us (19%)
  local copies, waits for them, and re-layouts  2.1 us (7%)
  between operations  0.8 us (3%)
    ppermute x3, starting transfers between devices, shards(): lax.ppermute(pay, 'space', [(i, i ^ s) for i in range(space)])  6.7 us
    pallas_call x8, Pallas kernels, call(): pl.pallas_call(body, out_shape=tuple((pltpu.VMEM(shape, dtype) if inside...  5.68 us
    ppermute x6, starting transfers between devices, exchange(): lax.ppermute(sends[s], axis, [(i, i ^ s) for i in range(count)])  5.04 us
    ppermute x6, waiting for transfers between devices, exchange(): lax.ppermute(sends[s], axis, [(i, i ^ s) for i in range(count)])  3.96 us
    ppermute x3, waiting for transfers between devices, shards(): lax.ppermute(pay, 'space', [(i, i ^ s) for i in range(space)])  2.37 us
    ppermute x1, starting transfers between devices, shards(): z_one = lax.ppermute(send_one, 'space', swap_pairs(space, 0))  1.64 us
    unnamed x11, local copies, waits for them, and re-layouts  1.41 us
    ppermute x1, waiting for transfers between devices, shards(): z_one = lax.ppermute(send_one, 'space', swap_pairs(space, 0))  1.26 us
  transfers between devices with their start and end apart: 11, of which 6 were waited for; matrix products, arithmetic and copies ran while one was open for 3% of the time, Pallas kernels for 4%

profile of v9, /device:TPU:0, one launch (start us, length us, event | category | flops | bytes accessed | tf_op | source)
XLA Modules:
  0.0 30.2 jit_solution(3650931245115700173)
XLA Ops:
  0.6 1.1 %split.1 = (bf16[104,128]{1,0:T(8,128)(2,1)S(1)}, bf16[104,128]{1,0:T(8,128)(2,1)S(1)}, bf16[104,128]{1,0:T(8,128)(2,1)S(1)}, bf16[104,128]{1,0:T(8,128)(2,1)S(1)}) custom-call(bf16[8,4,4,256]{3,2,1,0:T(4,128)(2,1)} %volume_ref.1, f32[4,4,256]{2,1,0:T(4,128)} %prior_ref.1), custom_call_target="tpu_custom_call" | custom-call | tf_op jit(solution)/shard_map/split/pallas_call | solution.py:55
  1.8 2.4 %collective-permute-start = (bf16[104,128]{1,0:T(8,128)(2,1)S(1)}, bf16[104,128]{1,0:T(8,128)(2,1)S(1)}, u32[]{:S(2)}, u32[]{:S(2)}) collective-permute-start(bf16[104,128]{1,0:T(8,128)(2,1)S(1)} %get-tuple-element.28), channel_id=1, source_target_pairs={{0,3},{1,2},{2,1},{3,0},{4,7},{5,6},{6,5},{7,4},{8,11},{9,10},{10,... | collective-permute-start | bytes 79880 | tf_op jit(solution)/shard_map/ppermute | solution.py:522
  4.2 0.6 %collective-permute-start.1 = (bf16[104,128]{1,0:T(8,128)(2,1)S(1)}, bf16[104,128]{1,0:T(8,128)(2,1)S(1)}, u32[]{:S(2)}, u32[]{:S(2)}) collective-permute-start(bf16[104,128]{1,0:T(8,128)(2,1)S(1)} %get-tuple-element.29), channel_id=1, source_target_pairs={{0,2},{1,3},{2,0},{3,1},{4,6},{5,7},{6,4},{7,5},{8,10},{9,11},{10,... | collective-permute-start | bytes 79880 | tf_op jit(solution)/shard_map/ppermute | solution.py:522
  4.9 0.0 collective-permute-start.2
  5.0 0.1 reshape.30
  5.1 0.1 copy.19
  5.1 0.6 %copy-done.2 = bf16[3,3,3,8,8]{4,3,2,1,0:T(8,128)(2,1)S(1)} copy-done((bf16[3,3,3,8,8]{4,3,2,1,0:T(8,128)(2,1)S(1)}, bf16[3,3,3,8,8]{4,3,2,1,0:T(8,128)(2,1)}, u32[]{:S(2)}) %copy-start.2) | copy-done | bytes 3480
  5.7 0.1 copy.22
  5.9 0.1 reshape.29
  6.1 0.1 reshape.26
  6.3 0.1 reshape.27
  6.5 1.6 %collective-permute-done.1.refs_1_ = bf16[104,128]{1,0:T(8,128)(2,1)S(1)} collective-permute-done((bf16[104,128]{1,0:T(8,128)(2,1)S(1)}, bf16[104,128]{1,0:T(8,128)(2,1)S(1)}, u32[]{:S(2)}, u32[]{:S(2)}) %collective-permute-start.1) | collective-permute-done | bytes 26656 | tf_op jit(solution)/shard_map/ppermute | solution.py:522
  8.1 0.2 rows.1
  8.3 1.6 %collective-permute-start.3 = (bf16[352,128]{1,0:T(8,128)(2,1)S(1)}, bf16[352,128]{1,0:T(8,128)(2,1)S(1)}, u32[]{:S(2)}, u32[]{:S(2)}) collective-permute-start(bf16[352,128]{1,0:T(8,128)(2,1)S(1)} %get-tuple-element.33), channel_id=1, source_target_pairs={{0,4},{4,0},{8,12},{12,8},{1,5},{5,1},{9,13},{13,9},{2,6},{6,2},{1... | collective-permute-start | bytes 270344 | tf_op jit(solution)/shard_map/ppermute | solution.py:599
  9.9 0.7 %collective-permute-start.4 = (bf16[352,128]{1,0:T(8,128)(2,1)S(1)}, bf16[352,128]{1,0:T(8,128)(2,1)S(1)}, u32[]{:S(2)}, u32[]{:S(2)}) collective-permute-start(bf16[352,128]{1,0:T(8,128)(2,1)S(1)} %get-tuple-element.34), channel_id=1, source_target_pairs={{0,0},{4,8},{8,4},{12,12},{1,1},{5,9},{9,5},{13,13},{2,2},{6,10},{... | collective-permute-start | bytes 270344 | tf_op jit(solution)/shard_map/ppermute | solution.py:600
  10.6 0.6 %copy-done.1 = f32[8]{0:T(128)S(1)} copy-done((f32[8]{0:T(128)S(1)}, f32[8]{0:T(128)}, u32[]{:S(2)}) %copy-start.1) | copy-done | bytes 56
  11.3 0.2 bands.1
  11.5 0.1 mine.1
  11.6 1.3 %collective-permute-done.3.refs_1_ = bf16[352,128]{1,0:T(8,128)(2,1)S(1)} collective-permute-done((bf16[352,128]{1,0:T(8,128)(2,1)S(1)}, bf16[352,128]{1,0:T(8,128)(2,1)S(1)}, u32[]{:S(2)}, u32[]{:S(2)}) %collective-permute-start.3) | collective-permute-done | bytes 90144 | tf_op jit(solution)/shard_map/ppermute | solution.py:599
  12.9 2.4 %main.1 = (bf16[104,128]{1,0:T(8,128)(2,1)S(1)}, bf16[104,128]{1,0:T(8,128)(2,1)S(1)}, bf16[104,128]{1,0:T(8,128)(2,1)S(1)}, bf16[104,128]{1,0:T(8,128)(2,1)S(1)}) custom-call(bf16[576,128]{1,0:T(8,128)(2,1)S(1)} %get-tuple-element.32.refs_0_, bf16[352,128]{1,0:T(8,128)(2,1)S(1)} %collective-permute-done.3.refs_1_, ...), custom_call_target="tpu_custom_call" | custom-call | tf_op jit(solution)/shard_map/main/pallas_call | solution.py:55
  15.3 0.1 collective-permute-start.5
  15.4 1.0 %collective-permute-start.6 = (bf16[104,128]{1,0:T(8,128)(2,1)S(1)}, bf16[104,128]{1,0:T(8,128)(2,1)S(1)}, u32[]{:S(2)}, u32[]{:S(2)}) collective-permute-start(bf16[104,128]{1,0:T(8,128)(2,1)S(1)} %get-tuple-element.43), channel_id=1, source_target_pairs={{0,2},{1,3},{2,0},{3,1},{4,6},{5,7},{6,4},{7,5},{8,10},{9,11},{10,... | collective-permute-start | bytes 79880 | tf_op jit(solution)/shard_map/ppermute | solution.py:522
  16.3 0.9 %collective-permute-start.7 = (bf16[104,128]{1,0:T(8,128)(2,1)S(1)}, bf16[104,128]{1,0:T(8,128)(2,1)S(1)}, u32[]{:S(2)}, u32[]{:S(2)}) collective-permute-start(bf16[104,128]{1,0:T(8,128)(2,1)S(1)} %get-tuple-element.44), channel_id=1, source_target_pairs={{0,1},{1,0},{2,3},{3,2},{4,5},{5,4},{6,7},{7,6},{8,9},{9,8},{10,11... | collective-permute-start | bytes 79880 | tf_op jit(solution)/shard_map/ppermute | solution.py:522
  17.2 1.4 %collective-permute-done.5.refs_0_ = bf16[104,128]{1,0:T(8,128)(2,1)S(1)} collective-permute-done((bf16[104,128]{1,0:T(8,128)(2,1)S(1)}, bf16[104,128]{1,0:T(8,128)(2,1)S(1)}, u32[]{:S(2)}, u32[]{:S(2)}) %collective-permute-start.5) | collective-permute-done | bytes 26656 | tf_op jit(solution)/shard_map/ppermute | solution.py:522
  18.6 0.9 %collective-permute-done.6.refs_1_ = bf16[104,128]{1,0:T(8,128)(2,1)S(1)} collective-permute-done((bf16[104,128]{1,0:T(8,128)(2,1)S(1)}, bf16[104,128]{1,0:T(8,128)(2,1)S(1)}, u32[]{:S(2)}, u32[]{:S(2)}) %collective-permute-start.6) | collective-permute-done | bytes 26656 | tf_op jit(solution)/shard_map/ppermute | solution.py:522
  19.6 3.7 %collective-permute-start.10 = (f32[16,128]{1,0:T(8,128)S(1)}, f32[16,128]{1,0:T(8,128)S(1)}, u32[]{:S(2)}, u32[]{:S(2)}) collective-permute-start(f32[16,128]{1,0:T(8,128)S(1)} %sum.1.refs_0_), channel_id=1, source_target_pairs={{0,12},{4,8},{8,4},{12,0},{1,13},{5,9},{9,5},{13,1},{2,14},{6,10},... | collective-permute-start | bytes 24584 | tf_op jit(solution)/shard_map/ppermute | solution.py:629
  23.2 2.6 %collective-permute-start.9 = (f32[16,128]{1,0:T(8,128)S(1)}, f32[16,128]{1,0:T(8,128)S(1)}, u32[]{:S(2)}, u32[]{:S(2)}) collective-permute-start(f32[16,128]{1,0:T(8,128)S(1)} %sum.1.refs_0_), channel_id=1, source_target_pairs={{0,8},{4,12},{8,0},{12,4},{1,9},{5,13},{9,1},{13,5},{2,10},{6,14},... | collective-permute-start | bytes 24584 | tf_op jit(solution)/shard_map/ppermute | solution.py:629
  25.8 0.5 %collective-permute-start.8 = (f32[16,128]{1,0:T(8,128)S(1)}, f32[16,128]{1,0:T(8,128)S(1)}, u32[]{:S(2)}, u32[]{:S(2)}) collective-permute-start(f32[16,128]{1,0:T(8,128)S(1)} %sum.1.refs_0_), channel_id=1, source_target_pairs={{0,4},{4,0},{8,12},{12,8},{1,5},{5,1},{9,13},{13,9},{2,6},{6,2},{1... | collective-permute-start | bytes 24584 | tf_op jit(solution)/shard_map/ppermute | solution.py:629
  26.3 0.8 %join.1 = (bf16[8,4,4,256]{3,2,1,0:T(4,128)(2,1)}, f32[4,256]{1,0:T(4,128)}) custom-call(bf16[104,128]{1,0:T(8,128)(2,1)S(1)} %collective-permute-done.5.refs_0_, bf16[104,128]{1,0:T(8,128)(2,1)S(1)} %collective-permute-done.6.refs_1_, bf16[104,128]{1,0:T(8,128)(2,1)S(1)} %collective-permute-done.7.refs_2_, bf16[104,128]{1,0:T(8,128)(2,1)S(1)} %get-tuple-element.45.refs_3_), custom_call_target="tpu_custom_call" | custom-call | tf_op jit(solution)/shard_map/join/pallas_call | solution.py:55
  27.1 0.7 %collective-permute-done.9.refs_2_ = f32[16,128]{1,0:T(8,128)S(1)} collective-permute-done((f32[16,128]{1,0:T(8,128)S(1)}, f32[16,128]{1,0:T(8,128)S(1)}, u32[]{:S(2)}, u32[]{:S(2)}) %collective-permute-start.9) | collective-permute-done | bytes 8224 | tf_op jit(solution)/shard_map/ppermute | solution.py:629
  27.8 1.7 %collective-permute-done.8.refs_1_ = f32[16,128]{1,0:T(8,128)S(1)} collective-permute-done((f32[16,128]{1,0:T(8,128)S(1)}, f32[16,128]{1,0:T(8,128)S(1)}, u32[]{:S(2)}, u32[]{:S(2)}) %collective-permute-start.8) | collective-permute-done | bytes 8224 | tf_op jit(solution)/shard_map/ppermute | solution.py:629
  29.4 0.8 %finish.1 = (f32[3,3,3,8,8]{4,3,2,1,0:T(8,128)}, f32[1,8]{1,0:T(1,128)}, f32[3,3,3,8]{3,2,1,0:T(4,128)}) custom-call(f32[16,128]{1,0:T(8,128)S(1)} %sum.1.refs_0_, f32[16,128]{1,0:T(8,128)S(1)} %collective-permute-done.8.refs_1_, f32[16,128]{1,0:T(8,128)S(1)} %collective-permute-done.9.refs_2_, f32[16,128]{1,0:T(8,128)S(1)} %collective-permute-done.10.refs_3_), custom_call_target="tpu_custom_call" | custom-call | tf_op jit(solution)/shard_map/finish/pallas_call | solution.py:55
  (23 shorter events, 0.2 us)
Async XLA Ops:
  0.6 4.3 %copy-start.3 = (bf16[3,3,3,8]{3,2,1,0:T(4,128)(2,1)S(1)}, bf16[3,3,3,8]{3,2,1,0:T(4,128)(2,1)}, u32[]{:S(2)}) copy-start(bf16[3,3,3,8]{3,2,1,0:T(4,128)(2,1)} %param.9) | copy-start | bytes 1300
  1.8 4.7 %collective-permute-start = (bf16[104,128]{1,0:T(8,128)(2,1)S(1)}, bf16[104,128]{1,0:T(8,128)(2,1)S(1)}, u32[]{:S(2)}, u32[]{:S(2)}) collective-permute-start(bf16[104,128]{1,0:T(8,128)(2,1)S(1)} %get-tuple-element.28), channel_id=1, source_target_pairs={{0,3},{1,2},{2,1},{3,0},{4,7},{5,6},{6,5},{7,4},{8,11},{9,10},{10,... | collective-permute-start | bytes 79880 | tf_op jit(solution)/shard_map/ppermute | solution.py:522
  4.2 3.8 %collective-permute-start.1 = (bf16[104,128]{1,0:T(8,128)(2,1)S(1)}, bf16[104,128]{1,0:T(8,128)(2,1)S(1)}, u32[]{:S(2)}, u32[]{:S(2)}) collective-permute-start(bf16[104,128]{1,0:T(8,128)(2,1)S(1)} %get-tuple-element.29), channel_id=1, source_target_pairs={{0,2},{1,3},{2,0},{3,1},{4,6},{5,7},{6,4},{7,5},{8,10},{9,11},{10,... | collective-permute-start | bytes 79880 | tf_op jit(solution)/shard_map/ppermute | solution.py:522
  4.9 3.2 %collective-permute-start.2 = (bf16[104,128]{1,0:T(8,128)(2,1)S(1)}, bf16[104,128]{1,0:T(8,128)(2,1)S(1)}, u32[]{:S(2)}, u32[]{:S(2)}) collective-permute-start(bf16[104,128]{1,0:T(8,128)(2,1)S(1)} %get-tuple-element.30), channel_id=1, source_target_pairs={{0,1},{1,0},{2,3},{3,2},{4,5},{5,4},{6,7},{7,6},{8,9},{9,8},{10,11... | collective-permute-start | bytes 79880 | tf_op jit(solution)/shard_map/ppermute | solution.py:522
  4.9 0.8 %copy-start.2 = (bf16[3,3,3,8,8]{4,3,2,1,0:T(8,128)(2,1)S(1)}, bf16[3,3,3,8,8]{4,3,2,1,0:T(8,128)(2,1)}, u32[]{:S(2)}) copy-start(bf16[3,3,3,8,8]{4,3,2,1,0:T(8,128)(2,1)} %param.7) | copy-start | bytes 10372
  6.3 1.8 %copy-start = (f32[4,256]{1,0:T(4,128)S(1)}, f32[4,256]{1,0:T(4,128)}, u32[]{:S(2)}) copy-start(f32[4,256]{1,0:T(4,128)} %refs_4_.3) | copy-start | bytes 12292
  8.3 4.6 %collective-permute-start.3 = (bf16[352,128]{1,0:T(8,128)(2,1)S(1)}, bf16[352,128]{1,0:T(8,128)(2,1)S(1)}, u32[]{:S(2)}, u32[]{:S(2)}) collective-permute-start(bf16[352,128]{1,0:T(8,128)(2,1)S(1)} %get-tuple-element.33), channel_id=1, source_target_pairs={{0,4},{4,0},{8,12},{12,8},{1,5},{5,1},{9,13},{13,9},{2,6},{6,2},{1... | collective-permute-start | bytes 270344 | tf_op jit(solution)/shard_map/ppermute | solution.py:599
  9.9 3.0 %collective-permute-start.4 = (bf16[352,128]{1,0:T(8,128)(2,1)S(1)}, bf16[352,128]{1,0:T(8,128)(2,1)S(1)}, u32[]{:S(2)}, u32[]{:S(2)}) collective-permute-start(bf16[352,128]{1,0:T(8,128)(2,1)S(1)} %get-tuple-element.34), channel_id=1, source_target_pairs={{0,0},{4,8},{8,4},{12,12},{1,1},{5,9},{9,5},{13,13},{2,2},{6,10},{... | collective-permute-start | bytes 270344 | tf_op jit(solution)/shard_map/ppermute | solution.py:600
  10.6 0.7 %copy-start.1 = (f32[8]{0:T(128)S(1)}, f32[8]{0:T(128)}, u32[]{:S(2)}) copy-start(f32[8]{0:T(128)} %param.8) | copy-start | bytes 100
  15.3 3.3 %collective-permute-start.5 = (bf16[104,128]{1,0:T(8,128)(2,1)S(1)}, bf16[104,128]{1,0:T(8,128)(2,1)S(1)}, u32[]{:S(2)}, u32[]{:S(2)}) collective-permute-start(bf16[104,128]{1,0:T(8,128)(2,1)S(1)} %get-tuple-element.42), channel_id=1, source_target_pairs={{0,3},{1,2},{2,1},{3,0},{4,7},{5,6},{6,5},{7,4},{8,11},{9,10},{10,... | collective-permute-start | bytes 79880 | tf_op jit(solution)/shard_map/ppermute | solution.py:522
  15.4 4.2 %collective-permute-start.6 = (bf16[104,128]{1,0:T(8,128)(2,1)S(1)}, bf16[104,128]{1,0:T(8,128)(2,1)S(1)}, u32[]{:S(2)}, u32[]{:S(2)}) collective-permute-start(bf16[104,128]{1,0:T(8,128)(2,1)S(1)} %get-tuple-element.43), channel_id=1, source_target_pairs={{0,2},{1,3},{2,0},{3,1},{4,6},{5,7},{6,4},{7,5},{8,10},{9,11},{10,... | collective-permute-start | bytes 79880 | tf_op jit(solution)/shard_map/ppermute | solution.py:522
  16.3 3.2 %collective-permute-start.7 = (bf16[104,128]{1,0:T(8,128)(2,1)S(1)}, bf16[104,128]{1,0:T(8,128)(2,1)S(1)}, u32[]{:S(2)}, u32[]{:S(2)}) collective-permute-start(bf16[104,128]{1,0:T(8,128)(2,1)S(1)} %get-tuple-element.44), channel_id=1, source_target_pairs={{0,1},{1,0},{2,3},{3,2},{4,5},{5,4},{6,7},{7,6},{8,9},{9,8},{10,11... | collective-permute-start | bytes 79880 | tf_op jit(solution)/shard_map/ppermute | solution.py:522
  19.6 7.5 %collective-permute-start.10 = (f32[16,128]{1,0:T(8,128)S(1)}, f32[16,128]{1,0:T(8,128)S(1)}, u32[]{:S(2)}, u32[]{:S(2)}) collective-permute-start(f32[16,128]{1,0:T(8,128)S(1)} %sum.1.refs_0_), channel_id=1, source_target_pairs={{0,12},{4,8},{8,4},{12,0},{1,13},{5,9},{9,5},{13,1},{2,14},{6,10},... | collective-permute-start | bytes 24584 | tf_op jit(solution)/shard_map/ppermute | solution.py:629
  23.2 4.5 %collective-permute-start.9 = (f32[16,128]{1,0:T(8,128)S(1)}, f32[16,128]{1,0:T(8,128)S(1)}, u32[]{:S(2)}, u32[]{:S(2)}) collective-permute-start(f32[16,128]{1,0:T(8,128)S(1)} %sum.1.refs_0_), channel_id=1, source_target_pairs={{0,8},{4,12},{8,0},{12,4},{1,9},{5,13},{9,1},{13,5},{2,10},{6,14},... | collective-permute-start | bytes 24584 | tf_op jit(solution)/shard_map/ppermute | solution.py:629
  25.8 3.7 %collective-permute-start.8 = (f32[16,128]{1,0:T(8,128)S(1)}, f32[16,128]{1,0:T(8,128)S(1)}, u32[]{:S(2)}, u32[]{:S(2)}) collective-permute-start(f32[16,128]{1,0:T(8,128)S(1)} %sum.1.refs_0_), channel_id=1, source_target_pairs={{0,4},{4,0},{8,12},{12,8},{1,5},{5,1},{9,13},{13,9},{2,6},{6,2},{1... | collective-permute-start | bytes 24584 | tf_op jit(solution)/shard_map/ppermute | solution.py:629

commit v10 on v9

--- a/solution.py
+++ b/solution.py
@@ -85,6 +85,8 @@
 def window(x, start, size):
     width = x.shape[1]
     moved = pltpu.roll(x, (width - start) % width, 1)[:, :size]
+    if isinstance(start, int) and 0 <= start <= width - 72:
+        return moved
     column = start + lax.broadcasted_iota(jnp.int32, moved.shape, 1)
     return jnp.where((column >= 0) & (column < width), moved, 0.0)
 

time: 30.5 us -> 30.5 us (level)
  no operation moved by 1% of the time
where the time goes in v10:
time: 30.5 us; the launch traced here: 30.2 us
  starting transfers between devices  14 us (46%)
  waiting for transfers between devices  7.58 us (25%)
  Pallas kernels  5.68 us (19%)
  local copies, waits for them, and re-layouts  2.1 us (7%)
  between operations  0.8 us (3%)
    ppermute x3, starting transfers between devices, shards(): lax.ppermute(pay, 'space', [(i, i ^ s) for i in range(space)])  6.7 us
    pallas_call x8, Pallas kernels, call(): pl.pallas_call(body, out_shape=tuple((pltpu.VMEM(shape, dtype) if inside...  5.68 us
    ppermute x6, starting transfers between devices, exchange(): lax.ppermute(sends[s], axis, [(i, i ^ s) for i in range(count)])  5.04 us
    ppermute x6, waiting for transfers between devices, exchange(): lax.ppermute(sends[s], axis, [(i, i ^ s) for i in range(count)])  3.96 us
    ppermute x3, waiting for transfers between devices, shards(): lax.ppermute(pay, 'space', [(i, i ^ s) for i in range(space)])  2.37 us
    ppermute x1, starting transfers between devices, shards(): z_one = lax.ppermute(send_one, 'space', swap_pairs(space, 0))  1.64 us
    unnamed x11, local copies, waits for them, and re-layouts  1.41 us
    ppermute x1, waiting for transfers between devices, shards(): z_one = lax.ppermute(send_one, 'space', swap_pairs(space, 0))  1.26 us
  transfers between devices with their start and end apart: 11, of which 6 were waited for; matrix products, arithmetic and copies ran while one was open for 3% of the time, Pallas kernels for 4%

profile of v10, /device:TPU:0, one launch (start us, length us, event | category | flops | bytes accessed | tf_op | source)
XLA Modules:
  0.0 30.2 jit_solution(3650931245115700173)
XLA Ops:
  0.6 1.1 %split.1 = (bf16[104,128]{1,0:T(8,128)(2,1)S(1)}, bf16[104,128]{1,0:T(8,128)(2,1)S(1)}, bf16[104,128]{1,0:T(8,128)(2,1)S(1)}, bf16[104,128]{1,0:T(8,128)(2,1)S(1)}) custom-call(bf16[8,4,4,256]{3,2,1,0:T(4,128)(2,1)} %volume_ref.1, f32[4,4,256]{2,1,0:T(4,128)} %prior_ref.1), custom_call_target="tpu_custom_call" | custom-call | tf_op jit(solution)/shard_map/split/pallas_call | solution.py:55
  1.8 2.4 %collective-permute-start = (bf16[104,128]{1,0:T(8,128)(2,1)S(1)}, bf16[104,128]{1,0:T(8,128)(2,1)S(1)}, u32[]{:S(2)}, u32[]{:S(2)}) collective-permute-start(bf16[104,128]{1,0:T(8,128)(2,1)S(1)} %get-tuple-element.28), channel_id=1, source_target_pairs={{0,3},{1,2},{2,1},{3,0},{4,7},{5,6},{6,5},{7,4},{8,11},{9,10},{10,... | collective-permute-start | bytes 79880 | tf_op jit(solution)/shard_map/ppermute | solution.py:524
  4.2 0.6 %collective-permute-start.1 = (bf16[104,128]{1,0:T(8,128)(2,1)S(1)}, bf16[104,128]{1,0:T(8,128)(2,1)S(1)}, u32[]{:S(2)}, u32[]{:S(2)}) collective-permute-start(bf16[104,128]{1,0:T(8,128)(2,1)S(1)} %get-tuple-element.29), channel_id=1, source_target_pairs={{0,2},{1,3},{2,0},{3,1},{4,6},{5,7},{6,4},{7,5},{8,10},{9,11},{10,... | collective-permute-start | bytes 79880 | tf_op jit(solution)/shard_map/ppermute | solution.py:524
  4.9 0.0 collective-permute-start.2
  5.0 0.1 reshape.30
  5.1 0.1 copy.19
  5.1 0.6 %copy-done.2 = bf16[3,3,3,8,8]{4,3,2,1,0:T(8,128)(2,1)S(1)} copy-done((bf16[3,3,3,8,8]{4,3,2,1,0:T(8,128)(2,1)S(1)}, bf16[3,3,3,8,8]{4,3,2,1,0:T(8,128)(2,1)}, u32[]{:S(2)}) %copy-start.2) | copy-done | bytes 3480
  5.7 0.1 copy.22
  5.9 0.1 reshape.29
  6.1 0.1 reshape.26
  6.3 0.1 reshape.27
  6.5 1.6 %collective-permute-done.1.refs_1_ = bf16[104,128]{1,0:T(8,128)(2,1)S(1)} collective-permute-done((bf16[104,128]{1,0:T(8,128)(2,1)S(1)}, bf16[104,128]{1,0:T(8,128)(2,1)S(1)}, u32[]{:S(2)}, u32[]{:S(2)}) %collective-permute-start.1) | collective-permute-done | bytes 26656 | tf_op jit(solution)/shard_map/ppermute | solution.py:524
  8.1 0.2 rows.1
  8.3 1.6 %collective-permute-start.3 = (bf16[352,128]{1,0:T(8,128)(2,1)S(1)}, bf16[352,128]{1,0:T(8,128)(2,1)S(1)}, u32[]{:S(2)}, u32[]{:S(2)}) collective-permute-start(bf16[352,128]{1,0:T(8,128)(2,1)S(1)} %get-tuple-element.33), channel_id=1, source_target_pairs={{0,4},{4,0},{8,12},{12,8},{1,5},{5,1},{9,13},{13,9},{2,6},{6,2},{1... | collective-permute-start | bytes 270344 | tf_op jit(solution)/shard_map/ppermute | solution.py:601
  9.9 0.7 %collective-permute-start.4 = (bf16[352,128]{1,0:T(8,128)(2,1)S(1)}, bf16[352,128]{1,0:T(8,128)(2,1)S(1)}, u32[]{:S(2)}, u32[]{:S(2)}) collective-permute-start(bf16[352,128]{1,0:T(8,128)(2,1)S(1)} %get-tuple-element.34), channel_id=1, source_target_pairs={{0,0},{4,8},{8,4},{12,12},{1,1},{5,9},{9,5},{13,13},{2,2},{6,10},{... | collective-permute-start | bytes 270344 | tf_op jit(solution)/shard_map/ppermute | solution.py:602
  10.6 0.6 %copy-done.1 = f32[8]{0:T(128)S(1)} copy-done((f32[8]{0:T(128)S(1)}, f32[8]{0:T(128)}, u32[]{:S(2)}) %copy-start.1) | copy-done | bytes 56
  11.3 0.2 bands.1
  11.5 0.1 mine.1
  11.6 1.3 %collective-permute-done.3.refs_1_ = bf16[352,128]{1,0:T(8,128)(2,1)S(1)} collective-permute-done((bf16[352,128]{1,0:T(8,128)(2,1)S(1)}, bf16[352,128]{1,0:T(8,128)(2,1)S(1)}, u32[]{:S(2)}, u32[]{:S(2)}) %collective-permute-start.3) | collective-permute-done | bytes 90144 | tf_op jit(solution)/shard_map/ppermute | solution.py:601
  12.9 2.4 %main.1 = (bf16[104,128]{1,0:T(8,128)(2,1)S(1)}, bf16[104,128]{1,0:T(8,128)(2,1)S(1)}, bf16[104,128]{1,0:T(8,128)(2,1)S(1)}, bf16[104,128]{1,0:T(8,128)(2,1)S(1)}) custom-call(bf16[576,128]{1,0:T(8,128)(2,1)S(1)} %get-tuple-element.32.refs_0_, bf16[352,128]{1,0:T(8,128)(2,1)S(1)} %collective-permute-done.3.refs_1_, ...), custom_call_target="tpu_custom_call" | custom-call | tf_op jit(solution)/shard_map/main/pallas_call | solution.py:55
  15.3 0.1 collective-permute-start.5
  15.4 1.0 %collective-permute-start.6 = (bf16[104,128]{1,0:T(8,128)(2,1)S(1)}, bf16[104,128]{1,0:T(8,128)(2,1)S(1)}, u32[]{:S(2)}, u32[]{:S(2)}) collective-permute-start(bf16[104,128]{1,0:T(8,128)(2,1)S(1)} %get-tuple-element.43), channel_id=1, source_target_pairs={{0,2},{1,3},{2,0},{3,1},{4,6},{5,7},{6,4},{7,5},{8,10},{9,11},{10,... | collective-permute-start | bytes 79880 | tf_op jit(solution)/shard_map/ppermute | solution.py:524
  16.3 0.9 %collective-permute-start.7 = (bf16[104,128]{1,0:T(8,128)(2,1)S(1)}, bf16[104,128]{1,0:T(8,128)(2,1)S(1)}, u32[]{:S(2)}, u32[]{:S(2)}) collective-permute-start(bf16[104,128]{1,0:T(8,128)(2,1)S(1)} %get-tuple-element.44), channel_id=1, source_target_pairs={{0,1},{1,0},{2,3},{3,2},{4,5},{5,4},{6,7},{7,6},{8,9},{9,8},{10,11... | collective-permute-start | bytes 79880 | tf_op jit(solution)/shard_map/ppermute | solution.py:524
  17.2 1.4 %collective-permute-done.5.refs_0_ = bf16[104,128]{1,0:T(8,128)(2,1)S(1)} collective-permute-done((bf16[104,128]{1,0:T(8,128)(2,1)S(1)}, bf16[104,128]{1,0:T(8,128)(2,1)S(1)}, u32[]{:S(2)}, u32[]{:S(2)}) %collective-permute-start.5) | collective-permute-done | bytes 26656 | tf_op jit(solution)/shard_map/ppermute | solution.py:524
  18.6 0.9 %collective-permute-done.6.refs_1_ = bf16[104,128]{1,0:T(8,128)(2,1)S(1)} collective-permute-done((bf16[104,128]{1,0:T(8,128)(2,1)S(1)}, bf16[104,128]{1,0:T(8,128)(2,1)S(1)}, u32[]{:S(2)}, u32[]{:S(2)}) %collective-permute-start.6) | collective-permute-done | bytes 26656 | tf_op jit(solution)/shard_map/ppermute | solution.py:524
  19.6 3.7 %collective-permute-start.10 = (f32[16,128]{1,0:T(8,128)S(1)}, f32[16,128]{1,0:T(8,128)S(1)}, u32[]{:S(2)}, u32[]{:S(2)}) collective-permute-start(f32[16,128]{1,0:T(8,128)S(1)} %sum.1.refs_0_), channel_id=1, source_target_pairs={{0,12},{4,8},{8,4},{12,0},{1,13},{5,9},{9,5},{13,1},{2,14},{6,10},... | collective-permute-start | bytes 24584 | tf_op jit(solution)/shard_map/ppermute | solution.py:631
  23.2 2.6 %collective-permute-start.9 = (f32[16,128]{1,0:T(8,128)S(1)}, f32[16,128]{1,0:T(8,128)S(1)}, u32[]{:S(2)}, u32[]{:S(2)}) collective-permute-start(f32[16,128]{1,0:T(8,128)S(1)} %sum.1.refs_0_), channel_id=1, source_target_pairs={{0,8},{4,12},{8,0},{12,4},{1,9},{5,13},{9,1},{13,5},{2,10},{6,14},... | collective-permute-start | bytes 24584 | tf_op jit(solution)/shard_map/ppermute | solution.py:631
  25.8 0.5 %collective-permute-start.8 = (f32[16,128]{1,0:T(8,128)S(1)}, f32[16,128]{1,0:T(8,128)S(1)}, u32[]{:S(2)}, u32[]{:S(2)}) collective-permute-start(f32[16,128]{1,0:T(8,128)S(1)} %sum.1.refs_0_), channel_id=1, source_target_pairs={{0,4},{4,0},{8,12},{12,8},{1,5},{5,1},{9,13},{13,9},{2,6},{6,2},{1... | collective-permute-start | bytes 24584 | tf_op jit(solution)/shard_map/ppermute | solution.py:631
  26.3 0.8 %join.1 = (bf16[8,4,4,256]{3,2,1,0:T(4,128)(2,1)}, f32[4,256]{1,0:T(4,128)}) custom-call(bf16[104,128]{1,0:T(8,128)(2,1)S(1)} %collective-permute-done.5.refs_0_, bf16[104,128]{1,0:T(8,128)(2,1)S(1)} %collective-permute-done.6.refs_1_, bf16[104,128]{1,0:T(8,128)(2,1)S(1)} %collective-permute-done.7.refs_2_, bf16[104,128]{1,0:T(8,128)(2,1)S(1)} %get-tuple-element.45.refs_3_), custom_call_target="tpu_custom_call" | custom-call | tf_op jit(solution)/shard_map/join/pallas_call | solution.py:55
  27.1 0.7 %collective-permute-done.9.refs_2_ = f32[16,128]{1,0:T(8,128)S(1)} collective-permute-done((f32[16,128]{1,0:T(8,128)S(1)}, f32[16,128]{1,0:T(8,128)S(1)}, u32[]{:S(2)}, u32[]{:S(2)}) %collective-permute-start.9) | collective-permute-done | bytes 8224 | tf_op jit(solution)/shard_map/ppermute | solution.py:631
  27.8 1.7 %collective-permute-done.8.refs_1_ = f32[16,128]{1,0:T(8,128)S(1)} collective-permute-done((f32[16,128]{1,0:T(8,128)S(1)}, f32[16,128]{1,0:T(8,128)S(1)}, u32[]{:S(2)}, u32[]{:S(2)}) %collective-permute-start.8) | collective-permute-done | bytes 8224 | tf_op jit(solution)/shard_map/ppermute | solution.py:631
  29.4 0.8 %finish.1 = (f32[3,3,3,8,8]{4,3,2,1,0:T(8,128)}, f32[1,8]{1,0:T(1,128)}, f32[3,3,3,8]{3,2,1,0:T(4,128)}) custom-call(f32[16,128]{1,0:T(8,128)S(1)} %sum.1.refs_0_, f32[16,128]{1,0:T(8,128)S(1)} %collective-permute-done.8.refs_1_, f32[16,128]{1,0:T(8,128)S(1)} %collective-permute-done.9.refs_2_, f32[16,128]{1,0:T(8,128)S(1)} %collective-permute-done.10.refs_3_), custom_call_target="tpu_custom_call" | custom-call | tf_op jit(solution)/shard_map/finish/pallas_call | solution.py:55
  (23 shorter events, 0.2 us)
Async XLA Ops:
  0.6 4.3 %copy-start.3 = (bf16[3,3,3,8]{3,2,1,0:T(4,128)(2,1)S(1)}, bf16[3,3,3,8]{3,2,1,0:T(4,128)(2,1)}, u32[]{:S(2)}) copy-start(bf16[3,3,3,8]{3,2,1,0:T(4,128)(2,1)} %param.9) | copy-start | bytes 1300
  1.8 4.7 %collective-permute-start = (bf16[104,128]{1,0:T(8,128)(2,1)S(1)}, bf16[104,128]{1,0:T(8,128)(2,1)S(1)}, u32[]{:S(2)}, u32[]{:S(2)}) collective-permute-start(bf16[104,128]{1,0:T(8,128)(2,1)S(1)} %get-tuple-element.28), channel_id=1, source_target_pairs={{0,3},{1,2},{2,1},{3,0},{4,7},{5,6},{6,5},{7,4},{8,11},{9,10},{10,... | collective-permute-start | bytes 79880 | tf_op jit(solution)/shard_map/ppermute | solution.py:524
  4.2 3.8 %collective-permute-start.1 = (bf16[104,128]{1,0:T(8,128)(2,1)S(1)}, bf16[104,128]{1,0:T(8,128)(2,1)S(1)}, u32[]{:S(2)}, u32[]{:S(2)}) collective-permute-start(bf16[104,128]{1,0:T(8,128)(2,1)S(1)} %get-tuple-element.29), channel_id=1, source_target_pairs={{0,2},{1,3},{2,0},{3,1},{4,6},{5,7},{6,4},{7,5},{8,10},{9,11},{10,... | collective-permute-start | bytes 79880 | tf_op jit(solution)/shard_map/ppermute | solution.py:524
  4.9 3.2 %collective-permute-start.2 = (bf16[104,128]{1,0:T(8,128)(2,1)S(1)}, bf16[104,128]{1,0:T(8,128)(2,1)S(1)}, u32[]{:S(2)}, u32[]{:S(2)}) collective-permute-start(bf16[104,128]{1,0:T(8,128)(2,1)S(1)} %get-tuple-element.30), channel_id=1, source_target_pairs={{0,1},{1,0},{2,3},{3,2},{4,5},{5,4},{6,7},{7,6},{8,9},{9,8},{10,11... | collective-permute-start | bytes 79880 | tf_op jit(solution)/shard_map/ppermute | solution.py:524
  4.9 0.8 %copy-start.2 = (bf16[3,3,3,8,8]{4,3,2,1,0:T(8,128)(2,1)S(1)}, bf16[3,3,3,8,8]{4,3,2,1,0:T(8,128)(2,1)}, u32[]{:S(2)}) copy-start(bf16[3,3,3,8,8]{4,3,2,1,0:T(8,128)(2,1)} %param.7) | copy-start | bytes 10372
  6.3 1.8 %copy-start = (f32[4,256]{1,0:T(4,128)S(1)}, f32[4,256]{1,0:T(4,128)}, u32[]{:S(2)}) copy-start(f32[4,256]{1,0:T(4,128)} %refs_4_.3) | copy-start | bytes 12292
  8.3 4.6 %collective-permute-start.3 = (bf16[352,128]{1,0:T(8,128)(2,1)S(1)}, bf16[352,128]{1,0:T(8,128)(2,1)S(1)}, u32[]{:S(2)}, u32[]{:S(2)}) collective-permute-start(bf16[352,128]{1,0:T(8,128)(2,1)S(1)} %get-tuple-element.33), channel_id=1, source_target_pairs={{0,4},{4,0},{8,12},{12,8},{1,5},{5,1},{9,13},{13,9},{2,6},{6,2},{1... | collective-permute-start | bytes 270344 | tf_op jit(solution)/shard_map/ppermute | solution.py:601
  9.9 3.0 %collective-permute-start.4 = (bf16[352,128]{1,0:T(8,128)(2,1)S(1)}, bf16[352,128]{1,0:T(8,128)(2,1)S(1)}, u32[]{:S(2)}, u32[]{:S(2)}) collective-permute-start(bf16[352,128]{1,0:T(8,128)(2,1)S(1)} %get-tuple-element.34), channel_id=1, source_target_pairs={{0,0},{4,8},{8,4},{12,12},{1,1},{5,9},{9,5},{13,13},{2,2},{6,10},{... | collective-permute-start | bytes 270344 | tf_op jit(solution)/shard_map/ppermute | solution.py:602
  10.6 0.7 %copy-start.1 = (f32[8]{0:T(128)S(1)}, f32[8]{0:T(128)}, u32[]{:S(2)}) copy-start(f32[8]{0:T(128)} %param.8) | copy-start | bytes 100
  15.3 3.3 %collective-permute-start.5 = (bf16[104,128]{1,0:T(8,128)(2,1)S(1)}, bf16[104,128]{1,0:T(8,128)(2,1)S(1)}, u32[]{:S(2)}, u32[]{:S(2)}) collective-permute-start(bf16[104,128]{1,0:T(8,128)(2,1)S(1)} %get-tuple-element.42), channel_id=1, source_target_pairs={{0,3},{1,2},{2,1},{3,0},{4,7},{5,6},{6,5},{7,4},{8,11},{9,10},{10,... | collective-permute-start | bytes 79880 | tf_op jit(solution)/shard_map/ppermute | solution.py:524
  15.4 4.2 %collective-permute-start.6 = (bf16[104,128]{1,0:T(8,128)(2,1)S(1)}, bf16[104,128]{1,0:T(8,128)(2,1)S(1)}, u32[]{:S(2)}, u32[]{:S(2)}) collective-permute-start(bf16[104,128]{1,0:T(8,128)(2,1)S(1)} %get-tuple-element.43), channel_id=1, source_target_pairs={{0,2},{1,3},{2,0},{3,1},{4,6},{5,7},{6,4},{7,5},{8,10},{9,11},{10,... | collective-permute-start | bytes 79880 | tf_op jit(solution)/shard_map/ppermute | solution.py:524
  16.3 3.2 %collective-permute-start.7 = (bf16[104,128]{1,0:T(8,128)(2,1)S(1)}, bf16[104,128]{1,0:T(8,128)(2,1)S(1)}, u32[]{:S(2)}, u32[]{:S(2)}) collective-permute-start(bf16[104,128]{1,0:T(8,128)(2,1)S(1)} %get-tuple-element.44), channel_id=1, source_target_pairs={{0,1},{1,0},{2,3},{3,2},{4,5},{5,4},{6,7},{7,6},{8,9},{9,8},{10,11... | collective-permute-start | bytes 79880 | tf_op jit(solution)/shard_map/ppermute | solution.py:524
  19.6 7.5 %collective-permute-start.10 = (f32[16,128]{1,0:T(8,128)S(1)}, f32[16,128]{1,0:T(8,128)S(1)}, u32[]{:S(2)}, u32[]{:S(2)}) collective-permute-start(f32[16,128]{1,0:T(8,128)S(1)} %sum.1.refs_0_), channel_id=1, source_target_pairs={{0,12},{4,8},{8,4},{12,0},{1,13},{5,9},{9,5},{13,1},{2,14},{6,10},... | collective-permute-start | bytes 24584 | tf_op jit(solution)/shard_map/ppermute | solution.py:631
  23.2 4.5 %collective-permute-start.9 = (f32[16,128]{1,0:T(8,128)S(1)}, f32[16,128]{1,0:T(8,128)S(1)}, u32[]{:S(2)}, u32[]{:S(2)}) collective-permute-start(f32[16,128]{1,0:T(8,128)S(1)} %sum.1.refs_0_), channel_id=1, source_target_pairs={{0,8},{4,12},{8,0},{12,4},{1,9},{5,13},{9,1},{13,5},{2,10},{6,14},... | collective-permute-start | bytes 24584 | tf_op jit(solution)/shard_map/ppermute | solution.py:631
  25.8 3.7 %collective-permute-start.8 = (f32[16,128]{1,0:T(8,128)S(1)}, f32[16,128]{1,0:T(8,128)S(1)}, u32[]{:S(2)}, u32[]{:S(2)}) collective-permute-start(f32[16,128]{1,0:T(8,128)S(1)} %sum.1.refs_0_), channel_id=1, source_target_pairs={{0,4},{4,0},{8,12},{12,8},{1,5},{5,1},{9,13},{13,9},{2,6},{6,2},{1... | collective-permute-start | bytes 24584 | tf_op jit(solution)/shard_map/ppermute | solution.py:631
